TPU v7x, 128 devices: a whole 4x4x4 slice. The times are simulated.
128 devices in a mesh: req: 8 (over x, core), mlp: 16 (over z, y).
Axes of the slice: x: 4, y: 4, z: 4, core: 2. Of those that a mesh axis runs over, the one named last changes fastest.
Arguments:
- tokens: bfloat16 [8192, 4096], P(('req', 'mlp')), may hold values from -6 to 6
- layer_norm_gain: float32 [4096], replicated, may hold values from 0.1 to 1.9
- layer_norm_bias: float32 [4096], replicated, may hold values from -2 to 2
- query_key_weight: bfloat16 [4096, 16, 768], P(None, 'mlp')
- output_weight: bfloat16 [16, 256, 4096], P('mlp'), may hold values from -0.09375 to 0.09375
- up_weight: bfloat16 [4096, 8192], P(None, 'mlp'), may hold values from -0.09375 to 0.09375
- input_bias: float32 [8192], P('mlp'), may hold values from -3 to 3
- down_weight: bfloat16 [8192, 4096], P('mlp'), may hold values from -0.0625 to 0.0625
- output_bias: float32 [4096], replicated, may hold values from -2 to 2
- input_adapter_left: bfloat16 [4096, 2048], P(None, 'mlp'), may hold values from -0.09375 to 0.09375
- query_key_value_right: bfloat16 [1024, 16, 768], P(None, 'mlp'), may hold values from -1.5 to 1.5
- up_adapter_right: bfloat16 [1024, 8192], P(None, 'mlp'), may hold values from -1.5 to 1.5
- output_adapter_left: bfloat16 [16, 256, 1024], P('mlp'), may hold values from -0.09375 to 0.09375
- down_adapter_left: bfloat16 [8192, 1024], P('mlp'), may hold values from -0.0625 to 0.0625
- output_adapter_right: bfloat16 [2048, 4096], P('mlp'), may hold values from -1 to 1
- lengths: int32 [257], replicated, may hold values from 8 to 4096, as said below
- request_adapter: int32 [257], replicated, may hold values from 0 to 63
- slot_adapter: int32 [64], P('mlp'), may hold values from 0 to 63, each once
Outputs:
- mixed: bfloat16 [8192, 4096], P(('req', 'mlp'))
Inputs may be any that keep to these rules, and one draw needn't show every extreme that they name: `lengths`: one request holds exactly 4096 tokens, every other one 8 to 24; together they hold 8192 tokens. `slot_adapter`: every adapter id stands in exactly one slot.
All inputs are finite; a program needn't handle non-finite values.
Results may differ from a plain program's by a relative error of at most 0.017.
Values may be sent and summed in bfloat16 or wider, within the bound.
A program may use at most 128 MiB of HBM per device.

v0:
```python
import math

import jax
import jax.numpy as jnp
from jax import lax
from jax.sharding import PartitionSpec as P

HEAD_SIZE = 256
ROT = 64
ADAPTER_RANK = 16
ADP_DEV = 4


EPSILON = 1e-05
NEGATIVE_FILL = -1e30


def rank_product(left_side, right_side):
    return jnp.dot(left_side, right_side, preferred_element_type=jnp.float32)


def normalize(inputs, layer_norm_gain, layer_norm_bias):
    values = inputs.astype(jnp.float32)
    center = values - jnp.mean(values, axis=1, keepdims=True)
    spread = jnp.mean(center * center, axis=1, keepdims=True)
    scaled = center * lax.rsqrt(spread + EPSILON)
    return (scaled * layer_norm_gain + layer_norm_bias).astype(jnp.bfloat16)


def token_info(lengths, request_adapter, first_row, row_count):
    endings = jnp.cumsum(lengths)
    anchors = endings - lengths
    token_index = first_row + lax.iota(jnp.int32, row_count)
    inside = anchors[None, :] <= token_index[:, None]
    request = jnp.sum(inside.astype(jnp.int32), axis=1) - 1
    request_start = jnp.max(jnp.where(inside, anchors[None, :], jnp.zeros((), jnp.int32)), axis=1)
    adapter_id = jnp.take(request_adapter, jnp.maximum(request, 0))
    return (token_index, request, token_index - request_start, adapter_id)


def rotate(matrix, position):
    row_count = matrix.shape[0]
    head_count = matrix.shape[1]
    half_rot = ROT // 2
    frequency = jnp.exp(jnp.arange(half_rot, dtype=jnp.float32) * (-2.0 * math.log(10000.0) / ROT))
    angles = position.astype(jnp.float32)[:, None] * frequency[None, :]
    cosine = jnp.cos(angles)[:, None, :]
    sine_value = jnp.sin(angles)[:, None, :]
    paired_part = matrix[:, :, :ROT].reshape(row_count, head_count, half_rot, 2)
    even_part = paired_part[:, :, :, 0]
    odd_part = paired_part[:, :, :, 1]
    turned = jnp.stack(
        [even_part * cosine - odd_part * sine_value, odd_part * cosine + even_part * sine_value],
        axis=-1,
    )
    return jnp.concatenate([turned.reshape(row_count, head_count, ROT), matrix[:, :, ROT:]], axis=2)


def slot_selector(products, chosen, adapter_id, column_count):
    row_count = products.shape[0]
    selector = (adapter_id[:, None] == chosen[None, :]).astype(jnp.float32)
    reshaped = products.reshape(row_count, chosen.shape[0], column_count)
    return jnp.sum(selector[:, :, None] * reshaped, axis=1)


def widen_rows(values, chosen, adapter_id):
    selector = adapter_id[:, None] == chosen[None, :]
    spread = jnp.where(selector[:, :, None], values[:, None, :], jnp.zeros((), values.dtype))
    return spread.reshape(values.shape[0], chosen.shape[0] * values.shape[1])


def per_device(
    tokens,
    layer_norm_gain,
    layer_norm_bias,
    query_key_weight,
    output_weight,
    up_weight,
    input_bias,
    down_weight,
    output_bias,
    input_adapter_left,
    query_key_value_right,
    up_adapter_right,
    output_adapter_left,
    down_adapter_left,
    output_adapter_right,
    lengths,
    request_adapter,
    slot_adapter,
):
    tok_dev = tokens.shape[0]
    model_width = tokens.shape[1]
    mlp_count = lax.axis_size("mlp")
    tok_grp = tok_dev * mlp_count
    group_first = lax.axis_index("req") * tok_grp
    heads_local = query_key_weight.shape[1]
    hid_local = up_weight.shape[1]
    adapter_ids = slot_adapter.shape[0] * mlp_count
    every_id = lax.iota(jnp.int32, adapter_ids)
    query_key_columns = heads_local * 3 * HEAD_SIZE
    attention_columns = heads_local * HEAD_SIZE
    query_key_rows = query_key_weight.reshape(model_width, query_key_columns)
    normed_rows = normalize(tokens, layer_norm_gain, layer_norm_bias)
    slot_portion = lax.all_gather(normed_rows, "mlp", axis=0, tiled=True)
    grouped = jnp.concatenate(
        [
            rank_product(slot_portion, query_key_rows),
            rank_product(slot_portion, up_weight),
            rank_product(slot_portion, input_adapter_left),
        ],
        axis=1,
    )
    token_index, request, position, adapter_id = token_info(
        lengths, request_adapter, group_first, tok_grp
    )
    rank_part = slot_selector(
        grouped[:, query_key_columns + hid_local :], slot_adapter, adapter_id, 2 * ADAPTER_RANK
    )
    rank_input = lax.psum(rank_part.astype(jnp.bfloat16), "mlp")
    qkv_extra = rank_product(
        widen_rows(rank_input[:, :ADAPTER_RANK], every_id, adapter_id),
        query_key_value_right.reshape(adapter_ids * ADAPTER_RANK, query_key_columns),
    )
    up_delta = rank_product(
        widen_rows(rank_input[:, ADAPTER_RANK:], every_id, adapter_id), up_adapter_right
    )
    projected_rows = (grouped[:, :query_key_columns] + qkv_extra).reshape(
        tok_grp, heads_local, 3 * HEAD_SIZE
    )
    hidden_units = jax.nn.gelu(
        grouped[:, query_key_columns : query_key_columns + hid_local] + up_delta + input_bias,
        approximate=True,
    ).astype(jnp.bfloat16)
    queries = rotate(projected_rows[:, :, :HEAD_SIZE], position).astype(jnp.bfloat16)
    key_rows = (
        rotate(projected_rows[:, :, HEAD_SIZE : 2 * HEAD_SIZE], position)
        .astype(jnp.bfloat16)
        .reshape(tok_grp, attention_columns)
    )
    value_rows = (
        projected_rows[:, :, 2 * HEAD_SIZE :]
        .astype(jnp.bfloat16)
        .reshape(tok_grp, attention_columns)
    )
    paired = jnp.stack([key_rows, value_rows])
    score_scale = HEAD_SIZE ** (-0.5)
    last_row = group_first + tok_grp - 1
    start_state = (
        jnp.full((tok_grp, heads_local), NEGATIVE_FILL, jnp.float32),
        jnp.zeros((tok_grp, heads_local), jnp.float32),
        jnp.zeros((tok_grp, heads_local, HEAD_SIZE), jnp.float32),
    )
    slot_portion = lax.all_gather(paired, "req", axis=1, tiled=True)
    offset = jnp.int32(0)
    amount = slot_portion.shape[1]
    key_index, key_request, key_position, key_adapter = token_info(
        lengths, request_adapter, offset, amount
    )
    useful = jnp.logical_and(offset <= last_row, key_request[amount - 1] >= request[0])

    def attend(current):
        running_top, running_total, running_sum = current
        part_keys = slot_portion[0].reshape(amount, heads_local, HEAD_SIZE)
        part_values = slot_portion[1].reshape(amount, heads_local, HEAD_SIZE)
        scores = (
            jnp.einsum("qhd,khd->qhk", queries, part_keys, preferred_element_type=jnp.float32)
            * score_scale
        )
        allowed = jnp.logical_and(
            key_request[None, :] == request[:, None], key_index[None, :] <= token_index[:, None]
        )[:, None, :]
        masked = jnp.where(allowed, scores, NEGATIVE_FILL)
        new_top = jnp.maximum(running_top, jnp.max(masked, axis=2))
        weights = jnp.where(allowed, jnp.exp(masked - new_top[:, :, None]), 0.0)
        new_total = jnp.sum(weights, axis=2)
        new_sum = jnp.einsum(
            "qhk,khd->qhd",
            weights.astype(jnp.bfloat16),
            part_values,
            preferred_element_type=jnp.float32,
        )
        return (new_top, new_total, new_sum)

    final_state = lax.cond(useful, attend, lambda current: current, start_state)
    attention_output = (
        (final_state[2] / final_state[1][:, :, None])
        .astype(jnp.bfloat16)
        .reshape(tok_grp, attention_columns)
    )
    output_rows = output_weight.reshape(attention_columns, model_width)
    own_ids = lax.axis_index("mlp") * ADP_DEV + lax.iota(jnp.int32, ADP_DEV)
    output_rank_rows = rank_product(
        attention_output, output_adapter_left.reshape(attention_columns, adapter_ids * ADAPTER_RANK)
    )
    down_rank_rows = rank_product(hidden_units, down_adapter_left)
    rank_part_out = jnp.concatenate(
        [
            slot_selector(output_rank_rows, every_id, adapter_id, ADAPTER_RANK),
            slot_selector(down_rank_rows, every_id, adapter_id, ADAPTER_RANK),
        ],
        axis=1,
    )
    rank_output = lax.psum(rank_part_out.astype(jnp.bfloat16), "mlp")
    rank_widened = widen_rows(rank_output, own_ids, adapter_id)
    mixed = lax.psum_scatter(
        (
            rank_product(attention_output, output_rows)
            + (
                rank_product(hidden_units, down_weight)
                + rank_product(rank_widened, output_adapter_right)
            )
        ).astype(jnp.bfloat16),
        "mlp",
        scatter_dimension=0,
        tiled=True,
    ).astype(jnp.float32)
    return (mixed + tokens.astype(jnp.float32) + output_bias).astype(jnp.bfloat16)


def solution(mesh):
    in_specs = (
        P(("req", "mlp"), None),
        P(),
        P(),
        P(None, "mlp", None),
        P("mlp", None, None),
        P(None, "mlp"),
        P("mlp"),
        P("mlp", None),
        P(),
        P(None, "mlp"),
        P(None, "mlp", None),
        P(None, "mlp"),
        P("mlp", None, None),
        P("mlp", None),
        P("mlp", None),
        P(),
        P(),
        P("mlp"),
    )
    out_specs = P(("req", "mlp"), None)
    return jax.shard_map(
        per_device, mesh=mesh, in_specs=in_specs, out_specs=out_specs, check_vma=False
    )
```

profile of v0, /device:TPU:0, one launch (start us, length us, event | category | flops | bytes accessed | tf_op | source)
XLA Modules:
  0.0 493.8 jit_solution(12925493245137740278)
XLA Ops:
  6.5 1.4 convert_reduce_fusion.1
  7.9 1.3 fusion.35
  9.3 2.1 fusion.38
  13.8 6.2 %gather_fusion = s32[1024]{0:T(1024)S(1)} fusion(s32[257]{0:T(512)} %param.36, s32[1024]{0:T(1024)S(1)} %maximum_clamp_fusion), kind=kCustom, calls=%fused_computation | custom fusion | bytes 12288 | tf_op jit(solution)/shard_map/jit(_take)/gather | solution.py:37
  20.8 64.1 %all-gather.3.cloned.1.call-done = bf16[1024,4096]{1,0:T(8,128)(2,1)} async-done(((bf16[64,4096]{1,0:T(8,128)(2,1)}), bf16[1024,4096]{1,0:T(8,128)(2,1)}) %all-gather.3.cloned.1.call-update) | async-done | bytes 8388624 | tf_op jit(solution)/shard_map/all_gather | solution.py:105
  84.9 6.3 %fusion.67 = f32[1024,128]{0,1:T(8,128)S(1)} fusion(bf16[1024,4096]{1,0:T(8,128)(2,1)} %all-gather.3.cloned.1.call-done, bf16[4096,128]{1,0:T(8,128)(2,1)S(1)} %copy-done.2), kind=kOutput, calls=%fused_computation.113 | convolution fusion | flops 1073741824 | bytes 9961472 | tf_op jit(solution)/shard_map/dot_general | solution.py:19
  92.5 80.1 %all-reduce.4.cloned.1.call-done = bf16[1024,32]{0,1:T(8,128)(2,1)} async-done(((bf16[1024,32]{0,1:T(8,128)(2,1)}), bf16[1024,32]{0,1:T(8,128)(2,1)}) %all-reduce.4.cloned.1.call-update) | async-done | bytes 65552 | tf_op jit(solution)/shard_map/psum | solution.py:120
  173.4 1.8 broadcast_select_fusion
  175.2 3.3 fusion.29
  178.5 11.0 %fusion.66 = (bf16[1024,1,768]{0,2,1:T(8,128)(2,1)S(1)}, f32[1024,1,768]{0,2,1:T(8,128)S(1)}) fusion(f32[1024,768]{0,1:T(8,128)S(1)} %fusion.29, bf16[1024,4096]{1,0:T(8,128)(2,1)} %all-gather.3.cloned.1.call-done, bf16[4096,1,768]{2,0,1:T(8,128)(2,1)} %param.23), kind=kOutput, calls=%fused_computation.112 | convolution fusion | flops 6444023808 | bytes 22544384 | tf_op jit(solution)/shard_map/dot_general | solution.py:19
  190.4 2.0 reshape.569
  192.4 1.6 fusion.63
  194.0 2.0 reshape.568
  197.0 2.2 fusion.57
  206.1 2.0 copy.47
  208.2 11.3 %fusion.68 = f32[1024,512]{1,0:T(8,128)} fusion(bf16[1024,4096]{1,0:T(8,128)(2,1)} %all-gather.3.cloned.1.call-done, bf16[4096,512]{1,0:T(8,128)(2,1)} %param.25), kind=kOutput, calls=%fused_computation.114 | convolution fusion | flops 4294967296 | bytes 14680064 | tf_op jit(solution)/shard_map/dot_general | solution.py:19
  220.6 4.5 fusion.24
  225.1 1.3 fusion.70
  226.5 2.4 fusion.16
  228.9 8.3 %fusion.69 = f32[1024,4096]{1,0:T(8,128)} fusion(bf16[1024,512]{1,0:T(8,128)(2,1)S(1)} %fusion.24, bf16[512,4096]{1,0:T(8,128)(2,1)S(1)} %copy-done.9), kind=kOutput, calls=%fused_computation.115 | convolution fusion | flops 4294967296 | bytes 22020096 | tf_op jit(solution)/shard_map/dot_general | solution.py:19
  237.2 14.0 %all-gather.5.cloned.1.call-done = bf16[2,8192,256]{1,2,0:T(8,128)(2,1)} async-done(((bf16[2,1024,256]{1,2,0:T(8,128)(2,1)}), bf16[2,8192,256]{1,2,0:T(8,128)(2,1)}) %all-gather.5.cloned.1.call-update) | async-done | bytes 8388624 | tf_op jit(solution)/shard_map/all_gather | solution.py:154
  251.2 49.0 %conditional.1 = (f32[1024,1]{0,1:T(1,128)S(1)}, f32[1024,1,256]{2,0,1:T(8,128)S(1)}) conditional(s32[]{:T(128)} %convert_element_type.83, () %tuple.13, (s32[8192]{0:T(1024)S(1)}, s32[1024]{0:T(1024)S(1)}, s32[8192]{0:T(1024)S(1)}, s32[]{:T(128)}, s32[1024]{0:T(1024)S(1)}, /*index=5*/bf16[2,8192,256]{1,2,0:T(8,128)(2,1)}, ...), branch_computations={%region_9.10_spmd, %region_10.13_spmd} | conditional | flops 8774483968 | bytes 129753136 | solution.py:185
  251.2 12.0 %copy.45 = bf16[2,8192,256]{2,1,0:T(8,128)(2,1)} copy(bf16[2,8192,256]{1,2,0:T(8,128)(2,1)} %get-tuple-element.65) | data formatting | bytes 16777216 | tf_op jit(solution)/shard_map
  263.2 10.0 %fusion = (f32[1024]{0:T(1024)S(1)}, f32[8192,1024]{1,0:T(8,128)S(1)}) fusion(s32[1024]{0:T(1024)S(1)} %broadcast_add_fusion, s32[1024]{0:T(1024)S(1)} %get-tuple-element.22, s32[8192]{0:T(1024)S(1)} %get-tuple-element.23, s32[8192]{0:T(1024)S(1)} %get-tuple-element.21, bf16[1024,1,256]{0,2,1:T(8,128)(2,1)S(1)} %copy-done.4, bf16[2,8192,256]{2,1,0:T(8,128)(2,1)} %copy.45), kind=kOutput, calls=%fused_computation.4 | convolution fusion | flops 4345297920 | bytes 38350848 | tf_op jit(solution)/shard_map/cond/branch_1_fun/qhd,khd->qhk/dot_general | solution.py:167
  273.2 14.2 %fusion.7 = f32[1024,1,256]{2,0,1:T(8,128)S(1)} fusion(bf16[2,8192,256]{2,1,0:T(8,128)(2,1)} %copy.45, f32[8192,1024]{1,0:T(8,128)S(1)} %get-tuple-element.70, f32[1024]{0:T(1024)S(1)} %broadcast_maximum_fusion, s32[1024]{0:T(1024)S(1)} %broadcast_add_fusion, s32[1024]{0:T(1024)S(1)} %get-tuple-element.22, s32[8192]{0:T(1024)S(1)} %get-tuple-element.23, ...), kind=kOutput, calls=%fused_computation.12 | convolution fusion | flops 4362076160 | bytes 38875136 | tf_op jit(solution)/shard_map/cond/branch_1_fun/qhk,khd->qhd/dot_general | solution.py:177
  287.4 12.8 %fusion.2 = f32[1024]{0:T(1024)S(1)} fusion(f32[8192,1024]{1,0:T(8,128)S(1)} %get-tuple-element.70, f32[1024]{0:T(1024)S(1)} %broadcast_maximum_fusion, s32[1024]{0:T(1024)S(1)} %broadcast_add_fusion, s32[1024]{0:T(1024)S(1)} %get-tuple-element.22, s32[8192]{0:T(1024)S(1)} %get-tuple-element.23, s32[8192]{0:T(1024)S(1)} %get-tuple-element.21), kind=kLoop, calls=%fused_computation.6 | loop fusion | flops 67107840 | bytes 33636352 | tf_op jit(solution)/shard_map/cond/branch_1_fun/reduce_sum | solution.py:176
  300.2 1.9 multiply_reduce_fusion
  302.9 8.1 %fusion.25 = f32[1024,4096]{1,0:T(8,128)} fusion(bf16[1,256,4096]{2,1,0:T(8,128)(2,1)S(1)} %copy-done, f32[1024,1,256]{2,0,1:T(8,128)S(1)} %get-tuple-element.30, f32[1024]{0:T(1024)S(1)} %bitcast.116), kind=kOutput, calls=%fused_computation.37 | convolution fusion | flops 2148007936 | bytes 19927040 | tf_op jit(solution)/shard_map/dot_general | solution.py:19
  311.0 73.2 %all-reduce.6.cloned.1.call-done = bf16[1024,32]{0,1:T(8,128)(2,1)} async-done(((bf16[1024,32]{0,1:T(8,128)(2,1)}), bf16[1024,32]{0,1:T(8,128)(2,1)}) %all-reduce.6.cloned.1.call-update) | async-done | bytes 65552 | tf_op jit(solution)/shard_map/psum | solution.py:204
  385.0 15.6 %add_convert_fusion = bf16[1024,4096]{1,0:T(8,128)(2,1)} fusion(f32[1024,4096]{1,0:T(8,128)} %fusion.25, f32[1024,4096]{1,0:T(8,128)} %fusion.69, bf16[1024,128]{0,1:T(8,128)(2,1)S(1)} %bitcast.112, bf16[128,4096]{1,0:T(8,128)(2,1)} %param.34), kind=kOutput, calls=%fused_computation.19 | convolution fusion | flops 1086324736 | bytes 43253760 | tf_op jit(solution)/shard_map/dot_general | solution.py:19
  400.7 84.6 %reduce-scatter.2.cloned.1.call-done = bf16[64,4096]{1,0:T(8,128)(2,1)} async-done(((bf16[1024,4096]{1,0:T(8,128)(2,1)}), bf16[64,4096]{1,0:T(8,128)(2,1)}) %reduce-scatter.2.cloned.1.call-update) | async-done | bytes 524304 | tf_op jit(solution)/shard_map/reduce_scatter | solution.py:206
  485.3 2.0 fusion.40
  (75 shorter events, 15.5 us)
Async XLA Ops:
  6.5 296.3 %copy-start = (bf16[1,256,4096]{2,1,0:T(8,128)(2,1)S(1)}, bf16[1,256,4096]{2,1,0:T(8,128)(2,1)}, u32[]{:S(2)}) copy-start(bf16[1,256,4096]{2,1,0:T(8,128)(2,1)} %param.24) | copy-start | bytes 6291460
  6.5 13.5 %copy-start.8 = (s32[4]{0:T(128)S(1)}, s32[4]{0:T(128)}, u32[]{:S(2)}) copy-start(s32[4]{0:T(128)} %param.37) | copy-start | bytes 52
  6.5 78.4 %copy-start.2 = (bf16[4096,128]{1,0:T(8,128)(2,1)S(1)}, bf16[4096,128]{1,0:T(8,128)(2,1)}, u32[]{:S(2)}) copy-start(bf16[4096,128]{1,0:T(8,128)(2,1)} %param.29) | copy-start | bytes 3145732
  6.5 78.4 %all-gather.3.cloned.1.call-start = ((), (), s32[]{:S(2)}) async-start(), calls=%async_computation.1 | async-start | bytes 8912896 | tf_op jit(solution)/shard_map/all_gather | solution.py:105
  11.4 161.2 %all-reduce.4.cloned.1.call-start = ((), (), s32[]{:S(2)}) async-start(), calls=%async_computation.2 | async-start | bytes 131072 | tf_op jit(solution)/shard_map/psum | solution.py:120
  91.9 159.3 %all-gather.5.cloned.1.call-start = ((), (), s32[]{:S(2)}) async-start(), calls=%async_computation.3 | async-start | bytes 9437184 | tf_op jit(solution)/shard_map/all_gather | solution.py:154
  202.1 182.1 %all-reduce.6.cloned.1.call-start = ((), (), s32[]{:S(2)}) async-start(), calls=%async_computation.4 | async-start | bytes 131072 | tf_op jit(solution)/shard_map/psum | solution.py:204
  208.2 11.3 %copy-start.5 = (bf16[1024,1,32,1]{0,2,3,1:T(8,128)(2,1)S(1)}, bf16[1024,1,32,1]{0,2,3,1:T(8,128)(2,1)}, u32[]{:S(2)}) copy-start(bf16[1024,1,32,1]{0,2,3,1:T(8,128)(2,1)} %get-tuple-element.75) | copy-start | bytes 196612
  208.2 11.3 %copy-start.6 = (bf16[1024,1,32,1]{0,2,3,1:T(8,128)(2,1)S(1)}, bf16[1024,1,32,1]{0,2,3,1:T(8,128)(2,1)}, u32[]{:S(2)}) copy-start(bf16[1024,1,32,1]{0,2,3,1:T(8,128)(2,1)} %get-tuple-element.76) | copy-start | bytes 196612
  208.2 12.4 %copy-start.11 = (f32[512]{0:T(512)S(1)}, f32[512]{0:T(512)}, u32[]{:S(2)}) copy-start(f32[512]{0:T(512)} %param.26) | copy-start | bytes 6148
  220.6 4.6 copy-start.10
  225.1 1.4 copy-start.3
  225.1 3.8 copy-start.9
  251.2 12.0 %copy-start.4 = (bf16[1024,1,256]{0,2,1:T(8,128)(2,1)S(1)}, bf16[1024,1,256]{0,2,1:T(8,128)(2,1)}, u32[]{:S(2)}) copy-start(bf16[1024,1,256]{0,2,1:T(8,128)(2,1)} %get-tuple-element.66) | copy-start | bytes 1572868 | tf_op jit(solution)/shard_map/cond
  302.8 182.5 %reduce-scatter.2.cloned.1.call-start = ((), (), s32[]{:S(2)}) async-start(), calls=%async_computation.5 | async-start | bytes 8912896 | tf_op jit(solution)/shard_map/reduce_scatter | solution.py:206
  400.6 84.7 %copy-start.1 = (bf16[64,4096]{1,0:T(8,128)(2,1)S(1)}, bf16[64,4096]{1,0:T(8,128)(2,1)}, u32[]{:S(2)}) copy-start(bf16[64,4096]{1,0:T(8,128)(2,1)} %param.20) | copy-start | bytes 1572868
  400.6 84.7 %copy-start.7 = (f32[4096]{0:T(1024)S(1)}, f32[4096]{0:T(1024)}, u32[]{:S(2)}) copy-start(f32[4096]{0:T(1024)} %param.28) | copy-start | bytes 49156
Sparse Core Ops, SparseCore 0:
  11.5 73.3 all-gather.2
  92.0 80.5 all-reduce.3
  202.2 48.9 all-gather.4
  302.9 81.1 all-reduce.5
  400.8 84.4 reduce-scatter.1
where the time goes:
time: 495 us; the launch traced here: 494 us
  waiting for transfers between devices  316 us (64%)
  matrix products  95.9 us (19%)
  other arithmetic  34.2 us (7%)
  local copies, waits for them, and re-layouts  32.5 us (7%)
  between operations  14.7 us (3%)
    reduce_scatter x1, waiting for transfers between devices, per_device(): lax.psum_scatter((rank_product(attention_output, output_rows) + (rank_pro...  84.6 us
    psum x1, waiting for transfers between devices, per_device(): rank_input = lax.psum(rank_part.astype(jnp.bfloat16), 'mlp')  80.1 us
    psum x1, waiting for transfers between devices, per_device(): rank_output = lax.psum(rank_part_out.astype(jnp.bfloat16), 'mlp')  73.2 us
    dot_general x10, matrix products, rank_product(): return jnp.dot(left_side, right_side, preferred_element_type=jnp.float32)  71.7 us
    all_gather x1, waiting for transfers between devices, per_device(): slot_portion = lax.all_gather(normed_rows, 'mlp', axis=0, tiled=True)  64.1 us
    dot_general x1, matrix products, attend(): jnp.einsum('qhk,khd->qhd', weights.astype(jnp.bfloat16), part_values, pre...  14.2 us
    all_gather x1, waiting for transfers between devices, per_device(): slot_portion = lax.all_gather(paired, 'req', axis=1, tiled=True)  14 us
    reduce_sum x1, other arithmetic, attend(): new_total = jnp.sum(weights, axis=2)  12.8 us
  transfers between devices with their start and end apart: 5, of which 5 were waited for; matrix products, arithmetic and copies ran while one was open for 10% of the time, Pallas kernels for 0%

commit v1 on v0

v1 whole, which is shorter than its diff:
```python
import functools
import math

import jax
import jax.numpy as jnp
from jax import lax
from jax.experimental import pallas as pl
from jax.experimental.pallas import tpu as pltpu
from jax.sharding import PartitionSpec as P

HEAD = 256
ROT = 64
RANK = 16
EPSILON = 1e-05
NEGATIVE_FILL = -1e30
MESH = pl.DeviceIdType.MESH
F32 = jnp.float32
BF16 = jnp.bfloat16
VMEM_LIMIT = 60 * 1024 * 1024
SIDE = 4
GROUP = 16
UNIT = 16
QKV = 3 * HEAD


def dot(a, b):
    return jnp.dot(a, b, preferred_element_type=F32)


class Plane:
    def __init__(self):
        self.me = lax.axis_index("mlp")
        self.z = self.me // SIDE
        self.y = self.me % SIDE

    def at(self, dz, dy):
        return ((self.z + dz + SIDE) % SIDE) * SIDE + (self.y + dy + SIDE) % SIDE

    def off(self, half, d1, d2):
        return self.at(d1, d2) if half == 0 else self.at(d2, d1)

    def source(self, half, d1, d2):
        return self.off(half, -d1, -d2)


def barrier_all(me, count):
    sem = pltpu.get_barrier_semaphore()
    for k in range(1, count):
        pl.semaphore_signal(sem, inc=1, device_id={"mlp": (me + k) % count}, device_id_type=MESH)
    return sem


def exchange_sum(me, packed, landed, full, sems):
    def scatter(k, carry):
        to = (me + k) % GROUP
        pltpu.make_async_remote_copy(
            packed.at[to], landed.at[me], sems.at[0], sems.at[1], device_id={"mlp": to}, device_id_type=MESH
        ).start()
        return carry

    lax.fori_loop(1, GROUP, scatter, 0)
    landed[me] = packed[me]
    many = landed.at[pl.ds(0, GROUP - 1)]
    pltpu.make_async_copy(many, many, sems.at[1]).wait()
    full[me] = jnp.sum(landed[...].astype(F32), axis=0).astype(BF16)

    def gather(k, carry):
        to = (me + k) % GROUP
        pltpu.make_async_remote_copy(
            full.at[me], full.at[me], sems.at[2], sems.at[3], device_id={"mlp": to}, device_id_type=MESH
        ).start()
        return carry

    lax.fori_loop(1, GROUP, gather, 0)
    pltpu.make_async_copy(many, many, sems.at[0]).wait()
    return many


def exchange_wait(many, sems):
    pltpu.make_async_copy(many, many, sems.at[3]).wait()
    pltpu.make_async_copy(many, many, sems.at[2]).wait()


GATHER_GROUPS = (
    tuple((h, d1, 0) for h in (0, 1) for d1 in (0, 1, -1, 2)),
    tuple((h, d1, d2) for h in (0, 1) for d1 in (0, 1) for d2 in (1, -1)),
    tuple((h, d1, d2) for h in (0, 1) for d1 in (-1, 2) for d2 in (1, -1)),
    tuple((h, d1, 2) for h in (0, 1) for d1 in (0, 1, -1, 2)),
)


def input_kernel(
    tokens, gain, bias, in_bias, adapter, slots, cosine, sine, w_qkv, w_up, w_left, w_qkv_right, w_up_right,
    out_qkv, out_hidden,
    xs, weights, right_qkv, right_up, rows_in, acc, picked, packed, landed, full,
    load_sems, send_sem, recv_sems, ex_sems,
):
    plane = Plane()
    me = plane.me
    hid = w_up.shape[1]
    loads = [
        pltpu.make_async_copy(w_qkv, weights.at[:, pl.ds(0, QKV)], load_sems.at[0]),
        pltpu.make_async_copy(w_up, weights.at[:, pl.ds(QKV, hid)], load_sems.at[1]),
        pltpu.make_async_copy(w_left, weights.at[:, pl.ds(QKV + hid, 128)], load_sems.at[2]),
        pltpu.make_async_copy(w_qkv_right, right_qkv, load_sems.at[3]),
        pltpu.make_async_copy(w_up_right, right_up, load_sems.at[4]),
    ]
    for load in loads:
        load.start()
    sem = barrier_all(me, GROUP)
    for part in range(0, 64, 16):
        values = tokens[part : part + 16, :].astype(F32)
        center = values - jnp.mean(values, axis=1, keepdims=True)
        spread = jnp.mean(center * center, axis=1, keepdims=True)
        scaled = center * lax.rsqrt(spread + EPSILON)
        xs[me, part : part + 16, :] = (scaled * gain[...] + bias[...]).astype(BF16)
    pl.semaphore_wait(sem, GROUP - 1)

    def send(slot, half, units, axis, step):
        first, count = units
        rows = pl.ds(half * 32 + first * UNIT, count * UNIT)
        to = plane.off(half, step, 0) if axis == 1 else plane.off(half, 0, step)
        pltpu.make_async_remote_copy(
            xs.at[slot, rows, :], xs.at[slot, rows, :], send_sem, recv_sems.at[slot, half * 2 + first],
            device_id={"mlp": to}, device_id_type=MESH,
        ).start()

    def landed_piece(half, d1, d2, units):
        first, count = units
        slot = plane.source(half, d1, d2)
        rows = pl.ds(half * 32 + first * UNIT, count * UNIT)
        view = xs.at[slot, rows, :]
        pltpu.make_async_copy(view, view, recv_sems.at[slot, half * 2 + first]).wait()
        return slot

    whole = (0, 2)
    for half in (0, 1):
        for step in (1, -1):
            send(me, half, whole, 1, step)
    for half in (0, 1):
        for step in (1, -1):
            send(me, half, whole, 2, step)
    for half in (0, 1):
        for d1 in (1, -1):
            slot = landed_piece(half, d1, 0, whole)
            send(slot, half, (0, 1) if d1 == 1 else (1, 1), 1, d1)
            for step in (1, -1):
                send(slot, half, whole, 2, step)

    def relay(half, d1, d2, pieces):
        for units in pieces:
            slot = landed_piece(half, d1, d2, units)
        send(slot, half, (0, 1) if d2 == 1 else (1, 1), 2, d2)

    def multiply(number):
        places = []
        for i, (half, d1, d2) in enumerate(GATHER_GROUPS[number]):
            slot = plane.source(half, d1, d2)
            rows_in[i * 32 : (i + 1) * 32, :] = xs[slot, pl.ds(half * 32, 32), :]
            places.append((slot, half))

        left = dot(rows_in[...], weights[:, QKV + hid :])
        for i, (slot, half) in enumerate(places):
            for u in (0, 1):
                unit = half * 2 + u
                at = i * 32 + u * UNIT
                picked[slot, unit] = left[at : at + UNIT, :].astype(BF16)

    def multiply_wide(number):
        def column(n, carry):
            columns = pl.ds(pl.multiple_of(n * 256, 256), 256)
            result = dot(rows_in[...], weights[:, columns])
            for i, (half, d1, d2) in enumerate(GATHER_GROUPS[number]):
                slot = plane.source(half, d1, d2)
                for u in (0, 1):
                    at = i * 32 + u * UNIT
                    acc[slot, half * 2 + u, :, columns] = result[at : at + UNIT, :]
            return carry

        lax.fori_loop(0, (QKV + hid) // 256, column, 0)

    for load in loads[:3]:
        load.wait()
    for half in (0, 1):
        for d2 in (1, -1):
            relay(half, 0, d2, (whole,))
    for half in (0, 1):
        for unit in ((0, 1), (1, 1)):
            slot = landed_piece(half, 2, 0, unit)
            for step in (1, -1):
                send(slot, half, unit, 2, step)
    multiply(0)
    multiply_wide(0)
    for half in (0, 1):
        for d1 in (1, -1):
            for d2 in (1, -1):
                relay(half, d1, d2, (whole,))
    multiply(1)
    multiply_wide(1)
    for half in (0, 1):
        for d2 in (1, -1):
            relay(half, 2, d2, ((0, 1), (1, 1)))
    multiply(2)
    multiply_wide(2)
    for half in (0, 1):
        for d1 in (0, 1, -1, 2):
            for unit in ((0, 1), (1, 1)):
                landed_piece(half, d1, 2, unit)
    multiply(3)

    lane = lax.broadcasted_iota(jnp.int32, (1, 128), 1)
    chosen = jnp.where(lane < 32, slots[0], jnp.where(lane < 64, slots[1], jnp.where(lane < 96, slots[2], slots[3])))
    row_id = lax.broadcasted_iota(jnp.int32, (128, 128), 0)
    col_id = lax.broadcasted_iota(jnp.int32, (128, 128), 1)
    together = jnp.zeros((256, 128), F32)
    for unit in range(4):
        mine = adapter[:, unit].reshape(256, 1) == chosen
        kept = jnp.where(mine, picked[:, unit].reshape(256, 128).astype(F32), 0.0).astype(BF16)
        fold = jnp.logical_and(col_id // 32 == unit, row_id % 32 == col_id % 32).astype(F32).astype(BF16)
        together = together + dot(kept, fold)
    packed[...] = together.astype(BF16).reshape(GROUP, UNIT, 128)
    many = exchange_sum(me, packed, landed, full, ex_sems)
    multiply_wide(3)
    exchange_wait(many, ex_sems)
    sent = xs.at[pl.ds(0, GROUP - 1)]
    pltpu.make_async_copy(sent, sent, send_sem).wait()
    for load in loads[3:]:
        load.wait()

    lane = lax.broadcasted_iota(jnp.int32, (1, 1024), 1)
    row_id = lax.broadcasted_iota(jnp.int32, (128, 1024), 0)
    col_id = lax.broadcasted_iota(jnp.int32, (128, 1024), 1)
    even = lax.broadcasted_iota(jnp.int32, (1, 128), 1) % 2 == 0

    def finish(unit, carry):
        ranks = full[...].reshape(256, 128)
        mine = adapter[:, unit].reshape(256, 1) == lane // RANK

        def widened(first):
            spread = (row_id == unit * 32 + first + col_id % RANK).astype(F32).astype(BF16)
            return jnp.where(mine, dot(ranks, spread), 0.0).astype(BF16)

        wide = widened(0)
        turn = cosine[:, unit].reshape(256, 128)
        sway = sine[:, unit].reshape(256, 128)
        for part in range(3):
            columns = slice(part * HEAD, (part + 1) * HEAD)
            value = acc[:, unit, :, columns].reshape(256, HEAD) + dot(wide, right_qkv[:, columns])
            if part < 2:
                head = value[:, :128]
                swapped = jnp.where(even, pltpu.roll(head, 127, 1), pltpu.roll(head, 1, 1))
                value = jnp.concatenate([head * turn + swapped * sway, value[:, 128:]], axis=1)
            out_qkv[:, unit, :, columns] = value.astype(BF16).reshape(GROUP, UNIT, HEAD)
        wide = widened(RANK)
        for part in range(hid // 256):
            columns = slice(part * 256, (part + 1) * 256)
            value = acc[:, unit, :, QKV + part * 256 : QKV + (part + 1) * 256].reshape(256, 256)
            value = value + dot(wide, right_up[:, columns]) + in_bias[:, columns]
            value = jax.nn.gelu(value, approximate=True)
            out_hidden[:, unit, :, columns] = value.astype(BF16).reshape(GROUP, UNIT, 256)
        return carry

    lax.fori_loop(0, 4, finish, 0)


def attend_kernel(first_chunk, queries, keys_values, starts, out, top, total, summed, *, chunk):
    block = queries.shape[0]
    number = pl.program_id(0)
    req = lax.axis_index("req")
    rows = keys_values.shape[1]
    first_row = req * rows + number * block
    per = rows // chunk
    top[...] = jnp.full_like(top, NEGATIVE_FILL)
    total[...] = jnp.zeros_like(total)
    summed[...] = jnp.zeros_like(summed)
    scaled = queries[...] * jnp.asarray(HEAD ** (-0.5), BF16)
    row_id = first_row + lax.broadcasted_iota(jnp.int32, (block, 1), 0)
    begin = starts[...]
    lane = lax.broadcasted_iota(jnp.int32, (1, chunk), 1)

    def step(c, carry):
        slot = req - c // per
        at = pl.ds(pl.multiple_of((c % per) * chunk, chunk), chunk)
        keys = keys_values[slot, at, :HEAD]
        values = keys_values[slot, at, HEAD:]
        scores = lax.dot_general(scaled, keys, (((1,), (1,)), ((), ())), preferred_element_type=F32)
        key_id = c * chunk + lane
        allowed = jnp.logical_and(key_id >= begin, key_id <= row_id)
        masked = jnp.where(allowed, scores, NEGATIVE_FILL)
        new_top = jnp.maximum(top[...], jnp.max(masked, axis=1, keepdims=True))
        weights = jnp.where(allowed, jnp.exp(masked - new_top), 0.0)
        decay = jnp.exp(top[...] - new_top)
        total[...] = total[...] * decay + jnp.sum(weights, axis=1, keepdims=True)
        summed[...] = summed[...] * decay + dot(weights.astype(BF16), values)
        top[...] = new_top
        return carry

    lax.fori_loop(first_chunk[number], (first_row + block - 1) // chunk + 1, step, 0)
    out[...] = (summed[...] / total[...]).astype(BF16)


REDUCE_GROUPS = (
    tuple((h, d1, 2) for h in (0, 1) for d1 in (2, 1, -1, 0)),
    tuple((h, d1, d2) for h in (0, 1) for d1 in (2, 1) for d2 in (1, -1)),
    tuple((h, d1, d2) for h in (0, 1) for d1 in (-1, 0) for d2 in (1, -1)),
    tuple((h, d1, 0) for h in (0, 1) for d1 in (2, 1, -1, 0)),
)
FAR = {2: 0, 1: 1, -1: 2, 0: 3}


def output_kernel(
    attended, hidden, adapter, tokens, out_bias, w_left_attn, w_left_hid, w_attn, w_down, w_right,
    out,
    inputs, left, weights, part, from2, from1, rows_in, packed, landed, full,
    load_sems, send_sem, sems2, sems1, ex_sems,
):
    plane = Plane()
    me = plane.me
    hid = w_left_hid.shape[0]
    depth = HEAD + hid
    loads = [
        pltpu.make_async_copy(attended, inputs.at[:, :, :, pl.ds(0, HEAD)], load_sems.at[0]),
        pltpu.make_async_copy(hidden, inputs.at[:, :, :, pl.ds(HEAD, hid)], load_sems.at[1]),
        pltpu.make_async_copy(w_left_attn, left.at[pl.ds(0, HEAD)], load_sems.at[2]),
        pltpu.make_async_copy(w_left_hid, left.at[pl.ds(HEAD, hid)], load_sems.at[3]),
        pltpu.make_async_copy(w_attn, weights.at[pl.ds(0, HEAD)], load_sems.at[4]),
        pltpu.make_async_copy(w_down, weights.at[pl.ds(HEAD, hid)], load_sems.at[5]),
        pltpu.make_async_copy(w_right, weights.at[pl.ds(depth, 128)], load_sems.at[6]),
    ]
    for load in loads:
        load.start()
    sem = barrier_all(me, GROUP)
    for load in loads[:4]:
        load.wait()

    lane = lax.broadcasted_iota(jnp.int32, (1, 1024), 1)
    fold_row = lax.broadcasted_iota(jnp.int32, (1024, 128), 0)
    fold_col = lax.broadcasted_iota(jnp.int32, (1024, 128), 1)

    def lower(unit, together):
        mine = adapter[:, unit].reshape(256, 1) == lane // RANK
        for first, begin, end in ((0, 0, HEAD), (RANK, HEAD, depth)):
            product = dot(inputs[:, unit, :, begin:end].reshape(256, end - begin), left[begin:end, :])
            kept = jnp.where(mine, product, 0.0).astype(BF16)
            fold = (fold_col == unit * 32 + first + fold_row % RANK).astype(F32).astype(BF16)
            together = together + dot(kept, fold)
        return together

    together = lax.fori_loop(0, 4, lower, jnp.zeros((256, 128), F32))
    packed[...] = together.astype(BF16).reshape(GROUP, UNIT, 128)
    pl.semaphore_wait(sem, GROUP - 1)
    many = exchange_sum(me, packed, landed, full, ex_sems)
    for load in loads[4:]:
        load.wait()
    exchange_wait(many, ex_sems)
    lane = lax.broadcasted_iota(jnp.int32, (1, 128), 1)
    row_id = lax.broadcasted_iota(jnp.int32, (128, 128), 0)
    col_id = lax.broadcasted_iota(jnp.int32, (128, 128), 1)
    for unit in range(4):
        mine = adapter[:, unit].reshape(256, 1) == me * 4 + lane // 32
        spread = (row_id == unit * 32 + col_id % 32).astype(F32).astype(BF16)
        wide = jnp.where(mine, dot(full[...].reshape(256, 128), spread), 0.0).astype(BF16)
        inputs[:, unit, :, depth:] = wide.reshape(GROUP, UNIT, 128)

    def multiply(number):
        for i, (half, d1, d2) in enumerate(REDUCE_GROUPS[number]):
            slot = plane.source(half, d1, d2)
            for u in (0, 1):
                at = i * 32 + u * UNIT
                rows_in[at : at + UNIT, :] = inputs[slot, half * 2 + u]

        def column(n, carry):
            columns = pl.ds(pl.multiple_of(n * 256, 256), 256)
            result = dot(rows_in[...], weights[:, columns]).astype(BF16)
            for i, (half, d1, d2) in enumerate(REDUCE_GROUPS[number]):
                slot = plane.source(half, d1, d2)
                part[slot, pl.ds(half * 32, 32), columns] = result[i * 32 : (i + 1) * 32, :]
            return carry

        lax.fori_loop(0, out.shape[1] // 256, column, 0)

    def rows_of(half, u):
        return pl.ds(half * 32 + u * UNIT, UNIT)

    def landing(half, axis, side, d1, place):
        index = half * 2 + side
        if axis == 2:
            return from2.at[index, FAR[d1], place], sems2.at[index, FAR[d1] * 3 + place]
        return from1.at[index, place], sems1.at[index, place]

    def send(half, d1, d2, u, axis):
        d = d2 if axis == 2 else d1
        back = d if d != 2 else (1 if u == 0 else -1)
        side = 0 if back == 1 else 1
        place = 2 if d == 2 else u
        slot = plane.source(half, d1, d2)
        to = plane.off(half, 0, -back) if axis == 2 else plane.off(half, -back, 0)
        target, arrived = landing(half, axis, side, d1, place)
        pltpu.make_async_remote_copy(
            part.at[slot, rows_of(half, u), :], target, send_sem, arrived, device_id={"mlp": to}, device_id_type=MESH
        ).start()

    def arrive(half, axis, side, d1, place):
        ref, arrived = landing(half, axis, side, d1, place)
        pltpu.make_async_copy(ref, ref, arrived).wait()
        return ref

    def add(half, d1, d2, u, children):
        refs = [arrive(half, axis, side, d1, place) for axis, side, place in children]
        slot = plane.source(half, d1, d2)
        here = part.at[slot, rows_of(half, u), :]
        value = here[...].astype(F32)
        for ref in refs:
            value = value + ref[...].astype(F32)
        here[...] = value.astype(BF16)

    multiply(0)
    for d1 in (2, 1, -1, 0):
        for half in (0, 1):
            for u in (0, 1):
                send(half, d1, 2, u, 2)
    for number in (1, 2):
        multiply(number)
        for half, d1, d2 in REDUCE_GROUPS[number]:
            send(half, d1, d2, 1 if d2 == 1 else 0, 2)
    for number in (1, 2):
        for half, d1, d2 in REDUCE_GROUPS[number]:
            u = 0 if d2 == 1 else 1
            add(half, d1, d2, u, ((2, 0 if d2 == 1 else 1, 2),))
            send(half, d1, d2, u, 2)
    multiply(3)
    both = lambda u: ((2, 0, u), (2, 1, u))
    for half in (0, 1):
        for u in (0, 1):
            add(half, 2, 0, u, both(u))
            send(half, 2, 0, u, 1)
    for d1 in (1, -1):
        for half in (0, 1):
            u = 1 if d1 == 1 else 0
            add(half, d1, 0, u, both(u))
            send(half, d1, 0, u, 1)
    for d1 in (1, -1):
        for half in (0, 1):
            u = 0 if d1 == 1 else 1
            add(half, d1, 0, u, both(u) + ((1, 0 if d1 == 1 else 1, 2),))
            send(half, d1, 0, u, 1)
    for half in (0, 1):
        for u in (0, 1):
            refs = [arrive(half, axis, side, 0, place) for axis, side, place in both(u) + ((1, 0, u), (1, 1, u))]
            rows = rows_of(half, u)
            value = part[me, rows, :].astype(F32)
            for ref in refs:
                value = value + ref[...].astype(F32)
            out[rows, :] = (value + tokens[rows, :].astype(F32) + out_bias[...]).astype(BF16)
    sent = part.at[pl.ds(0, GROUP - 1)]
    pltpu.make_async_copy(sent, sent, send_sem).wait()


def per_device(
    tokens, layer_norm_gain, layer_norm_bias, query_key_weight, output_weight, up_weight, input_bias, down_weight,
    output_bias, input_adapter_left, query_key_value_right, up_adapter_right, output_adapter_left, down_adapter_left,
    output_adapter_right, lengths, request_adapter, slot_adapter,
):
    rows, width = tokens.shape
    group_rows = rows * GROUP
    req = lax.axis_index("req")
    hid = up_weight.shape[1]

    ends = jnp.cumsum(lengths)
    begins = ends - lengths
    index = req * group_rows + lax.iota(jnp.int32, group_rows)
    inside = jnp.logical_and(begins[None, :] <= index[:, None], index[:, None] < ends[None, :])
    start = jnp.sum(jnp.where(inside, begins[None, :], 0), axis=1)
    adapter = jnp.sum(jnp.where(inside, request_adapter[None, :], 0), axis=1)
    lane = lax.iota(jnp.int32, 128)
    frequency = jnp.exp((lane // 2).astype(F32) * (-2.0 * math.log(10000.0) / ROT))
    angle = (index - start).astype(F32)[:, None] * frequency[None, :]
    turned = (lane < ROT)[None, :]
    cosine = jnp.where(turned, jnp.cos(angle), 1.0)
    sine = jnp.where(turned, jnp.where(lane % 2 == 0, -1.0, 1.0)[None, :] * jnp.sin(angle), 0.0)

    vmem = pl.BlockSpec(memory_space=pltpu.VMEM)
    smem = pl.BlockSpec(memory_space=pltpu.SMEM)
    anywhere = pl.BlockSpec(memory_space=pl.ANY)
    dma = pltpu.SemaphoreType.DMA
    by_unit = (GROUP, 4, UNIT)
    adapter_units = adapter.reshape(by_unit + (1,))
    qkv, hidden = pl.pallas_call(
        input_kernel,
        out_shape=(
            jax.ShapeDtypeStruct(by_unit + (QKV,), BF16),
            jax.ShapeDtypeStruct(by_unit + (hid,), BF16),
        ),
        in_specs=[vmem] * 5 + [smem] + [vmem] * 2 + [anywhere] * 5,
        out_specs=(vmem, vmem),
        scratch_shapes=[
            pltpu.VMEM((GROUP, rows, width), BF16),
            pltpu.VMEM((width, QKV + hid + 128), BF16),
            pltpu.VMEM(query_key_value_right.shape[:1] + (QKV,), BF16),
            pltpu.VMEM(up_adapter_right.shape, BF16),
            pltpu.VMEM((256, width), BF16),
            pltpu.VMEM(by_unit + (QKV + hid,), F32),
            pltpu.VMEM(by_unit + (128,), BF16),
            pltpu.VMEM((GROUP, UNIT, 128), BF16),
            pltpu.VMEM((GROUP, UNIT, 128), BF16),
            pltpu.VMEM((GROUP, UNIT, 128), BF16),
            dma((5,)),
            dma,
            dma((GROUP, 4)),
            dma((4,)),
        ],
        compiler_params=pltpu.CompilerParams(
            collective_id=0, has_side_effects=True, vmem_limit_bytes=VMEM_LIMIT
        ),
        name="input_stage",
    )(
        tokens, layer_norm_gain[None, :], layer_norm_bias[None, :], input_bias[None, :], adapter_units, slot_adapter,
        cosine.reshape(by_unit + (128,)), sine.reshape(by_unit + (128,)),
        query_key_weight.reshape(width, QKV), up_weight, input_adapter_left,
        query_key_value_right.reshape(-1, QKV), up_adapter_right,
    )
    qkv = qkv.reshape(group_rows, QKV)

    gathered = lax.all_gather(qkv[:, HEAD:], "req", axis=0)
    slots = jnp.maximum(req - lax.iota(jnp.int32, 5), 0)
    window = jnp.stack([lax.dynamic_index_in_dim(gathered, slots[i], 0, keepdims=False) for i in range(5)])

    block, chunk = 256, 512
    blocks = group_rows // block
    first_chunk = start.reshape(blocks, block)[:, 0] // chunk
    attended = pl.pallas_call(
        functools.partial(attend_kernel, chunk=chunk),
        out_shape=jax.ShapeDtypeStruct((group_rows, HEAD), BF16),
        grid_spec=pltpu.PrefetchScalarGridSpec(
            num_scalar_prefetch=1,
            grid=(blocks,),
            in_specs=[
                pl.BlockSpec((block, HEAD), lambda i, s: (i, 0)),
                pl.BlockSpec((5, group_rows, 2 * HEAD), lambda i, s: (0, 0, 0), pipeline_mode=pl.Buffered(1)),
                pl.BlockSpec((block, 1), lambda i, s: (i, 0)),
            ],
            out_specs=pl.BlockSpec((block, HEAD), lambda i, s: (i, 0)),
            scratch_shapes=[
                pltpu.VMEM((block, 1), F32),
                pltpu.VMEM((block, 1), F32),
                pltpu.VMEM((block, HEAD), F32),
            ],
        ),
        compiler_params=pltpu.CompilerParams(vmem_limit_bytes=VMEM_LIMIT),
        name="attend_stage",
    )(first_chunk, qkv[:, :HEAD], window, start[:, None])

    depth = HEAD + hid + 128
    return pl.pallas_call(
        output_kernel,
        out_shape=jax.ShapeDtypeStruct((rows, width), BF16),
        in_specs=[anywhere] * 2 + [vmem] * 3 + [anywhere] * 5,
        out_specs=vmem,
        scratch_shapes=[
            pltpu.VMEM(by_unit + (depth,), BF16),
            pltpu.VMEM((HEAD + hid, 1024), BF16),
            pltpu.VMEM((depth, width), BF16),
            pltpu.VMEM((GROUP, rows, width), BF16),
            pltpu.VMEM((4, 4, 3, UNIT, width), BF16),
            pltpu.VMEM((4, 3, UNIT, width), BF16),
            pltpu.VMEM((256, depth), BF16),
            pltpu.VMEM((GROUP, UNIT, 128), BF16),
            pltpu.VMEM((GROUP, UNIT, 128), BF16),
            pltpu.VMEM((GROUP, UNIT, 128), BF16),
            dma((7,)),
            dma,
            dma((4, 12)),
            dma((4, 3)),
            dma((4,)),
        ],
        compiler_params=pltpu.CompilerParams(
            collective_id=1, has_side_effects=True, vmem_limit_bytes=VMEM_LIMIT
        ),
        name="output_stage",
    )(
        attended.reshape(by_unit + (HEAD,)), hidden, adapter_units, tokens, output_bias[None, :],
        output_adapter_left.reshape(HEAD, -1), down_adapter_left, output_weight.reshape(HEAD, width), down_weight,
        output_adapter_right,
    )


def solution(mesh):
    in_specs = (
        P(("req", "mlp"), None), P(), P(), P(None, "mlp", None), P("mlp", None, None), P(None, "mlp"), P("mlp"),
        P("mlp", None), P(), P(None, "mlp"), P(None, "mlp", None), P(None, "mlp"), P("mlp", None, None),
        P("mlp", None), P("mlp", None), P(), P(), P("mlp"),
    )
    return jax.shard_map(
        per_device, mesh=mesh, in_specs=in_specs, out_specs=P(("req", "mlp"), None), check_vma=False
    )
```

time: 495 us -> 248 us (0.50)
  the two profiles are of different devices: /device:TPU:0 before, /device:TPU:3 now
where the time goes in v1:
time: 248 us
  Pallas kernels  160 us (65%)
  waiting for transfers between devices  37.7 us (15%)
  between operations  22.3 us (9%)
  local copies, waits for them, and re-layouts  21.4 us (9%)
  other arithmetic  5.78 us (2%)
    pallas_call x1, Pallas kernels, per_device(): pl.pallas_call(input_kernel, out_shape=(jax.ShapeDtypeStruct(by_unit + (Q...  66.8 us
    pallas_call x1, Pallas kernels, per_device(): pl.pallas_call(output_kernel, out_shape=jax.ShapeDtypeStruct((rows, width...  65.1 us
    all_gather x1, waiting for transfers between devices, per_device(): gathered = lax.all_gather(qkv[:, HEAD:], 'req', axis=0)  37.7 us
    pallas_call x1, Pallas kernels, per_device(): pl.pallas_call(functools.partial(attend_kernel, chunk=chunk), out_shape=j...  28.6 us
    unnamed x5, local copies, waits for them, and re-layouts  11 us
  transfers between devices with their start and end apart: 1, of which 1 were waited for; matrix products, arithmetic and copies ran while one was open for 2% of the time, Pallas kernels for 0%

profile of v1, /device:TPU:3, one launch (start us, length us, event | category | flops | bytes accessed | tf_op | source)
XLA Modules:
  0.0 247.7 jit_solution(6829711879945702180)
XLA Ops:
  6.5 0.0 all-gather.3.cloned.1.call-start
  6.6 0.7 pad_bitcast_fusion
  7.3 0.3 reduce-window.9
  7.6 0.1 slice.34
  7.7 0.1 slice_reduce_fusion.1
  7.8 0.1 add_bitcast_fusion
  7.9 0.7 slice_subtract_fusion
  8.6 1.0 select_reduce_fusion
  9.5 1.1 reshape.131.adapter
  10.7 0.1 reduce_sum.24
  10.8 3.1 %fusion.2 = (f32[16,4,16,128]{3,2,1,0:T(8,128)}, f32[16,4,16,128]{3,2,1,0:T(8,128)}) fusion(f32[128]{0:T(128)S(1)} %get-tuple-element.20, f32[128]{0:T(128)S(1)} %get-tuple-element.21, f32[16,4,16]{2,1,0:T(4,128)S(1)} %subtract_convert_fusion, pred[128]{0:T(512)(128)(4,1)S(1)} %iota_compare_fusion), kind=kLoop, calls=%fused_computation.12 | loop fusion | flops 524288 | bytes 1053824 | tf_op jit(solution)/shard_map/jit(_where)/select_n | solution.py:480
  13.9 66.8 %input_stage.1 = (bf16[16,4,16,768]{3,2,1,0:T(8,128)(2,1)}, bf16[16,4,16,512]{3,2,1,0:T(8,128)(2,1)}) custom-call(bf16[64,4096]{1,0:T(8,128)(2,1)} %tokens.3, f32[1,4096]{1,0:T(1,128)} %bitcast.34, f32[1,4096]{1,0:T(1,128)} %bitcast.35, f32[1,512]{1,0:T(1,128)} %bitcast.37, s32[16,4,16,1]{3,2,1,0:T(8,128)} %reshape.131.adapter, s32[4]{0:T(128)} %slots.1, ...), custom_call_target="tpu_custom_call" | custom-call | tf_op jit(solution)/shard_map/input_stage/pallas_call | solution.py:488
  80.7 2.3 slice.47
  83.0 0.0 all-gather.3.cloned.1.call-update
  83.0 1.9 slice.46.queries
  84.9 0.6 fusion.6
  91.4 1.0 copy.26.starts
  95.4 0.1 slice_reduce_fusion
  95.5 0.6 and_select_fusion.2.first_chunk
  96.0 37.7 %all-gather.3.cloned.1.call-done = bf16[8192,512]{1,0:T(8,128)(2,1)} async-done(((bf16[1024,512]{1,0:T(8,128)(2,1)}), bf16[8192,512]{1,0:T(8,128)(2,1)}) %all-gather.3.cloned.1.call-update) | async-done | bytes 8388624 | tf_op jit(solution)/shard_map/all_gather | solution.py:524
  133.8 2.4 dynamic-slice_dynamic-update-slice_fusion.4
  136.1 2.3 dynamic-slice_dynamic-update-slice_fusion.3
  138.4 2.3 dynamic-slice_dynamic-update-slice_fusion.2
  140.6 2.3 dynamic-slice_dynamic-update-slice_fusion.1
  142.9 2.3 dynamic-slice_dynamic-update-slice_fusion.keys_values
  145.3 28.6 %attend_stage.1 = bf16[1024,256]{1,0:T(8,128)(2,1)} custom-call(s32[4]{0:T(128)} %and_select_fusion.2.first_chunk, bf16[1024,256]{1,0:T(8,128)(2,1)} %slice.46.queries, bf16[5,1024,512]{2,1,0:T(8,128)(2,1)} %dynamic-slice_dynamic-update-slice_fusion.keys_values, s32[1024,1]{1,0:T(8,128)} %copy.26.starts), custom_call_target="tpu_custom_call" | custom-call | tf_op jit(solution)/shard_map/attend_stage/pallas_call | solution.py:531
  173.8 65.1 %output_stage.1 = bf16[64,4096]{1,0:T(8,128)(2,1)} custom-call(bf16[16,4,16,256]{3,2,1,0:T(8,128)(2,1)} %bitcast.28, bf16[16,4,16,512]{3,2,1,0:T(8,128)(2,1)} %get-tuple-element.8.hidden, s32[16,4,16,1]{3,2,1,0:T(8,128)} %reshape.131.adapter, bf16[64,4096]{1,0:T(8,128)(2,1)} %tokens.3, f32[1,4096]{1,0:T(1,128)} %bitcast.36, bf16[256,1024]{1,0:T(8,128)(2,1)} %bitcast.32, ...), custom_call_target="tpu_custom_call" | custom-call | tf_op jit(solution)/shard_map/output_stage/pallas_call | solution.py:554
  238.9 1.9 copy.33
  (7 shorter events, 0.1 us)
Async XLA Ops:
  6.5 127.2 %all-gather.3.cloned.1.call-start = ((), (), s32[]{:S(2)}) async-start(), calls=%async_computation | async-start | bytes 9437184 | tf_op jit(solution)/shard_map/all_gather | solution.py:524
Sparse Core Ops, SparseCore 0:
  83.1 50.5 all-gather.2

commit v2 on v1

--- a/solution.py
+++ b/solution.py
@@ -1,4 +1,3 @@
-import functools
 import math
 
 import jax
@@ -21,6 +20,7 @@
 GROUP = 16
 UNIT = 16
 QKV = 3 * HEAD
+CUT = 6
 
 
 def dot(a, b):
@@ -50,7 +50,7 @@
     return sem
 
 
-def exchange_sum(me, packed, landed, full, sems):
+def exchange_sum(me, packed, landed, full, sems, meanwhile):
     def scatter(k, carry):
         to = (me + k) % GROUP
         pltpu.make_async_remote_copy(
@@ -60,6 +60,7 @@
 
     lax.fori_loop(1, GROUP, scatter, 0)
     landed[me] = packed[me]
+    meanwhile()
     many = landed.at[pl.ds(0, GROUP - 1)]
     pltpu.make_async_copy(many, many, sems.at[1]).wait()
     full[me] = jnp.sum(landed[...].astype(F32), axis=0).astype(BF16)
@@ -89,15 +90,22 @@
 )
 
 
-def input_kernel(
-    tokens, gain, bias, in_bias, adapter, slots, cosine, sine, w_qkv, w_up, w_left, w_qkv_right, w_up_right,
-    out_qkv, out_hidden,
+def front_kernel(
+    tokens, gain, bias, in_bias, lengths, request_adapter, slots, frequency, w_qkv, w_up, w_left, w_qkv_right, w_up_right,
+    out_attended, out_hidden, adapter,
     xs, weights, right_qkv, right_up, rows_in, acc, picked, packed, landed, full,
-    load_sems, send_sem, recv_sems, ex_sems,
+    starts, cosine, sine, queries, window, passing, top, total, summed,
+    load_sems, send_sem, recv_sems, ex_sems, near_send, near_recv,
 ):
     plane = Plane()
     me = plane.me
+    req = lax.axis_index("req")
+    chip, core = req // 2, req % 2
+    ahead = ((chip + 1) % SIDE) * 2 + core
+    behind = ((chip + 3) % SIDE) * 2 + core
+    other = chip * 2 + 1 - core
     hid = w_up.shape[1]
+    count = GROUP * 64
     loads = [
         pltpu.make_async_copy(w_qkv, weights.at[:, pl.ds(0, QKV)], load_sems.at[0]),
         pltpu.make_async_copy(w_up, weights.at[:, pl.ds(QKV, hid)], load_sems.at[1]),
@@ -108,17 +116,19 @@
     for load in loads:
         load.start()
     sem = barrier_all(me, GROUP)
+    for device in (ahead, behind, other):
+        pl.semaphore_signal(sem, inc=1, device_id={"req": device}, device_id_type=MESH)
     for part in range(0, 64, 16):
         values = tokens[part : part + 16, :].astype(F32)
         center = values - jnp.mean(values, axis=1, keepdims=True)
         spread = jnp.mean(center * center, axis=1, keepdims=True)
         scaled = center * lax.rsqrt(spread + EPSILON)
         xs[me, part : part + 16, :] = (scaled * gain[...] + bias[...]).astype(BF16)
-    pl.semaphore_wait(sem, GROUP - 1)
+    pl.semaphore_wait(sem, GROUP + 2)
 
     def send(slot, half, units, axis, step):
-        first, count = units
-        rows = pl.ds(half * 32 + first * UNIT, count * UNIT)
+        first, many = units
+        rows = pl.ds(half * 32 + first * UNIT, many * UNIT)
         to = plane.off(half, step, 0) if axis == 1 else plane.off(half, 0, step)
         pltpu.make_async_remote_copy(
             xs.at[slot, rows, :], xs.at[slot, rows, :], send_sem, recv_sems.at[slot, half * 2 + first],
@@ -126,9 +136,9 @@
         ).start()
 
     def landed_piece(half, d1, d2, units):
-        first, count = units
+        first, many = units
         slot = plane.source(half, d1, d2)
-        rows = pl.ds(half * 32 + first * UNIT, count * UNIT)
+        rows = pl.ds(half * 32 + first * UNIT, many * UNIT)
         view = xs.at[slot, rows, :]
         pltpu.make_async_copy(view, view, recv_sems.at[slot, half * 2 + first]).wait()
         return slot
@@ -140,6 +150,28 @@
     for half in (0, 1):
         for step in (1, -1):
             send(me, half, whole, 2, step)
+
+    long = lengths[...].astype(F32)
+    requests = long.shape[1]
+    before = lax.broadcasted_iota(jnp.int32, (requests, requests), 0) < lax.broadcasted_iota(
+        jnp.int32, (requests, requests), 1
+    )
+    begins = dot(jnp.broadcast_to(long, (8, requests)).astype(BF16), before.astype(F32).astype(BF16))[:1, :]
+    ends = begins + long
+    ids = request_adapter[...].astype(F32)
+
+    def locate(block, carry):
+        rows = lax.broadcasted_iota(jnp.int32, (64, 1), 0)
+        index = (req * count + block * 64 + rows).astype(F32)
+        inside = jnp.logical_and(begins <= index, index < ends)
+        start = jnp.sum(jnp.where(inside, begins, 0.0), axis=1, keepdims=True)
+        mine = jnp.sum(jnp.where(inside, ids, 0.0), axis=1, keepdims=True)
+        starts[block] = start.reshape(4, UNIT, 1)
+        adapter[block] = mine.reshape(4, UNIT, 1)
+        return carry
+
+    lax.fori_loop(0, GROUP, locate, 0)
+
     for half in (0, 1):
         for d1 in (1, -1):
             slot = landed_piece(half, d1, 0, whole)
@@ -152,21 +184,29 @@
             slot = landed_piece(half, d1, d2, units)
         send(slot, half, (0, 1) if d2 == 1 else (1, 1), 2, d2)
 
+    lane = lax.broadcasted_iota(jnp.int32, (1, 128), 1)
+    even = lane % 2 == 0
+
+    def angles(block, carry):
+        rows = lax.broadcasted_iota(jnp.int32, (64, 1), 0)
+        index = (req * count + block * 64 + rows).astype(F32)
+        angle = (index - starts[block].reshape(64, 1)) * frequency[...]
+        turned = lane < ROT
+        cosine[block] = jnp.where(turned, jnp.cos(angle), 1.0).reshape(4, UNIT, 128)
+        sine[block] = jnp.where(turned, jnp.where(even, -1.0, 1.0) * jnp.sin(angle), 0.0).reshape(4, UNIT, 128)
+        return carry
+
     def multiply(number):
-        places = []
+        for i, (half, d1, d2) in enumerate(GATHER_GROUPS[number]):
+            rows_in[i * 32 : (i + 1) * 32, :] = xs[plane.source(half, d1, d2), pl.ds(half * 32, 32), :]
+        left = dot(rows_in[...], weights[:, QKV + hid :])
         for i, (half, d1, d2) in enumerate(GATHER_GROUPS[number]):
             slot = plane.source(half, d1, d2)
-            rows_in[i * 32 : (i + 1) * 32, :] = xs[slot, pl.ds(half * 32, 32), :]
-            places.append((slot, half))
-
-        left = dot(rows_in[...], weights[:, QKV + hid :])
-        for i, (slot, half) in enumerate(places):
             for u in (0, 1):
-                unit = half * 2 + u
                 at = i * 32 + u * UNIT
-                picked[slot, unit] = left[at : at + UNIT, :].astype(BF16)
-
-    def multiply_wide(number):
+                picked[slot, half * 2 + u] = left[at : at + UNIT, :].astype(BF16)
+
+    def multiply_wide(number, begin, end):
         def column(n, carry):
             columns = pl.ds(pl.multiple_of(n * 256, 256), 256)
             result = dot(rows_in[...], weights[:, columns])
@@ -177,10 +217,10 @@
                     acc[slot, half * 2 + u, :, columns] = result[at : at + UNIT, :]
             return carry
 
-        lax.fori_loop(0, (QKV + hid) // 256, column, 0)
-
-    for load in loads[:3]:
-        load.wait()
+        lax.fori_loop(begin, end, column, 0)
+
+    tiles = (QKV + hid) // 256
+    lax.fori_loop(0, GROUP // 2, angles, 0)
     for half in (0, 1):
         for d2 in (1, -1):
             relay(half, 0, d2, (whole,))
@@ -189,27 +229,30 @@
             slot = landed_piece(half, 2, 0, unit)
             for step in (1, -1):
                 send(slot, half, unit, 2, step)
+    for load in loads[:3]:
+        load.wait()
     multiply(0)
-    multiply_wide(0)
+    multiply_wide(0, 0, tiles)
     for half in (0, 1):
         for d1 in (1, -1):
             for d2 in (1, -1):
                 relay(half, d1, d2, (whole,))
     multiply(1)
-    multiply_wide(1)
+    multiply_wide(1, 0, tiles)
+    lax.fori_loop(GROUP // 2, GROUP, angles, 0)
     for half in (0, 1):
         for d2 in (1, -1):
             relay(half, 2, d2, ((0, 1), (1, 1)))
     multiply(2)
-    multiply_wide(2)
+    multiply_wide(2, 0, tiles)
     for half in (0, 1):
         for d1 in (0, 1, -1, 2):
             for unit in ((0, 1), (1, 1)):
                 landed_piece(half, d1, 2, unit)
     multiply(3)
 
-    lane = lax.broadcasted_iota(jnp.int32, (1, 128), 1)
     chosen = jnp.where(lane < 32, slots[0], jnp.where(lane < 64, slots[1], jnp.where(lane < 96, slots[2], slots[3])))
+    chosen = chosen.astype(F32)
     row_id = lax.broadcasted_iota(jnp.int32, (128, 128), 0)
     col_id = lax.broadcasted_iota(jnp.int32, (128, 128), 1)
     together = jnp.zeros((256, 128), F32)
@@ -219,28 +262,24 @@
         fold = jnp.logical_and(col_id // 32 == unit, row_id % 32 == col_id % 32).astype(F32).astype(BF16)
         together = together + dot(kept, fold)
     packed[...] = together.astype(BF16).reshape(GROUP, UNIT, 128)
-    many = exchange_sum(me, packed, landed, full, ex_sems)
-    multiply_wide(3)
+    many = exchange_sum(me, packed, landed, full, ex_sems, lambda: multiply_wide(3, 0, 2))
+    multiply_wide(3, 2, tiles)
     exchange_wait(many, ex_sems)
-    sent = xs.at[pl.ds(0, GROUP - 1)]
-    pltpu.make_async_copy(sent, sent, send_sem).wait()
     for load in loads[3:]:
         load.wait()
 
-    lane = lax.broadcasted_iota(jnp.int32, (1, 1024), 1)
+    wide_lane = lax.broadcasted_iota(jnp.int32, (1, 1024), 1)
+    owner = (wide_lane // RANK).astype(F32)
     row_id = lax.broadcasted_iota(jnp.int32, (128, 1024), 0)
     col_id = lax.broadcasted_iota(jnp.int32, (128, 1024), 1)
-    even = lax.broadcasted_iota(jnp.int32, (1, 128), 1) % 2 == 0
-
-    def finish(unit, carry):
-        ranks = full[...].reshape(256, 128)
-        mine = adapter[:, unit].reshape(256, 1) == lane // RANK
-
-        def widened(first):
-            spread = (row_id == unit * 32 + first + col_id % RANK).astype(F32).astype(BF16)
-            return jnp.where(mine, dot(ranks, spread), 0.0).astype(BF16)
-
-        wide = widened(0)
+
+    def widened(unit, first):
+        spread = (row_id == unit * 32 + first + col_id % RANK).astype(F32).astype(BF16)
+        mine = adapter[:, unit].reshape(256, 1) == owner
+        return jnp.where(mine, dot(full[...].reshape(256, 128), spread), 0.0).astype(BF16)
+
+    def finish_heads(unit, carry):
+        wide = widened(unit, 0)
         turn = cosine[:, unit].reshape(256, 128)
         sway = sine[:, unit].reshape(256, 128)
         for part in range(3):
@@ -250,8 +289,15 @@
                 head = value[:, :128]
                 swapped = jnp.where(even, pltpu.roll(head, 127, 1), pltpu.roll(head, 1, 1))
                 value = jnp.concatenate([head * turn + swapped * sway, value[:, 128:]], axis=1)
-            out_qkv[:, unit, :, columns] = value.astype(BF16).reshape(GROUP, UNIT, HEAD)
-        wide = widened(RANK)
+            value = value.astype(BF16)
+            if part == 0:
+                queries[:, unit] = (value * jnp.asarray(HEAD ** (-0.5), BF16)).reshape(GROUP, UNIT, HEAD)
+            else:
+                window[0, :, unit, :, (part - 1) * HEAD : part * HEAD] = value.reshape(GROUP, UNIT, HEAD)
+        return carry
+
+    def finish_hidden(unit, carry):
+        wide = widened(unit, RANK)
         for part in range(hid // 256):
             columns = slice(part * 256, (part + 1) * 256)
             value = acc[:, unit, :, QKV + part * 256 : QKV + (part + 1) * 256].reshape(256, 256)
@@ -260,43 +306,107 @@
             out_hidden[:, unit, :, columns] = value.astype(BF16).reshape(GROUP, UNIT, 256)
         return carry
 
-    lax.fori_loop(0, 4, finish, 0)
-
-
-def attend_kernel(first_chunk, queries, keys_values, starts, out, top, total, summed, *, chunk):
-    block = queries.shape[0]
-    number = pl.program_id(0)
-    req = lax.axis_index("req")
-    rows = keys_values.shape[1]
-    first_row = req * rows + number * block
-    per = rows // chunk
-    top[...] = jnp.full_like(top, NEGATIVE_FILL)
-    total[...] = jnp.zeros_like(total)
-    summed[...] = jnp.zeros_like(summed)
-    scaled = queries[...] * jnp.asarray(HEAD ** (-0.5), BF16)
-    row_id = first_row + lax.broadcasted_iota(jnp.int32, (block, 1), 0)
-    begin = starts[...]
-    lane = lax.broadcasted_iota(jnp.int32, (1, chunk), 1)
-
-    def step(c, carry):
-        slot = req - c // per
-        at = pl.ds(pl.multiple_of((c % per) * chunk, chunk), chunk)
-        keys = keys_values[slot, at, :HEAD]
-        values = keys_values[slot, at, HEAD:]
-        scores = lax.dot_general(scaled, keys, (((1,), (1,)), ((), ())), preferred_element_type=F32)
-        key_id = c * chunk + lane
-        allowed = jnp.logical_and(key_id >= begin, key_id <= row_id)
-        masked = jnp.where(allowed, scores, NEGATIVE_FILL)
-        new_top = jnp.maximum(top[...], jnp.max(masked, axis=1, keepdims=True))
-        weights = jnp.where(allowed, jnp.exp(masked - new_top), 0.0)
-        decay = jnp.exp(top[...] - new_top)
-        total[...] = total[...] * decay + jnp.sum(weights, axis=1, keepdims=True)
-        summed[...] = summed[...] * decay + dot(weights.astype(BF16), values)
-        top[...] = new_top
-        return carry
-
-    lax.fori_loop(first_chunk[number], (first_row + block - 1) // chunk + 1, step, 0)
-    out[...] = (summed[...] / total[...]).astype(BF16)
+    lax.fori_loop(0, 4, finish_heads, 0)
+
+    low, high = pl.ds(0, CUT), pl.ds(CUT, GROUP - CUT)
+    started = []
+
+    def pass_on(src, dst, number, device):
+        copy = pltpu.make_async_remote_copy(
+            src, dst, near_send.at[number], near_recv.at[number], device_id={"req": device}, device_id_type=MESH
+        )
+        copy.start()
+        started.append(copy)
+
+    def take(ref, number):
+        pltpu.make_async_copy(ref, ref, near_recv.at[number]).wait()
+
+    pass_on(window.at[0, low], window.at[2, low], 0, ahead)
+    pass_on(window.at[0, high], passing, 2, behind)
+    pass_on(window.at[0, high], window.at[2, high], 1, ahead)
+    pass_on(window.at[0], window.at[1 + 4 * core], 3, other)
+
+    def attend(slot, m0, m1, b, causal):
+        keys = window[slot, m0:m1, :, :, :HEAD].reshape((m1 - m0) * 64, HEAD)
+        values = window[slot, m0:m1, :, :, HEAD:].reshape((m1 - m0) * 64, HEAD)
+        four = pl.ds(b * 4, 4)
+        scores = lax.dot_general(
+            queries[four].reshape(256, HEAD), keys, (((1,), (1,)), ((), ())), preferred_element_type=F32
+        )
+        key_id = lax.broadcasted_iota(jnp.int32, (1, (m1 - m0) * 64), 1) + (req - slot) * count + m0 * 64
+        allowed = key_id.astype(F32) >= starts[four].reshape(256, 1)
+        if causal:
+            row = lax.broadcasted_iota(jnp.int32, (256, 1), 0) + req * count + b * 256
+            allowed = jnp.logical_and(allowed, key_id <= row)
+        scores = jnp.where(allowed, scores, NEGATIVE_FILL)
+        peak = jnp.max(scores, axis=1, keepdims=True)
+        if causal:
+            kept = jnp.exp(scores - peak)
+            top[b] = peak
+            total[b] = jnp.sum(kept, axis=1, keepdims=True)
+            summed[b] = dot(kept.astype(BF16), values)
+        else:
+            old = top[b]
+            peak = jnp.maximum(old, peak)
+            kept = jnp.exp(scores - peak)
+            decay = jnp.exp(old - peak)
+            top[b] = peak
+            total[b] = total[b] * decay + jnp.sum(kept, axis=1, keepdims=True)
+            summed[b] = summed[b] * decay + dot(kept.astype(BF16), values)
+
+    def attend_all(slot, m0, m1):
+        def body(b, carry):
+            attend(slot, m0, m1, b, False)
+            return carry
+
+        lax.fori_loop(0, 4, body, 0)
+
+    for b in range(4):
+        attend(0, 0, (b + 1) * 4, b, True)
+    take(window.at[2, low], 0)
+    pass_on(window.at[2, low], window.at[4, low], 6, ahead)
+    pass_on(window.at[2, low], window.at[3 - 2 * core, low], 4, other)
+    take(window.at[5 - 4 * core], 3)
+
+    @pl.when(core == 1)
+    def _():
+        attend_all(1, 0, GROUP)
+
+    take(passing, 2)
+    pass_on(passing, window.at[4, high], 7, behind)
+    lax.fori_loop(0, 4, finish_hidden, 0)
+    attend_all(2, 0, CUT)
+    take(window.at[2, high], 1)
+    pass_on(window.at[2, high], window.at[3 - 2 * core, high], 5, other)
+    attend_all(2, CUT, GROUP)
+    take(window.at[1 + 2 * core, low], 4)
+    attend_all(1 + 2 * core, 0, CUT)
+    take(window.at[1 + 2 * core, high], 5)
+    attend_all(1 + 2 * core, CUT, GROUP)
+    take(window.at[4, high], 7)
+    pass_on(window.at[4, high], window.at[5 - 2 * core, high], 9, other)
+    attend_all(4, CUT, GROUP)
+    take(window.at[4, low], 6)
+    pass_on(window.at[4, low], window.at[5 - 2 * core, low], 8, other)
+    attend_all(4, 0, CUT)
+    take(window.at[3 + 2 * core, high], 9)
+
+    @pl.when(core == 0)
+    def _():
+        attend_all(3, CUT, GROUP)
+
+    take(window.at[3 + 2 * core, low], 8)
+
+    @pl.when(core == 0)
+    def _():
+        attend_all(3, 0, CUT)
+
+    for b in range(4):
+        out_attended[b * 4 : (b + 1) * 4] = (summed[b] / total[b]).astype(BF16).reshape(4, 4, UNIT, HEAD)
+    for copy in started:
+        copy.wait_send()
+    sent = xs.at[pl.ds(0, GROUP - 1)]
+    pltpu.make_async_copy(sent, sent, send_sem).wait()
 
 
 REDUCE_GROUPS = (
@@ -338,7 +448,7 @@
     fold_col = lax.broadcasted_iota(jnp.int32, (1024, 128), 1)
 
     def lower(unit, together):
-        mine = adapter[:, unit].reshape(256, 1) == lane // RANK
+        mine = adapter[:, unit].reshape(256, 1) == (lane // RANK).astype(F32)
         for first, begin, end in ((0, 0, HEAD), (RANK, HEAD, depth)):
             product = dot(inputs[:, unit, :, begin:end].reshape(256, end - begin), left[begin:end, :])
             kept = jnp.where(mine, product, 0.0).astype(BF16)
@@ -349,7 +459,7 @@
     together = lax.fori_loop(0, 4, lower, jnp.zeros((256, 128), F32))
     packed[...] = together.astype(BF16).reshape(GROUP, UNIT, 128)
     pl.semaphore_wait(sem, GROUP - 1)
-    many = exchange_sum(me, packed, landed, full, ex_sems)
+    many = exchange_sum(me, packed, landed, full, ex_sems, lambda: None)
     for load in loads[4:]:
         load.wait()
     exchange_wait(many, ex_sems)
@@ -357,7 +467,7 @@
     row_id = lax.broadcasted_iota(jnp.int32, (128, 128), 0)
     col_id = lax.broadcasted_iota(jnp.int32, (128, 128), 1)
     for unit in range(4):
-        mine = adapter[:, unit].reshape(256, 1) == me * 4 + lane // 32
+        mine = adapter[:, unit].reshape(256, 1) == (me * 4 + lane // 32).astype(F32)
         spread = (row_id == unit * 32 + col_id % 32).astype(F32).astype(BF16)
         wide = jnp.where(mine, dot(full[...].reshape(256, 128), spread), 0.0).astype(BF16)
         inputs[:, unit, :, depth:] = wide.reshape(GROUP, UNIT, 128)
@@ -462,37 +572,23 @@
     output_adapter_right, lengths, request_adapter, slot_adapter,
 ):
     rows, width = tokens.shape
-    group_rows = rows * GROUP
-    req = lax.axis_index("req")
     hid = up_weight.shape[1]
-
-    ends = jnp.cumsum(lengths)
-    begins = ends - lengths
-    index = req * group_rows + lax.iota(jnp.int32, group_rows)
-    inside = jnp.logical_and(begins[None, :] <= index[:, None], index[:, None] < ends[None, :])
-    start = jnp.sum(jnp.where(inside, begins[None, :], 0), axis=1)
-    adapter = jnp.sum(jnp.where(inside, request_adapter[None, :], 0), axis=1)
     lane = lax.iota(jnp.int32, 128)
     frequency = jnp.exp((lane // 2).astype(F32) * (-2.0 * math.log(10000.0) / ROT))
-    angle = (index - start).astype(F32)[:, None] * frequency[None, :]
-    turned = (lane < ROT)[None, :]
-    cosine = jnp.where(turned, jnp.cos(angle), 1.0)
-    sine = jnp.where(turned, jnp.where(lane % 2 == 0, -1.0, 1.0)[None, :] * jnp.sin(angle), 0.0)
-
     vmem = pl.BlockSpec(memory_space=pltpu.VMEM)
     smem = pl.BlockSpec(memory_space=pltpu.SMEM)
     anywhere = pl.BlockSpec(memory_space=pl.ANY)
     dma = pltpu.SemaphoreType.DMA
     by_unit = (GROUP, 4, UNIT)
-    adapter_units = adapter.reshape(by_unit + (1,))
-    qkv, hidden = pl.pallas_call(
-        input_kernel,
+    attended, hidden, adapter = pl.pallas_call(
+        front_kernel,
         out_shape=(
-            jax.ShapeDtypeStruct(by_unit + (QKV,), BF16),
+            jax.ShapeDtypeStruct(by_unit + (HEAD,), BF16),
             jax.ShapeDtypeStruct(by_unit + (hid,), BF16),
+            jax.ShapeDtypeStruct(by_unit + (1,), F32),
         ),
-        in_specs=[vmem] * 5 + [smem] + [vmem] * 2 + [anywhere] * 5,
-        out_specs=(vmem, vmem),
+        in_specs=[vmem] * 6 + [smem] + [vmem] + [anywhere] * 5,
+        out_specs=(vmem, vmem, vmem),
         scratch_shapes=[
             pltpu.VMEM((GROUP, rows, width), BF16),
             pltpu.VMEM((width, QKV + hid + 128), BF16),
@@ -504,51 +600,32 @@
             pltpu.VMEM((GROUP, UNIT, 128), BF16),
             pltpu.VMEM((GROUP, UNIT, 128), BF16),
             pltpu.VMEM((GROUP, UNIT, 128), BF16),
+            pltpu.VMEM(by_unit + (1,), F32),
+            pltpu.VMEM(by_unit + (128,), F32),
+            pltpu.VMEM(by_unit + (128,), F32),
+            pltpu.VMEM(by_unit + (HEAD,), BF16),
+            pltpu.VMEM((6,) + by_unit + (2 * HEAD,), BF16),
+            pltpu.VMEM((GROUP - CUT, 4, UNIT, 2 * HEAD), BF16),
+            pltpu.VMEM((4, 256, 1), F32),
+            pltpu.VMEM((4, 256, 1), F32),
+            pltpu.VMEM((4, 256, HEAD), F32),
             dma((5,)),
             dma,
             dma((GROUP, 4)),
             dma((4,)),
+            dma((10,)),
+            dma((10,)),
         ],
         compiler_params=pltpu.CompilerParams(
             collective_id=0, has_side_effects=True, vmem_limit_bytes=VMEM_LIMIT
         ),
-        name="input_stage",
+        name="front_stage",
     )(
-        tokens, layer_norm_gain[None, :], layer_norm_bias[None, :], input_bias[None, :], adapter_units, slot_adapter,
-        cosine.reshape(by_unit + (128,)), sine.reshape(by_unit + (128,)),
+        tokens, layer_norm_gain[None, :], layer_norm_bias[None, :], input_bias[None, :], lengths[None, :],
+        request_adapter[None, :], slot_adapter, frequency[None, :],
         query_key_weight.reshape(width, QKV), up_weight, input_adapter_left,
         query_key_value_right.reshape(-1, QKV), up_adapter_right,
     )
-    qkv = qkv.reshape(group_rows, QKV)
-
-    gathered = lax.all_gather(qkv[:, HEAD:], "req", axis=0)
-    slots = jnp.maximum(req - lax.iota(jnp.int32, 5), 0)
-    window = jnp.stack([lax.dynamic_index_in_dim(gathered, slots[i], 0, keepdims=False) for i in range(5)])
-
-    block, chunk = 256, 512
-    blocks = group_rows // block
-    first_chunk = start.reshape(blocks, block)[:, 0] // chunk
-    attended = pl.pallas_call(
-        functools.partial(attend_kernel, chunk=chunk),
-        out_shape=jax.ShapeDtypeStruct((group_rows, HEAD), BF16),
-        grid_spec=pltpu.PrefetchScalarGridSpec(
-            num_scalar_prefetch=1,
-            grid=(blocks,),
-            in_specs=[
-                pl.BlockSpec((block, HEAD), lambda i, s: (i, 0)),
-                pl.BlockSpec((5, group_rows, 2 * HEAD), lambda i, s: (0, 0, 0), pipeline_mode=pl.Buffered(1)),
-                pl.BlockSpec((block, 1), lambda i, s: (i, 0)),
-            ],
-            out_specs=pl.BlockSpec((block, HEAD), lambda i, s: (i, 0)),
-            scratch_shapes=[
-                pltpu.VMEM((block, 1), F32),
-                pltpu.VMEM((block, 1), F32),
-                pltpu.VMEM((block, HEAD), F32),
-            ],
-        ),
-        compiler_params=pltpu.CompilerParams(vmem_limit_bytes=VMEM_LIMIT),
-        name="attend_stage",
-    )(first_chunk, qkv[:, :HEAD], window, start[:, None])
 
     depth = HEAD + hid + 128
     return pl.pallas_call(
@@ -578,7 +655,7 @@
         ),
         name="output_stage",
     )(
-        attended.reshape(by_unit + (HEAD,)), hidden, adapter_units, tokens, output_bias[None, :],
+        attended, hidden, adapter, tokens, output_bias[None, :],
         output_adapter_left.reshape(HEAD, -1), down_adapter_left, output_weight.reshape(HEAD, width), down_weight,
         output_adapter_right,
     )

time: 248 us -> 185 us (0.75)
  the two profiles are of different devices: /device:TPU:3 before, /device:TPU:0 now
where the time goes in v2:
time: 185 us
  Pallas kernels  180 us (97%)
  local copies, waits for them, and re-layouts  4.37 us (2%)
    pallas_call x1, Pallas kernels, per_device(): pl.pallas_call(front_kernel, out_shape=(jax.ShapeDtypeStruct(by_unit + (H...  117 us
    pallas_call x1, Pallas kernels, per_device(): pl.pallas_call(output_kernel, out_shape=jax.ShapeDtypeStruct((rows, width...  62.3 us

profile of v2, /device:TPU:0, one launch (start us, length us, event | category | flops | bytes accessed | tf_op | source)
XLA Modules:
  0.0 184.7 jit_solution(17275799960944646498)
XLA Ops:
  0.0 0.5 fusion.2.frequency
  0.5 1.2 broadcast_in_dim.22.lengths
  1.8 1.3 broadcast_in_dim.23.request_adapter
  3.0 117.5 %front_stage.1 = (bf16[16,4,16,256]{3,2,1,0:T(8,128)(2,1)}, bf16[16,4,16,512]{3,2,1,0:T(8,128)(2,1)}, f32[16,4,16,1]{3,2,1,0:T(8,128)}) custom-call(bf16[64,4096]{1,0:T(8,128)(2,1)} %tokens.3, f32[1,4096]{1,0:T(1,128)} %bitcast.13, f32[1,4096]{1,0:T(1,128)} %bitcast.14, f32[1,512]{1,0:T(1,128)} %bitcast.15, s32[1,257]{1,0:T(1,128)} %broadcast_in_dim.22.lengths, ...), custom_call_target="tpu_custom_call" | custom-call | tf_op jit(solution)/shard_map/front_stage/pallas_call | solution.py:583
  120.5 62.3 %output_stage.1 = bf16[64,4096]{1,0:T(8,128)(2,1)} custom-call(bf16[16,4,16,256]{3,2,1,0:T(8,128)(2,1)} %get-tuple-element.8.attended, bf16[16,4,16,512]{3,2,1,0:T(8,128)(2,1)} %get-tuple-element.9.hidden, f32[16,4,16,1]{3,2,1,0:T(8,128)} %get-tuple-element.10.adapter, bf16[64,4096]{1,0:T(8,128)(2,1)} %tokens.3, f32[1,4096]{1,0:T(1,128)} %bitcast.12, ...), custom_call_target="tpu_custom_call" | custom-call | tf_op jit(solution)/shard_map/output_stage/pallas_call | solution.py:631
  182.8 1.9 %copy.20 = bf16[64,4096]{1,0:T(8,128)(2,1)} copy(bf16[64,4096]{1,0:T(8,128)(2,1)} %output_stage.1) | data formatting | bytes 1048576

commit v3 on v2

--- a/solution.py
+++ b/solution.py
@@ -21,6 +21,7 @@
 UNIT = 16
 QKV = 3 * HEAD
 CUT = 6
+PLACES = (0, 3, 1, 2)
 
 
 def dot(a, b):
@@ -50,7 +51,7 @@
     return sem
 
 
-def exchange_sum(me, packed, landed, full, sems, meanwhile):
+def exchange_start(me, packed, landed, sems):
     def scatter(k, carry):
         to = (me + k) % GROUP
         pltpu.make_async_remote_copy(
@@ -60,7 +61,9 @@
 
     lax.fori_loop(1, GROUP, scatter, 0)
     landed[me] = packed[me]
-    meanwhile()
+
+
+def exchange_middle(me, landed, full, sems):
     many = landed.at[pl.ds(0, GROUP - 1)]
     pltpu.make_async_copy(many, many, sems.at[1]).wait()
     full[me] = jnp.sum(landed[...].astype(F32), axis=0).astype(BF16)
@@ -73,25 +76,24 @@
         return carry
 
     lax.fori_loop(1, GROUP, gather, 0)
-    pltpu.make_async_copy(many, many, sems.at[0]).wait()
-    return many
-
-
-def exchange_wait(many, sems):
-    pltpu.make_async_copy(many, many, sems.at[3]).wait()
-    pltpu.make_async_copy(many, many, sems.at[2]).wait()
-
-
-GATHER_GROUPS = (
-    tuple((h, d1, 0) for h in (0, 1) for d1 in (0, 1, -1, 2)),
-    tuple((h, d1, d2) for h in (0, 1) for d1 in (0, 1) for d2 in (1, -1)),
-    tuple((h, d1, d2) for h in (0, 1) for d1 in (-1, 2) for d2 in (1, -1)),
-    tuple((h, d1, 2) for h in (0, 1) for d1 in (0, 1, -1, 2)),
+
+
+def exchange_end(landed, sems):
+    many = landed.at[pl.ds(0, GROUP - 1)]
+    for number in (3, 0, 2):
+        pltpu.make_async_copy(many, many, sems.at[number]).wait()
+
+
+EARLY = tuple((h, d1, 0) for h in (0, 1) for d1 in (0, 1, -1, 2)) + tuple(
+    (h, d1, d2) for h in (0, 1) for d1 in (0, 1) for d2 in (1, -1)
 )
+LATE = tuple((h, d1, d2) for h in (0, 1) for d1 in (-1, 2) for d2 in (1, -1)) + tuple(
+    (h, d1, 2) for h in (0, 1) for d1 in (0, 1, -1, 2)
+)
 
 
 def front_kernel(
-    tokens, gain, bias, in_bias, lengths, request_adapter, slots, frequency, w_qkv, w_up, w_left, w_qkv_right, w_up_right,
+    tokens, gain, bias, in_bias, table, slots, w_qkv, w_up, w_left, w_qkv_right, w_up_right,
     out_attended, out_hidden, adapter,
     xs, weights, right_qkv, right_up, rows_in, acc, picked, packed, landed, full,
     starts, cosine, sine, queries, window, passing, top, total, summed,
@@ -126,39 +128,81 @@
         xs[me, part : part + 16, :] = (scaled * gain[...] + bias[...]).astype(BF16)
     pl.semaphore_wait(sem, GROUP + 2)
 
-    def send(slot, half, units, axis, step):
-        first, many = units
-        rows = pl.ds(half * 32 + first * UNIT, many * UNIT)
+    def unit_of(half, chunk):
+        return chunk if half == 0 else 1 - chunk
+
+    def far_way(half, chunk):
+        return 1 if unit_of(half, chunk) == 0 else -1
+
+    def rows_of(half, chunk):
+        return pl.ds(half * 32 + unit_of(half, chunk) * UNIT, UNIT)
+
+    def send(slot, half, chunk, axis, step):
+        view = xs.at[slot, rows_of(half, chunk), :]
         to = plane.off(half, step, 0) if axis == 1 else plane.off(half, 0, step)
         pltpu.make_async_remote_copy(
-            xs.at[slot, rows, :], xs.at[slot, rows, :], send_sem, recv_sems.at[slot, half * 2 + first],
+            view, view, send_sem, recv_sems.at[slot, half * 2 + unit_of(half, chunk)],
             device_id={"mlp": to}, device_id_type=MESH,
         ).start()
 
-    def landed_piece(half, d1, d2, units):
-        first, many = units
+    def arrive(half, chunk, d1, d2):
         slot = plane.source(half, d1, d2)
-        rows = pl.ds(half * 32 + first * UNIT, many * UNIT)
-        view = xs.at[slot, rows, :]
-        pltpu.make_async_copy(view, view, recv_sems.at[slot, half * 2 + first]).wait()
+        view = xs.at[slot, rows_of(half, chunk), :]
+        pltpu.make_async_copy(view, view, recv_sems.at[slot, half * 2 + unit_of(half, chunk)]).wait()
         return slot
 
-    whole = (0, 2)
-    for half in (0, 1):
-        for step in (1, -1):
-            send(me, half, whole, 1, step)
-    for half in (0, 1):
-        for step in (1, -1):
-            send(me, half, whole, 2, step)
-
-    long = lengths[...].astype(F32)
+    def own_sends(chunk, ways):
+        for axis in (1, 2):
+            for half in (0, 1):
+                along_z = (half == 0) == (axis == 1)
+                for step in (1, -1):
+                    if (along_z, step) in ways:
+                        send(me, half, chunk, axis, step)
+
+    def first_hop(chunk):
+        for d1 in (1, -1):
+            for half in (0, 1):
+                slot = arrive(half, chunk, d1, 0)
+                for step in (1, -1):
+                    send(slot, half, chunk, 2, step)
+                if d1 == far_way(half, chunk):
+                    send(slot, half, chunk, 1, d1)
+
+    def relay(chunk, d1):
+        for half in (0, 1):
+            way = far_way(half, chunk)
+            send(arrive(half, chunk, d1, way), half, chunk, 2, way)
+
+    def far(chunk):
+        for half in (0, 1):
+            slot = arrive(half, chunk, 2, 0)
+            for step in (1, -1):
+                send(slot, half, chunk, 2, step)
+
+    def rest_early(chunk):
+        for d1 in (0, 1):
+            for half in (0, 1):
+                arrive(half, chunk, d1, -far_way(half, chunk))
+
+    def rest_late(chunk):
+        for d1 in (-1, 2):
+            for half in (0, 1):
+                arrive(half, chunk, d1, -far_way(half, chunk))
+        for d1 in (0, 1, -1, 2):
+            for half in (0, 1):
+                arrive(half, chunk, d1, 2)
+
+    light, heavy = ((True, 1), (False, -1)), ((True, -1), (False, 1))
+    own_sends(0, light + heavy)
+
+    long = table[0:1, :].astype(F32)
     requests = long.shape[1]
     before = lax.broadcasted_iota(jnp.int32, (requests, requests), 0) < lax.broadcasted_iota(
         jnp.int32, (requests, requests), 1
     )
     begins = dot(jnp.broadcast_to(long, (8, requests)).astype(BF16), before.astype(F32).astype(BF16))[:1, :]
     ends = begins + long
-    ids = request_adapter[...].astype(F32)
+    ids = table[1:2, :].astype(F32)
 
     def locate(block, carry):
         rows = lax.broadcasted_iota(jnp.int32, (64, 1), 0)
@@ -172,114 +216,78 @@
 
     lax.fori_loop(0, GROUP, locate, 0)
 
-    for half in (0, 1):
-        for d1 in (1, -1):
-            slot = landed_piece(half, d1, 0, whole)
-            send(slot, half, (0, 1) if d1 == 1 else (1, 1), 1, d1)
-            for step in (1, -1):
-                send(slot, half, whole, 2, step)
-
-    def relay(half, d1, d2, pieces):
-        for units in pieces:
-            slot = landed_piece(half, d1, d2, units)
-        send(slot, half, (0, 1) if d2 == 1 else (1, 1), 2, d2)
+    first_hop(0)
+    relay(0, 0)
+    far(0)
+    own_sends(1, light)
+    relay(0, 1)
+    relay(0, -1)
+    own_sends(1, heavy)
 
     lane = lax.broadcasted_iota(jnp.int32, (1, 128), 1)
     even = lane % 2 == 0
+    frequency = jnp.exp((lane // 2).astype(F32) * (-2.0 * math.log(10000.0) / ROT))
 
     def angles(block, carry):
         rows = lax.broadcasted_iota(jnp.int32, (64, 1), 0)
         index = (req * count + block * 64 + rows).astype(F32)
-        angle = (index - starts[block].reshape(64, 1)) * frequency[...]
+        angle = (index - starts[block].reshape(64, 1)) * frequency
         turned = lane < ROT
         cosine[block] = jnp.where(turned, jnp.cos(angle), 1.0).reshape(4, UNIT, 128)
         sine[block] = jnp.where(turned, jnp.where(even, -1.0, 1.0) * jnp.sin(angle), 0.0).reshape(4, UNIT, 128)
         return carry
 
-    def multiply(number):
-        for i, (half, d1, d2) in enumerate(GATHER_GROUPS[number]):
-            rows_in[i * 32 : (i + 1) * 32, :] = xs[plane.source(half, d1, d2), pl.ds(half * 32, 32), :]
+    def multiply(chunk, pieces):
+        for i, (half, d1, d2) in enumerate(pieces):
+            slot = plane.source(half, d1, d2)
+            rows_in[i * UNIT : (i + 1) * UNIT, :] = xs[slot, rows_of(half, chunk), :]
         left = dot(rows_in[...], weights[:, QKV + hid :])
-        for i, (half, d1, d2) in enumerate(GATHER_GROUPS[number]):
-            slot = plane.source(half, d1, d2)
-            for u in (0, 1):
-                at = i * 32 + u * UNIT
-                picked[slot, half * 2 + u] = left[at : at + UNIT, :].astype(BF16)
-
-    def multiply_wide(number, begin, end):
+        for i, (half, d1, d2) in enumerate(pieces):
+            unit = half * 2 + unit_of(half, chunk)
+            picked[plane.source(half, d1, d2), unit] = left[i * UNIT : (i + 1) * UNIT, :].astype(BF16)
+
+    def multiply_wide(chunk, pieces, begin, end):
         def column(n, carry):
             columns = pl.ds(pl.multiple_of(n * 256, 256), 256)
             result = dot(rows_in[...], weights[:, columns])
-            for i, (half, d1, d2) in enumerate(GATHER_GROUPS[number]):
-                slot = plane.source(half, d1, d2)
-                for u in (0, 1):
-                    at = i * 32 + u * UNIT
-                    acc[slot, half * 2 + u, :, columns] = result[at : at + UNIT, :]
+            for i, (half, d1, d2) in enumerate(pieces):
+                unit = half * 2 + unit_of(half, chunk)
+                acc[plane.source(half, d1, d2), unit, :, columns] = result[i * UNIT : (i + 1) * UNIT, :]
             return carry
 
         lax.fori_loop(begin, end, column, 0)
-
-    tiles = (QKV + hid) // 256
-    lax.fori_loop(0, GROUP // 2, angles, 0)
-    for half in (0, 1):
-        for d2 in (1, -1):
-            relay(half, 0, d2, (whole,))
-    for half in (0, 1):
-        for unit in ((0, 1), (1, 1)):
-            slot = landed_piece(half, 2, 0, unit)
-            for step in (1, -1):
-                send(slot, half, unit, 2, step)
-    for load in loads[:3]:
-        load.wait()
-    multiply(0)
-    multiply_wide(0, 0, tiles)
-    for half in (0, 1):
-        for d1 in (1, -1):
-            for d2 in (1, -1):
-                relay(half, d1, d2, (whole,))
-    multiply(1)
-    multiply_wide(1, 0, tiles)
-    lax.fori_loop(GROUP // 2, GROUP, angles, 0)
-    for half in (0, 1):
-        for d2 in (1, -1):
-            relay(half, 2, d2, ((0, 1), (1, 1)))
-    multiply(2)
-    multiply_wide(2, 0, tiles)
-    for half in (0, 1):
-        for d1 in (0, 1, -1, 2):
-            for unit in ((0, 1), (1, 1)):
-                landed_piece(half, d1, 2, unit)
-    multiply(3)
 
     chosen = jnp.where(lane < 32, slots[0], jnp.where(lane < 64, slots[1], jnp.where(lane < 96, slots[2], slots[3])))
     chosen = chosen.astype(F32)
-    row_id = lax.broadcasted_iota(jnp.int32, (128, 128), 0)
-    col_id = lax.broadcasted_iota(jnp.int32, (128, 128), 1)
-    together = jnp.zeros((256, 128), F32)
-    for unit in range(4):
-        mine = adapter[:, unit].reshape(256, 1) == chosen
-        kept = jnp.where(mine, picked[:, unit].reshape(256, 128).astype(F32), 0.0).astype(BF16)
-        fold = jnp.logical_and(col_id // 32 == unit, row_id % 32 == col_id % 32).astype(F32).astype(BF16)
-        together = together + dot(kept, fold)
-    packed[...] = together.astype(BF16).reshape(GROUP, UNIT, 128)
-    many = exchange_sum(me, packed, landed, full, ex_sems, lambda: multiply_wide(3, 0, 2))
-    multiply_wide(3, 2, tiles)
-    exchange_wait(many, ex_sems)
-    for load in loads[3:]:
-        load.wait()
+
+    def pack(chunk):
+        row_id = lax.broadcasted_iota(jnp.int32, (128, 128), 0)
+        col_id = lax.broadcasted_iota(jnp.int32, (128, 128), 1)
+        together = jnp.zeros((256, 128), F32)
+        for unit in PLACES[chunk * 2 : chunk * 2 + 2]:
+            mine = adapter[:, unit].reshape(256, 1) == chosen
+            kept = jnp.where(mine, picked[:, unit].reshape(256, 128).astype(F32), 0.0).astype(BF16)
+            fold = jnp.logical_and(col_id // 32 == unit, row_id % 32 == col_id % 32).astype(F32).astype(BF16)
+            together = together + dot(kept, fold)
+        packed[chunk] = together.astype(BF16).reshape(GROUP, UNIT, 128)
+        exchange_start(me, packed.at[chunk], landed.at[chunk], ex_sems.at[chunk])
+
+    def middle(chunk):
+        exchange_middle(me, landed.at[chunk], full.at[chunk], ex_sems.at[chunk])
 
     wide_lane = lax.broadcasted_iota(jnp.int32, (1, 1024), 1)
     owner = (wide_lane // RANK).astype(F32)
     row_id = lax.broadcasted_iota(jnp.int32, (128, 1024), 0)
     col_id = lax.broadcasted_iota(jnp.int32, (128, 1024), 1)
 
-    def widened(unit, first):
+    def widened(chunk, unit, first):
         spread = (row_id == unit * 32 + first + col_id % RANK).astype(F32).astype(BF16)
         mine = adapter[:, unit].reshape(256, 1) == owner
-        return jnp.where(mine, dot(full[...].reshape(256, 128), spread), 0.0).astype(BF16)
-
-    def finish_heads(unit, carry):
-        wide = widened(unit, 0)
+        return jnp.where(mine, dot(full[chunk].reshape(256, 128), spread), 0.0).astype(BF16)
+
+    def finish_heads(place):
+        unit = PLACES[place]
+        wide = widened(place // 2, unit, 0)
         turn = cosine[:, unit].reshape(256, 128)
         sway = sine[:, unit].reshape(256, 128)
         for part in range(3):
@@ -293,20 +301,17 @@
             if part == 0:
                 queries[:, unit] = (value * jnp.asarray(HEAD ** (-0.5), BF16)).reshape(GROUP, UNIT, HEAD)
             else:
-                window[0, :, unit, :, (part - 1) * HEAD : part * HEAD] = value.reshape(GROUP, UNIT, HEAD)
-        return carry
-
-    def finish_hidden(unit, carry):
-        wide = widened(unit, RANK)
+                window[0, place, :, :, (part - 1) * HEAD : part * HEAD] = value.reshape(GROUP, UNIT, HEAD)
+
+    def finish_hidden(place):
+        unit = PLACES[place]
+        wide = widened(place // 2, unit, RANK)
         for part in range(hid // 256):
             columns = slice(part * 256, (part + 1) * 256)
             value = acc[:, unit, :, QKV + part * 256 : QKV + (part + 1) * 256].reshape(256, 256)
             value = value + dot(wide, right_up[:, columns]) + in_bias[:, columns]
             value = jax.nn.gelu(value, approximate=True)
             out_hidden[:, unit, :, columns] = value.astype(BF16).reshape(GROUP, UNIT, 256)
-        return carry
-
-    lax.fori_loop(0, 4, finish_heads, 0)
 
     low, high = pl.ds(0, CUT), pl.ds(CUT, GROUP - CUT)
     started = []
@@ -321,19 +326,56 @@
     def take(ref, number):
         pltpu.make_async_copy(ref, ref, near_recv.at[number]).wait()
 
-    pass_on(window.at[0, low], window.at[2, low], 0, ahead)
-    pass_on(window.at[0, high], passing, 2, behind)
-    pass_on(window.at[0, high], window.at[2, high], 1, ahead)
-    pass_on(window.at[0], window.at[1 + 4 * core], 3, other)
-
-    def attend(slot, m0, m1, b, causal):
-        keys = window[slot, m0:m1, :, :, :HEAD].reshape((m1 - m0) * 64, HEAD)
-        values = window[slot, m0:m1, :, :, HEAD:].reshape((m1 - m0) * 64, HEAD)
+    def part_of(slot, chunk, blocks=None):
+        if blocks is None:
+            return window.at[slot, pl.ds(2 * chunk, 2)]
+        return window.at[slot, pl.ds(2 * chunk, 2), blocks]
+
+    def near_sends(chunk):
+        at = 10 * chunk
+        pass_on(part_of(0, chunk, low), part_of(2, chunk, low), at, ahead)
+        pass_on(part_of(0, chunk, high), passing.at[chunk], at + 2, behind)
+        pass_on(part_of(0, chunk, high), part_of(2, chunk, high), at + 1, ahead)
+        pass_on(part_of(0, chunk), part_of(1 + 4 * core, chunk), at + 3, other)
+
+    def near_low(chunk):
+        at = 10 * chunk
+        take(part_of(2, chunk, low), at)
+        pass_on(part_of(2, chunk, low), part_of(4, chunk, low), at + 6, ahead)
+        pass_on(part_of(2, chunk, low), part_of(3 - 2 * core, chunk, low), at + 4, other)
+
+    def near_passing(chunk):
+        at = 10 * chunk
+        take(passing.at[chunk], at + 2)
+        pass_on(passing.at[chunk], part_of(4, chunk, high), at + 7, behind)
+
+    def near_high(chunk):
+        at = 10 * chunk
+        take(part_of(2, chunk, high), at + 1)
+        pass_on(part_of(2, chunk, high), part_of(3 - 2 * core, chunk, high), at + 5, other)
+
+    def next_high(chunk):
+        at = 10 * chunk
+        take(part_of(4, chunk, high), at + 7)
+        pass_on(part_of(4, chunk, high), part_of(5 - 2 * core, chunk, high), at + 9, other)
+
+    def next_low(chunk):
+        at = 10 * chunk
+        take(part_of(4, chunk, low), at + 6)
+        pass_on(part_of(4, chunk, low), part_of(5 - 2 * core, chunk, low), at + 8, other)
+
+    def attend(slot, p0, p1, blocks, b, causal):
+        many = (p1 - p0) * blocks * UNIT
+        keys = window[slot, p0:p1, :blocks, :, :HEAD].reshape(many, HEAD)
+        values = window[slot, p0:p1, :blocks, :, HEAD:].reshape(many, HEAD)
         four = pl.ds(b * 4, 4)
         scores = lax.dot_general(
             queries[four].reshape(256, HEAD), keys, (((1,), (1,)), ((), ())), preferred_element_type=F32
         )
-        key_id = lax.broadcasted_iota(jnp.int32, (1, (m1 - m0) * 64), 1) + (req - slot) * count + m0 * 64
+        index = lax.broadcasted_iota(jnp.int32, (1, many), 1)
+        place = index // (blocks * UNIT) + p0
+        unit = jnp.where(place == 0, 0, jnp.where(place == 1, 3, place - 1))
+        key_id = ((index // UNIT) % blocks) * 64 + unit * UNIT + index % UNIT + (req - slot) * count
         allowed = key_id.astype(F32) >= starts[four].reshape(256, 1)
         if causal:
             row = lax.broadcasted_iota(jnp.int32, (256, 1), 0) + req * count + b * 256
@@ -354,52 +396,92 @@
             total[b] = total[b] * decay + jnp.sum(kept, axis=1, keepdims=True)
             summed[b] = summed[b] * decay + dot(kept.astype(BF16), values)
 
-    def attend_all(slot, m0, m1):
+    def attend_all(slot, chunk):
         def body(b, carry):
-            attend(slot, m0, m1, b, False)
+            attend(slot, 2 * chunk, 2 * chunk + 2, GROUP, b, False)
             return carry
 
         lax.fori_loop(0, 4, body, 0)
 
+    def attend_on(which, slot, chunk):
+        @pl.when(core == which)
+        def _():
+            attend_all(slot, chunk)
+
+    tiles = (QKV + hid) // 256
+    lax.fori_loop(0, GROUP // 2, angles, 0)
+    for load in loads[:3]:
+        load.wait()
+    rest_early(0)
+    multiply(0, EARLY)
+    multiply_wide(0, EARLY, 0, tiles)
+    relay(0, 2)
+    first_hop(1)
+    lax.fori_loop(GROUP // 2, GROUP, angles, 0)
+    rest_late(0)
+    multiply(0, LATE)
+    pack(0)
+    relay(1, 0)
+    multiply_wide(0, LATE, 0, 2)
+    far(1)
+    middle(0)
+    multiply_wide(0, LATE, 2, tiles)
+    for load in loads[3:]:
+        load.wait()
+    relay(1, 1)
+    exchange_end(landed.at[0], ex_sems.at[0])
+    finish_heads(0)
+    finish_heads(1)
+    near_sends(0)
+    relay(1, -1)
+    rest_early(1)
+    multiply(1, EARLY)
+    multiply_wide(1, EARLY, 0, tiles)
+    relay(1, 2)
+    near_low(0)
+    near_passing(0)
+    rest_late(1)
+    multiply(1, LATE)
+    pack(1)
+    multiply_wide(1, LATE, 0, 2)
+    middle(1)
+    near_high(0)
+    multiply_wide(1, LATE, 2, tiles)
+    exchange_end(landed.at[1], ex_sems.at[1])
+    finish_heads(2)
+    finish_heads(3)
+    near_sends(1)
+    next_high(0)
     for b in range(4):
-        attend(0, 0, (b + 1) * 4, b, True)
-    take(window.at[2, low], 0)
-    pass_on(window.at[2, low], window.at[4, low], 6, ahead)
-    pass_on(window.at[2, low], window.at[3 - 2 * core, low], 4, other)
-    take(window.at[5 - 4 * core], 3)
-
-    @pl.when(core == 1)
-    def _():
-        attend_all(1, 0, GROUP)
-
-    take(passing, 2)
-    pass_on(passing, window.at[4, high], 7, behind)
-    lax.fori_loop(0, 4, finish_hidden, 0)
-    attend_all(2, 0, CUT)
-    take(window.at[2, high], 1)
-    pass_on(window.at[2, high], window.at[3 - 2 * core, high], 5, other)
-    attend_all(2, CUT, GROUP)
-    take(window.at[1 + 2 * core, low], 4)
-    attend_all(1 + 2 * core, 0, CUT)
-    take(window.at[1 + 2 * core, high], 5)
-    attend_all(1 + 2 * core, CUT, GROUP)
-    take(window.at[4, high], 7)
-    pass_on(window.at[4, high], window.at[5 - 2 * core, high], 9, other)
-    attend_all(4, CUT, GROUP)
-    take(window.at[4, low], 6)
-    pass_on(window.at[4, low], window.at[5 - 2 * core, low], 8, other)
-    attend_all(4, 0, CUT)
-    take(window.at[3 + 2 * core, high], 9)
-
-    @pl.when(core == 0)
-    def _():
-        attend_all(3, CUT, GROUP)
-
-    take(window.at[3 + 2 * core, low], 8)
-
-    @pl.when(core == 0)
-    def _():
-        attend_all(3, 0, CUT)
+        attend(0, 0, 4, (b + 1) * 4, b, True)
+    next_low(0)
+    take(part_of(5 - 4 * core, 0), 3)
+    attend_on(1, 1, 0)
+    attend_all(2, 0)
+    near_low(1)
+    take(part_of(1 + 2 * core, 0, low), 4)
+    take(part_of(1 + 2 * core, 0, high), 5)
+    attend_all(1 + 2 * core, 0)
+    near_passing(1)
+    attend_all(4, 0)
+    take(part_of(3 + 2 * core, 0, low), 8)
+    take(part_of(3 + 2 * core, 0, high), 9)
+    attend_on(0, 3, 0)
+    for place in range(4):
+        finish_hidden(place)
+    take(part_of(5 - 4 * core, 1), 13)
+    attend_on(1, 1, 1)
+    near_high(1)
+    attend_all(2, 1)
+    take(part_of(1 + 2 * core, 1, low), 14)
+    take(part_of(1 + 2 * core, 1, high), 15)
+    attend_all(1 + 2 * core, 1)
+    next_high(1)
+    next_low(1)
+    attend_all(4, 1)
+    take(part_of(3 + 2 * core, 1, high), 19)
+    take(part_of(3 + 2 * core, 1, low), 18)
+    attend_on(0, 3, 1)
 
     for b in range(4):
         out_attended[b * 4 : (b + 1) * 4] = (summed[b] / total[b]).astype(BF16).reshape(4, 4, UNIT, HEAD)
@@ -459,10 +541,11 @@
     together = lax.fori_loop(0, 4, lower, jnp.zeros((256, 128), F32))
     packed[...] = together.astype(BF16).reshape(GROUP, UNIT, 128)
     pl.semaphore_wait(sem, GROUP - 1)
-    many = exchange_sum(me, packed, landed, full, ex_sems, lambda: None)
+    exchange_start(me, packed, landed, ex_sems)
+    exchange_middle(me, landed, full, ex_sems)
     for load in loads[4:]:
         load.wait()
-    exchange_wait(many, ex_sems)
+    exchange_end(landed, ex_sems)
     lane = lax.broadcasted_iota(jnp.int32, (1, 128), 1)
     row_id = lax.broadcasted_iota(jnp.int32, (128, 128), 0)
     col_id = lax.broadcasted_iota(jnp.int32, (128, 128), 1)
@@ -573,8 +656,6 @@
 ):
     rows, width = tokens.shape
     hid = up_weight.shape[1]
-    lane = lax.iota(jnp.int32, 128)
-    frequency = jnp.exp((lane // 2).astype(F32) * (-2.0 * math.log(10000.0) / ROT))
     vmem = pl.BlockSpec(memory_space=pltpu.VMEM)
     smem = pl.BlockSpec(memory_space=pltpu.SMEM)
     anywhere = pl.BlockSpec(memory_space=pl.ANY)
@@ -587,7 +668,7 @@
             jax.ShapeDtypeStruct(by_unit + (hid,), BF16),
             jax.ShapeDtypeStruct(by_unit + (1,), F32),
         ),
-        in_specs=[vmem] * 6 + [smem] + [vmem] + [anywhere] * 5,
+        in_specs=[vmem] * 5 + [smem] + [anywhere] * 5,
         out_specs=(vmem, vmem, vmem),
         scratch_shapes=[
             pltpu.VMEM((GROUP, rows, width), BF16),
@@ -597,32 +678,32 @@
             pltpu.VMEM((256, width), BF16),
             pltpu.VMEM(by_unit + (QKV + hid,), F32),
             pltpu.VMEM(by_unit + (128,), BF16),
-            pltpu.VMEM((GROUP, UNIT, 128), BF16),
-            pltpu.VMEM((GROUP, UNIT, 128), BF16),
-            pltpu.VMEM((GROUP, UNIT, 128), BF16),
+            pltpu.VMEM((2, GROUP, UNIT, 128), BF16),
+            pltpu.VMEM((2, GROUP, UNIT, 128), BF16),
+            pltpu.VMEM((2, GROUP, UNIT, 128), BF16),
             pltpu.VMEM(by_unit + (1,), F32),
             pltpu.VMEM(by_unit + (128,), F32),
             pltpu.VMEM(by_unit + (128,), F32),
             pltpu.VMEM(by_unit + (HEAD,), BF16),
-            pltpu.VMEM((6,) + by_unit + (2 * HEAD,), BF16),
-            pltpu.VMEM((GROUP - CUT, 4, UNIT, 2 * HEAD), BF16),
+            pltpu.VMEM((6, 4, GROUP, UNIT, 2 * HEAD), BF16),
+            pltpu.VMEM((2, 2, GROUP - CUT, UNIT, 2 * HEAD), BF16),
             pltpu.VMEM((4, 256, 1), F32),
             pltpu.VMEM((4, 256, 1), F32),
             pltpu.VMEM((4, 256, HEAD), F32),
             dma((5,)),
             dma,
             dma((GROUP, 4)),
-            dma((4,)),
-            dma((10,)),
-            dma((10,)),
+            dma((2, 4)),
+            dma((20,)),
+            dma((20,)),
         ],
         compiler_params=pltpu.CompilerParams(
             collective_id=0, has_side_effects=True, vmem_limit_bytes=VMEM_LIMIT
         ),
         name="front_stage",
     )(
-        tokens, layer_norm_gain[None, :], layer_norm_bias[None, :], input_bias[None, :], lengths[None, :],
-        request_adapter[None, :], slot_adapter, frequency[None, :],
+        tokens, layer_norm_gain[None, :], layer_norm_bias[None, :], input_bias[None, :],
+        jnp.stack([lengths, request_adapter]), slot_adapter,
         query_key_weight.reshape(width, QKV), up_weight, input_adapter_left,
         query_key_value_right.reshape(-1, QKV), up_adapter_right,
     )

time: 185 us -> 182 us (0.984)
  Pallas kernels: 180 us -> 178 us
    pallas_call x1, Pallas kernels: 117 us -> 115 us  [per_device(): pl.pallas_call(front_kernel, out_shape=(jax.ShapeDtypeStruct(by_unit + (H...]
    broadcast_in_dim x2 -> x0, local copies, waits for them, and re-layouts: 2.5 us -> none  [the longest x1 1.26 us: per_device(): request_adapter[None, :]]
where the time goes in v3:
time: 182 us
  Pallas kernels  178 us (98%)
  local copies, waits for them, and re-layouts  3.23 us (2%)
    pallas_call x1, Pallas kernels, per_device(): pl.pallas_call(front_kernel, out_shape=(jax.ShapeDtypeStruct(by_unit + (H...  115 us
    pallas_call x1, Pallas kernels, per_device(): pl.pallas_call(output_kernel, out_shape=jax.ShapeDtypeStruct((rows, width...  63.4 us

profile of v3, /device:TPU:0, one launch (start us, length us, event | category | flops | bytes accessed | tf_op | source)
XLA Modules:
  0.0 182.1 jit_solution(7095242002518625290)
XLA Ops:
  0.0 0.7 stack.9
  0.7 0.7 stack.10
  1.4 0.6 pad_add_fusion.table
  2.0 114.9 %front_stage.1 = (bf16[16,4,16,256]{3,2,1,0:T(8,128)(2,1)}, bf16[16,4,16,512]{3,2,1,0:T(8,128)(2,1)}, f32[16,4,16,1]{3,2,1,0:T(8,128)}) custom-call(bf16[64,4096]{1,0:T(8,128)(2,1)} %tokens.3, f32[1,4096]{1,0:T(1,128)} %bitcast.12, f32[1,4096]{1,0:T(1,128)} %bitcast.13, f32[1,512]{1,0:T(1,128)} %bitcast.15, s32[2,257]{1,0:T(2,128)} %pad_add_fusion.table, ...), custom_call_target="tpu_custom_call" | custom-call | tf_op jit(solution)/shard_map/front_stage/pallas_call | solution.py:664
  116.9 63.4 %output_stage.1 = bf16[64,4096]{1,0:T(8,128)(2,1)} custom-call(bf16[16,4,16,256]{3,2,1,0:T(8,128)(2,1)} %get-tuple-element.8.attended, bf16[16,4,16,512]{3,2,1,0:T(8,128)(2,1)} %get-tuple-element.9.hidden, f32[16,4,16,1]{3,2,1,0:T(8,128)} %get-tuple-element.10.adapter, bf16[64,4096]{1,0:T(8,128)(2,1)} %tokens.3, f32[1,4096]{1,0:T(1,128)} %bitcast.14, ...), custom_call_target="tpu_custom_call" | custom-call | tf_op jit(solution)/shard_map/output_stage/pallas_call | solution.py:712
  180.2 1.9 %copy.20 = bf16[64,4096]{1,0:T(8,128)(2,1)} copy(bf16[64,4096]{1,0:T(8,128)(2,1)} %output_stage.1) | data formatting | bytes 1048576

commit v4 on v2

--- a/solution.py
+++ b/solution.py
@@ -20,7 +20,8 @@
 GROUP = 16
 UNIT = 16
 QKV = 3 * HEAD
-CUT = 6
+CUT = 96
+LATE = 128
 
 
 def dot(a, b):
@@ -50,7 +51,7 @@
     return sem
 
 
-def exchange_sum(me, packed, landed, full, sems, meanwhile):
+def exchange_start(me, packed, landed, sems):
     def scatter(k, carry):
         to = (me + k) % GROUP
         pltpu.make_async_remote_copy(
@@ -60,7 +61,9 @@
 
     lax.fori_loop(1, GROUP, scatter, 0)
     landed[me] = packed[me]
-    meanwhile()
+
+
+def exchange_middle(me, landed, full, sems):
     many = landed.at[pl.ds(0, GROUP - 1)]
     pltpu.make_async_copy(many, many, sems.at[1]).wait()
     full[me] = jnp.sum(landed[...].astype(F32), axis=0).astype(BF16)
@@ -73,13 +76,12 @@
         return carry
 
     lax.fori_loop(1, GROUP, gather, 0)
-    pltpu.make_async_copy(many, many, sems.at[0]).wait()
-    return many
-
-
-def exchange_wait(many, sems):
-    pltpu.make_async_copy(many, many, sems.at[3]).wait()
-    pltpu.make_async_copy(many, many, sems.at[2]).wait()
+
+
+def exchange_end(landed, sems):
+    many = landed.at[pl.ds(0, GROUP - 1)]
+    for number in (3, 0, 2):
+        pltpu.make_async_copy(many, many, sems.at[number]).wait()
 
 
 GATHER_GROUPS = (
@@ -91,10 +93,11 @@
 
 
 def front_kernel(
-    tokens, gain, bias, in_bias, lengths, request_adapter, slots, frequency, w_qkv, w_up, w_left, w_qkv_right, w_up_right,
+    tokens, gain, bias, in_bias, table, slots, w_qkv, w_up, w_left, w_qkv_right, w_up_right,
     out_attended, out_hidden, adapter,
     xs, weights, right_qkv, right_up, rows_in, acc, picked, packed, landed, full,
-    starts, cosine, sine, queries, window, passing, top, total, summed,
+    starts, row_index, row_start, row_adapter, names, cosine, sine, ranks, row_ranks, queries,
+    early, late, pass_early, pass_late, top, total, summed,
     load_sems, send_sem, recv_sems, ex_sems, near_send, near_recv,
 ):
     plane = Plane()
@@ -151,14 +154,14 @@
         for step in (1, -1):
             send(me, half, whole, 2, step)
 
-    long = lengths[...].astype(F32)
+    long = table[0:1, :].astype(F32)
     requests = long.shape[1]
     before = lax.broadcasted_iota(jnp.int32, (requests, requests), 0) < lax.broadcasted_iota(
         jnp.int32, (requests, requests), 1
     )
     begins = dot(jnp.broadcast_to(long, (8, requests)).astype(BF16), before.astype(F32).astype(BF16))[:1, :]
     ends = begins + long
-    ids = request_adapter[...].astype(F32)
+    ids = table[1:2, :].astype(F32)
 
     def locate(block, carry):
         rows = lax.broadcasted_iota(jnp.int32, (64, 1), 0)
@@ -172,6 +175,22 @@
 
     lax.fori_loop(0, GROUP, locate, 0)
 
+    def pieces(number):
+        return [(i, plane.source(h, d1, d2), h) for i, (h, d1, d2) in enumerate(GATHER_GROUPS[number])]
+
+    piece_row = lax.broadcasted_iota(jnp.int32, (32, 1), 0)
+    piece_lane = lax.broadcasted_iota(jnp.int32, (1, 256), 1)
+    for number in range(4):
+        name = piece_lane
+        for i, slot, half in pieces(number):
+            at = slice(i * 32, (i + 1) * 32)
+            first = slot * 64 + half * 32
+            row_index[number, at, :] = (req * count + first + piece_row).astype(F32)
+            row_start[number, at, :] = starts[slot, 2 * half : 2 * half + 2].reshape(32, 1)
+            row_adapter[number, at, :] = adapter[slot, 2 * half : 2 * half + 2].reshape(32, 1)
+            name = jnp.where(piece_lane // 32 == i, first + piece_lane % 32, name)
+        names[:, number * 256 : (number + 1) * 256] = name.astype(F32)
+
     for half in (0, 1):
         for d1 in (1, -1):
             slot = landed_piece(half, d1, 0, whole)
@@ -187,40 +206,100 @@
     lane = lax.broadcasted_iota(jnp.int32, (1, 128), 1)
     even = lane % 2 == 0
 
-    def angles(block, carry):
-        rows = lax.broadcasted_iota(jnp.int32, (64, 1), 0)
-        index = (req * count + block * 64 + rows).astype(F32)
-        angle = (index - starts[block].reshape(64, 1)) * frequency[...]
+    frequency = jnp.exp((lane // 2).astype(F32) * (-2.0 * math.log(10000.0) / ROT))
+
+    def angles(number, carry):
+        angle = (row_index[number] - row_start[number]) * frequency
         turned = lane < ROT
-        cosine[block] = jnp.where(turned, jnp.cos(angle), 1.0).reshape(4, UNIT, 128)
-        sine[block] = jnp.where(turned, jnp.where(even, -1.0, 1.0) * jnp.sin(angle), 0.0).reshape(4, UNIT, 128)
+        cosine[number] = jnp.where(turned, jnp.cos(angle), 1.0)
+        sine[number] = jnp.where(turned, jnp.where(even, -1.0, 1.0) * jnp.sin(angle), 0.0)
         return carry
 
+    chosen = jnp.where(lane < 32, slots[0], jnp.where(lane < 64, slots[1], jnp.where(lane < 96, slots[2], slots[3])))
+    chosen = chosen.astype(F32)
+
     def multiply(number):
-        for i, (half, d1, d2) in enumerate(GATHER_GROUPS[number]):
-            rows_in[i * 32 : (i + 1) * 32, :] = xs[plane.source(half, d1, d2), pl.ds(half * 32, 32), :]
+        for i, slot, half in pieces(number):
+            rows_in[i * 32 : (i + 1) * 32, :] = xs[slot, pl.ds(half * 32, 32), :]
         left = dot(rows_in[...], weights[:, QKV + hid :])
-        for i, (half, d1, d2) in enumerate(GATHER_GROUPS[number]):
-            slot = plane.source(half, d1, d2)
-            for u in (0, 1):
-                at = i * 32 + u * UNIT
-                picked[slot, half * 2 + u] = left[at : at + UNIT, :].astype(BF16)
+        kept = jnp.where(row_adapter[number] == chosen, left, 0.0).astype(BF16)
+        for i, slot, half in pieces(number):
+            picked[slot, 2 * half : 2 * half + 2] = kept[i * 32 : (i + 1) * 32, :].reshape(2, UNIT, 128)
 
     def multiply_wide(number, begin, end):
         def column(n, carry):
             columns = pl.ds(pl.multiple_of(n * 256, 256), 256)
-            result = dot(rows_in[...], weights[:, columns])
-            for i, (half, d1, d2) in enumerate(GATHER_GROUPS[number]):
-                slot = plane.source(half, d1, d2)
-                for u in (0, 1):
-                    at = i * 32 + u * UNIT
-                    acc[slot, half * 2 + u, :, columns] = result[at : at + UNIT, :]
+            acc[number, :, columns] = dot(rows_in[...], weights[:, columns])
             return carry
 
         lax.fori_loop(begin, end, column, 0)
 
+    low, high, every = pl.ds(0, CUT), pl.ds(CUT, 256 - CUT), pl.ds(0, 256)
+    started = []
+
+    def view(slot, part, rows=every):
+        return early.at[slot, part, rows] if part < 4 else late.at[slot, :, rows]
+
+    def pass_on(src, dst, number, device):
+        copy = pltpu.make_async_remote_copy(
+            src, dst, near_send.at[number], near_recv.at[number], device_id={"req": device}, device_id_type=MESH
+        )
+        copy.start()
+        started.append(copy)
+
+    def take(ref, number):
+        pltpu.make_async_copy(ref, ref, near_recv.at[number]).wait()
+
+    def by_way(part):
+        return pass_early.at[part] if part < 4 else pass_late
+
+    def near_sends(part):
+        if part < 4:
+            early[0, part] = acc[part, :, HEAD:QKV].astype(BF16)
+        at = 10 * part
+        pass_on(view(0, part, low), view(2, part, low), at, ahead)
+        pass_on(view(0, part, high), by_way(part), at + 2, behind)
+        pass_on(view(0, part, high), view(2, part, high), at + 1, ahead)
+        pass_on(view(0, part), view(1 + 4 * core, part), at + 3, other)
+
+    def near_low(part):
+        at = 10 * part
+        take(view(2, part, low), at)
+        pass_on(view(2, part, low), view(4, part, low), at + 6, ahead)
+        pass_on(view(2, part, low), view(3 - 2 * core, part, low), at + 4, other)
+
+    def near_passing(part):
+        at = 10 * part
+        take(by_way(part), at + 2)
+        pass_on(by_way(part), view(4, part, high), at + 7, behind)
+
+    def near_high(part):
+        at = 10 * part
+        take(view(2, part, high), at + 1)
+        pass_on(view(2, part, high), view(3 - 2 * core, part, high), at + 5, other)
+
+    def near_relays(part):
+        near_low(part)
+        near_passing(part)
+        near_high(part)
+
+    def next_relays(part):
+        at = 10 * part
+        take(view(4, part, high), at + 7)
+        pass_on(view(4, part, high), view(5 - 2 * core, part, high), at + 9, other)
+        take(view(4, part, low), at + 6)
+        pass_on(view(4, part, low), view(5 - 2 * core, part, low), at + 8, other)
+
+    def take_all(slot, first, second=None):
+        for part in range(5):
+            if second is None:
+                take(view(slot, part), 10 * part + first)
+            else:
+                take(view(slot, part, low), 10 * part + first)
+                take(view(slot, part, high), 10 * part + second)
+
     tiles = (QKV + hid) // 256
-    lax.fori_loop(0, GROUP // 2, angles, 0)
+    lax.fori_loop(0, 2, angles, 0)
     for half in (0, 1):
         for d2 in (1, -1):
             relay(half, 0, d2, (whole,))
@@ -233,176 +312,164 @@
         load.wait()
     multiply(0)
     multiply_wide(0, 0, tiles)
+    near_sends(0)
     for half in (0, 1):
         for d1 in (1, -1):
             for d2 in (1, -1):
                 relay(half, d1, d2, (whole,))
     multiply(1)
     multiply_wide(1, 0, tiles)
-    lax.fori_loop(GROUP // 2, GROUP, angles, 0)
+    near_sends(1)
+    near_low(0)
+    near_passing(0)
+    lax.fori_loop(2, 4, angles, 0)
     for half in (0, 1):
         for d2 in (1, -1):
             relay(half, 2, d2, ((0, 1), (1, 1)))
+    near_high(0)
     multiply(2)
     multiply_wide(2, 0, tiles)
+    near_sends(2)
+    near_relays(1)
     for half in (0, 1):
         for d1 in (0, 1, -1, 2):
             for unit in ((0, 1), (1, 1)):
                 landed_piece(half, d1, 2, unit)
     multiply(3)
 
-    chosen = jnp.where(lane < 32, slots[0], jnp.where(lane < 64, slots[1], jnp.where(lane < 96, slots[2], slots[3])))
-    chosen = chosen.astype(F32)
     row_id = lax.broadcasted_iota(jnp.int32, (128, 128), 0)
     col_id = lax.broadcasted_iota(jnp.int32, (128, 128), 1)
     together = jnp.zeros((256, 128), F32)
     for unit in range(4):
-        mine = adapter[:, unit].reshape(256, 1) == chosen
-        kept = jnp.where(mine, picked[:, unit].reshape(256, 128).astype(F32), 0.0).astype(BF16)
         fold = jnp.logical_and(col_id // 32 == unit, row_id % 32 == col_id % 32).astype(F32).astype(BF16)
-        together = together + dot(kept, fold)
+        together = together + dot(picked[:, unit].reshape(256, 128), fold)
     packed[...] = together.astype(BF16).reshape(GROUP, UNIT, 128)
-    many = exchange_sum(me, packed, landed, full, ex_sems, lambda: multiply_wide(3, 0, 2))
-    multiply_wide(3, 2, tiles)
-    exchange_wait(many, ex_sems)
+    exchange_start(me, packed, landed, ex_sems)
+    multiply_wide(3, 1, 3)
+    near_sends(3)
+    exchange_middle(me, landed, full, ex_sems)
+    multiply_wide(3, 0, 1)
+    multiply_wide(3, 3, tiles)
+    near_relays(2)
+    next_relays(0)
     for load in loads[3:]:
         load.wait()
-
-    wide_lane = lax.broadcasted_iota(jnp.int32, (1, 1024), 1)
-    owner = (wide_lane // RANK).astype(F32)
-    row_id = lax.broadcasted_iota(jnp.int32, (128, 1024), 0)
-    col_id = lax.broadcasted_iota(jnp.int32, (128, 1024), 1)
-
-    def widened(unit, first):
-        spread = (row_id == unit * 32 + first + col_id % RANK).astype(F32).astype(BF16)
-        mine = adapter[:, unit].reshape(256, 1) == owner
-        return jnp.where(mine, dot(full[...].reshape(256, 128), spread), 0.0).astype(BF16)
-
-    def finish_heads(unit, carry):
-        wide = widened(unit, 0)
-        turn = cosine[:, unit].reshape(256, 128)
-        sway = sine[:, unit].reshape(256, 128)
-        for part in range(3):
-            columns = slice(part * HEAD, (part + 1) * HEAD)
-            value = acc[:, unit, :, columns].reshape(256, HEAD) + dot(wide, right_qkv[:, columns])
-            if part < 2:
-                head = value[:, :128]
-                swapped = jnp.where(even, pltpu.roll(head, 127, 1), pltpu.roll(head, 1, 1))
-                value = jnp.concatenate([head * turn + swapped * sway, value[:, 128:]], axis=1)
-            value = value.astype(BF16)
-            if part == 0:
-                queries[:, unit] = (value * jnp.asarray(HEAD ** (-0.5), BF16)).reshape(GROUP, UNIT, HEAD)
-            else:
-                window[0, :, unit, :, (part - 1) * HEAD : part * HEAD] = value.reshape(GROUP, UNIT, HEAD)
+    exchange_end(landed, ex_sems)
+    for unit in range(4):
+        spread = jnp.logical_and(row_id - unit * 32 == col_id - 64, row_id // 32 == unit).astype(F32).astype(BF16)
+        ranks[:, unit] = dot(full[...].reshape(256, 128), spread).astype(BF16).reshape(GROUP, UNIT, 128)
+    for number in range(4):
+        for i, slot, half in pieces(number):
+            row_ranks[number, i * 32 : (i + 1) * 32, :] = ranks[slot, 2 * half : 2 * half + 2].reshape(32, 128)
+
+    owner = (lax.broadcasted_iota(jnp.int32, (1, 1024), 1) // RANK).astype(F32)
+    spread_row = lax.broadcasted_iota(jnp.int32, (128, 1024), 0)
+    spread_col = lax.broadcasted_iota(jnp.int32, (128, 1024), 1)
+    fold_row = lax.broadcasted_iota(jnp.int32, (1024, 128), 0)
+    fold_col = lax.broadcasted_iota(jnp.int32, (1024, 128), 1)
+
+    def widened(values, mine, first):
+        spread = (spread_row == 64 + first + spread_col % RANK).astype(F32).astype(BF16)
+        return jnp.where(mine, dot(values, spread), 0.0).astype(BF16)
+
+    def turn(head, number):
+        swapped = jnp.where(even, pltpu.roll(head, 127, 1), pltpu.roll(head, 1, 1))
+        return head * cosine[number] + swapped * sine[number]
+
+    def heads(number, carry):
+        mine = row_adapter[number] == owner
+        own = row_ranks[number]
+        wide = widened(own, mine, 0)
+        query = acc[number, :, :HEAD] + dot(wide, right_qkv[:, :HEAD])
+        scale = jnp.asarray(HEAD ** (-0.5), BF16)
+        first = turn(query[:, :128], number).astype(BF16) * scale
+        second = query[:, 128:].astype(BF16) * scale
+        main = jnp.concatenate([jnp.where(lane < ROT, 0.0, first.astype(F32)).astype(BF16), second], axis=1)
+        back = lax.dot_general(
+            main, right_qkv[:, HEAD : 2 * HEAD], (((1,), (1,)), ((), ())), preferred_element_type=F32
+        )
+        fold = (fold_col == 64 + fold_row % RANK).astype(F32).astype(BF16)
+        low_rank = dot(jnp.where(mine, back, 0.0).astype(BF16), fold)
+        queries[number, :, :HEAD] = main
+        queries[number, :, HEAD:] = jnp.where(lane < ROT, first.astype(F32), low_rank).astype(BF16)
+        key = acc[number, :, HEAD : HEAD + 128] + dot(wide, right_qkv[:, HEAD : HEAD + 128])
+        late[0, number] = jnp.where(lane < ROT, turn(key, number), own.astype(F32)).astype(BF16)
         return carry
 
-    def finish_hidden(unit, carry):
-        wide = widened(unit, RANK)
+    lax.fori_loop(0, 4, heads, 0)
+    near_sends(4)
+
+    def finish_hidden(number):
+        wide = widened(row_ranks[number], row_adapter[number] == owner, RANK)
         for part in range(hid // 256):
             columns = slice(part * 256, (part + 1) * 256)
-            value = acc[:, unit, :, QKV + part * 256 : QKV + (part + 1) * 256].reshape(256, 256)
+            value = acc[number, :, QKV + part * 256 : QKV + (part + 1) * 256]
             value = value + dot(wide, right_up[:, columns]) + in_bias[:, columns]
-            value = jax.nn.gelu(value, approximate=True)
-            out_hidden[:, unit, :, columns] = value.astype(BF16).reshape(GROUP, UNIT, 256)
-        return carry
-
-    lax.fori_loop(0, 4, finish_heads, 0)
-
-    low, high = pl.ds(0, CUT), pl.ds(CUT, GROUP - CUT)
-    started = []
-
-    def pass_on(src, dst, number, device):
-        copy = pltpu.make_async_remote_copy(
-            src, dst, near_send.at[number], near_recv.at[number], device_id={"req": device}, device_id_type=MESH
-        )
-        copy.start()
-        started.append(copy)
-
-    def take(ref, number):
-        pltpu.make_async_copy(ref, ref, near_recv.at[number]).wait()
-
-    pass_on(window.at[0, low], window.at[2, low], 0, ahead)
-    pass_on(window.at[0, high], passing, 2, behind)
-    pass_on(window.at[0, high], window.at[2, high], 1, ahead)
-    pass_on(window.at[0], window.at[1 + 4 * core], 3, other)
-
-    def attend(slot, m0, m1, b, causal):
-        keys = window[slot, m0:m1, :, :, :HEAD].reshape((m1 - m0) * 64, HEAD)
-        values = window[slot, m0:m1, :, :, HEAD:].reshape((m1 - m0) * 64, HEAD)
-        four = pl.ds(b * 4, 4)
-        scores = lax.dot_general(
-            queries[four].reshape(256, HEAD), keys, (((1,), (1,)), ((), ())), preferred_element_type=F32
-        )
-        key_id = lax.broadcasted_iota(jnp.int32, (1, (m1 - m0) * 64), 1) + (req - slot) * count + m0 * 64
-        allowed = key_id.astype(F32) >= starts[four].reshape(256, 1)
-        if causal:
-            row = lax.broadcasted_iota(jnp.int32, (256, 1), 0) + req * count + b * 256
-            allowed = jnp.logical_and(allowed, key_id <= row)
-        scores = jnp.where(allowed, scores, NEGATIVE_FILL)
-        peak = jnp.max(scores, axis=1, keepdims=True)
-        if causal:
-            kept = jnp.exp(scores - peak)
+            value = jax.nn.gelu(value, approximate=True).astype(BF16)
+            for i, slot, half in pieces(number):
+                out_hidden[slot, 2 * half : 2 * half + 2, :, columns] = value[i * 32 : (i + 1) * 32, :].reshape(
+                    2, UNIT, 256
+                )
+
+    def attend_all(slot, own=False):
+        def body(b, carry):
+            tail = late[slot].reshape(count, LATE)
+            keys = jnp.concatenate([early[slot, :, :, :HEAD].reshape(count, HEAD), tail], axis=1)
+            values = jnp.concatenate([early[slot, :, :, HEAD:].reshape(count, HEAD), tail], axis=1)
+            scores = lax.dot_general(queries[b], keys, (((1,), (1,)), ((), ())), preferred_element_type=F32)
+            key_id = names[...] + ((req - slot) * count).astype(F32)
+            allowed = key_id >= row_start[b]
+            if own:
+                allowed = jnp.logical_and(allowed, key_id <= row_index[b])
+            scores = jnp.where(allowed, scores, NEGATIVE_FILL)
+            peak = jnp.max(scores, axis=1, keepdims=True)
+            if own:
+                kept = jnp.exp(scores - peak)
+                total[b] = jnp.sum(kept, axis=1, keepdims=True)
+                summed[b] = dot(kept.astype(BF16), values)
+            else:
+                old = top[b]
+                peak = jnp.maximum(old, peak)
+                kept = jnp.exp(scores - peak)
+                decay = jnp.exp(old - peak)
+                total[b] = total[b] * decay + jnp.sum(kept, axis=1, keepdims=True)
+                summed[b] = summed[b] * decay + dot(kept.astype(BF16), values)
             top[b] = peak
-            total[b] = jnp.sum(kept, axis=1, keepdims=True)
-            summed[b] = dot(kept.astype(BF16), values)
-        else:
-            old = top[b]
-            peak = jnp.maximum(old, peak)
-            kept = jnp.exp(scores - peak)
-            decay = jnp.exp(old - peak)
-            top[b] = peak
-            total[b] = total[b] * decay + jnp.sum(kept, axis=1, keepdims=True)
-            summed[b] = summed[b] * decay + dot(kept.astype(BF16), values)
-
-    def attend_all(slot, m0, m1):
-        def body(b, carry):
-            attend(slot, m0, m1, b, False)
             return carry
 
         lax.fori_loop(0, 4, body, 0)
 
-    for b in range(4):
-        attend(0, 0, (b + 1) * 4, b, True)
-    take(window.at[2, low], 0)
-    pass_on(window.at[2, low], window.at[4, low], 6, ahead)
-    pass_on(window.at[2, low], window.at[3 - 2 * core, low], 4, other)
-    take(window.at[5 - 4 * core], 3)
-
-    @pl.when(core == 1)
-    def _():
-        attend_all(1, 0, GROUP)
-
-    take(passing, 2)
-    pass_on(passing, window.at[4, high], 7, behind)
-    lax.fori_loop(0, 4, finish_hidden, 0)
-    attend_all(2, 0, CUT)
-    take(window.at[2, high], 1)
-    pass_on(window.at[2, high], window.at[3 - 2 * core, high], 5, other)
-    attend_all(2, CUT, GROUP)
-    take(window.at[1 + 2 * core, low], 4)
-    attend_all(1 + 2 * core, 0, CUT)
-    take(window.at[1 + 2 * core, high], 5)
-    attend_all(1 + 2 * core, CUT, GROUP)
-    take(window.at[4, high], 7)
-    pass_on(window.at[4, high], window.at[5 - 2 * core, high], 9, other)
-    attend_all(4, CUT, GROUP)
-    take(window.at[4, low], 6)
-    pass_on(window.at[4, low], window.at[5 - 2 * core, low], 8, other)
-    attend_all(4, 0, CUT)
-    take(window.at[3 + 2 * core, high], 9)
-
-    @pl.when(core == 0)
-    def _():
-        attend_all(3, CUT, GROUP)
-
-    take(window.at[3 + 2 * core, low], 8)
-
-    @pl.when(core == 0)
-    def _():
-        attend_all(3, 0, CUT)
-
-    for b in range(4):
-        out_attended[b * 4 : (b + 1) * 4] = (summed[b] / total[b]).astype(BF16).reshape(4, 4, UNIT, HEAD)
+    def attend_on(which, slot):
+        @pl.when(core == which)
+        def _():
+            attend_all(slot)
+
+    near_relays(3)
+    next_relays(1)
+    next_relays(2)
+    attend_all(0, True)
+    near_low(4)
+    near_passing(4)
+    next_relays(3)
+    take_all(5 - 4 * core, 3)
+    attend_on(1, 1)
+    near_high(4)
+    attend_all(2)
+    next_relays(4)
+    take_all(1 + 2 * core, 4, 5)
+    attend_all(1 + 2 * core)
+    attend_all(4)
+    take_all(3 + 2 * core, 8, 9)
+    attend_on(0, 3)
+    for number in range(4):
+        finish_hidden(number)
+    for number in range(4):
+        share = 1.0 / total[number]
+        tail = (summed[number, :, HEAD:] * share).astype(BF16)
+        wide = widened(tail, row_adapter[number] == owner, 0)
+        value = (summed[number, :, :HEAD] * share + dot(wide, right_qkv[:, 2 * HEAD :])).astype(BF16)
+        for i, slot, half in pieces(number):
+            out_attended[slot, 2 * half : 2 * half + 2] = value[i * 32 : (i + 1) * 32, :].reshape(2, UNIT, HEAD)
     for copy in started:
         copy.wait_send()
     sent = xs.at[pl.ds(0, GROUP - 1)]
@@ -459,10 +526,11 @@
     together = lax.fori_loop(0, 4, lower, jnp.zeros((256, 128), F32))
     packed[...] = together.astype(BF16).reshape(GROUP, UNIT, 128)
     pl.semaphore_wait(sem, GROUP - 1)
-    many = exchange_sum(me, packed, landed, full, ex_sems, lambda: None)
+    exchange_start(me, packed, landed, ex_sems)
+    exchange_middle(me, landed, full, ex_sems)
     for load in loads[4:]:
         load.wait()
-    exchange_wait(many, ex_sems)
+    exchange_end(landed, ex_sems)
     lane = lax.broadcasted_iota(jnp.int32, (1, 128), 1)
     row_id = lax.broadcasted_iota(jnp.int32, (128, 128), 0)
     col_id = lax.broadcasted_iota(jnp.int32, (128, 128), 1)
@@ -573,8 +641,6 @@
 ):
     rows, width = tokens.shape
     hid = up_weight.shape[1]
-    lane = lax.iota(jnp.int32, 128)
-    frequency = jnp.exp((lane // 2).astype(F32) * (-2.0 * math.log(10000.0) / ROT))
     vmem = pl.BlockSpec(memory_space=pltpu.VMEM)
     smem = pl.BlockSpec(memory_space=pltpu.SMEM)
     anywhere = pl.BlockSpec(memory_space=pl.ANY)
@@ -587,7 +653,7 @@
             jax.ShapeDtypeStruct(by_unit + (hid,), BF16),
             jax.ShapeDtypeStruct(by_unit + (1,), F32),
         ),
-        in_specs=[vmem] * 6 + [smem] + [vmem] + [anywhere] * 5,
+        in_specs=[vmem] * 5 + [smem] + [anywhere] * 5,
         out_specs=(vmem, vmem, vmem),
         scratch_shapes=[
             pltpu.VMEM((GROUP, rows, width), BF16),
@@ -595,34 +661,42 @@
             pltpu.VMEM(query_key_value_right.shape[:1] + (QKV,), BF16),
             pltpu.VMEM(up_adapter_right.shape, BF16),
             pltpu.VMEM((256, width), BF16),
-            pltpu.VMEM(by_unit + (QKV + hid,), F32),
+            pltpu.VMEM((4, 256, QKV + hid), F32),
             pltpu.VMEM(by_unit + (128,), BF16),
             pltpu.VMEM((GROUP, UNIT, 128), BF16),
             pltpu.VMEM((GROUP, UNIT, 128), BF16),
             pltpu.VMEM((GROUP, UNIT, 128), BF16),
             pltpu.VMEM(by_unit + (1,), F32),
-            pltpu.VMEM(by_unit + (128,), F32),
-            pltpu.VMEM(by_unit + (128,), F32),
-            pltpu.VMEM(by_unit + (HEAD,), BF16),
-            pltpu.VMEM((6,) + by_unit + (2 * HEAD,), BF16),
-            pltpu.VMEM((GROUP - CUT, 4, UNIT, 2 * HEAD), BF16),
             pltpu.VMEM((4, 256, 1), F32),
             pltpu.VMEM((4, 256, 1), F32),
-            pltpu.VMEM((4, 256, HEAD), F32),
+            pltpu.VMEM((4, 256, 1), F32),
+            pltpu.VMEM((1, 1024), F32),
+            pltpu.VMEM((4, 256, 128), F32),
+            pltpu.VMEM((4, 256, 128), F32),
+            pltpu.VMEM(by_unit + (128,), BF16),
+            pltpu.VMEM((4, 256, 128), BF16),
+            pltpu.VMEM((4, 256, HEAD + LATE), BF16),
+            pltpu.VMEM((6, 4, 256, 2 * HEAD), BF16),
+            pltpu.VMEM((6, 4, 256, LATE), BF16),
+            pltpu.VMEM((4, 256 - CUT, 2 * HEAD), BF16),
+            pltpu.VMEM((4, 256 - CUT, LATE), BF16),
+            pltpu.VMEM((4, 256, 1), F32),
+            pltpu.VMEM((4, 256, 1), F32),
+            pltpu.VMEM((4, 256, HEAD + LATE), F32),
             dma((5,)),
             dma,
             dma((GROUP, 4)),
             dma((4,)),
-            dma((10,)),
-            dma((10,)),
+            dma((50,)),
+            dma((50,)),
         ],
         compiler_params=pltpu.CompilerParams(
             collective_id=0, has_side_effects=True, vmem_limit_bytes=VMEM_LIMIT
         ),
         name="front_stage",
     )(
-        tokens, layer_norm_gain[None, :], layer_norm_bias[None, :], input_bias[None, :], lengths[None, :],
-        request_adapter[None, :], slot_adapter, frequency[None, :],
+        tokens, layer_norm_gain[None, :], layer_norm_bias[None, :], input_bias[None, :],
+        jnp.stack([lengths, request_adapter]), slot_adapter,
         query_key_weight.reshape(width, QKV), up_weight, input_adapter_left,
         query_key_value_right.reshape(-1, QKV), up_adapter_right,
     )

time: 185 us -> 172 us (0.930)
  Pallas kernels: 180 us -> 168 us
    pallas_call x1, Pallas kernels: 117 us -> 103 us  [per_device(): pl.pallas_call(front_kernel, out_shape=(jax.ShapeDtypeStruct(by_unit + (H...]
    pallas_call x1, Pallas kernels: 62.3 us -> 65.2 us  [per_device(): pl.pallas_call(output_kernel, out_shape=jax.ShapeDtypeStruct((rows, width...]
    broadcast_in_dim x2 -> x0, local copies, waits for them, and re-layouts: 2.5 us -> none  [the longest x1 1.26 us: per_device(): request_adapter[None, :]]
where the time goes in v4:
time: 172 us
  Pallas kernels  168 us (98%)
  local copies, waits for them, and re-layouts  3.23 us (2%)
    pallas_call x1, Pallas kernels, per_device(): pl.pallas_call(front_kernel, out_shape=(jax.ShapeDtypeStruct(by_unit + (H...  103 us
    pallas_call x1, Pallas kernels, per_device(): pl.pallas_call(output_kernel, out_shape=jax.ShapeDtypeStruct((rows, width...  65.2 us

profile of v4, /device:TPU:0, one launch (start us, length us, event | category | flops | bytes accessed | tf_op | source)
XLA Modules:
  0.0 172.0 jit_solution(2714389544995398526)
XLA Ops:
  0.0 0.7 stack.9
  0.7 0.7 stack.10
  1.4 0.6 pad_add_fusion.table
  2.0 102.9 %front_stage.1 = (bf16[16,4,16,256]{3,2,1,0:T(8,128)(2,1)}, bf16[16,4,16,512]{3,2,1,0:T(8,128)(2,1)}, f32[16,4,16,1]{3,2,1,0:T(8,128)}) custom-call(bf16[64,4096]{1,0:T(8,128)(2,1)} %tokens.3, f32[1,4096]{1,0:T(1,128)} %bitcast.12, f32[1,4096]{1,0:T(1,128)} %bitcast.13, f32[1,512]{1,0:T(1,128)} %bitcast.15, s32[2,257]{1,0:T(2,128)} %pad_add_fusion.table, ...), custom_call_target="tpu_custom_call" | custom-call | tf_op jit(solution)/shard_map/front_stage/pallas_call | solution.py:649
  104.9 65.2 %output_stage.1 = bf16[64,4096]{1,0:T(8,128)(2,1)} custom-call(bf16[16,4,16,256]{3,2,1,0:T(8,128)(2,1)} %get-tuple-element.8.attended, bf16[16,4,16,512]{3,2,1,0:T(8,128)(2,1)} %get-tuple-element.9.hidden, f32[16,4,16,1]{3,2,1,0:T(8,128)} %get-tuple-element.10.adapter, bf16[64,4096]{1,0:T(8,128)(2,1)} %tokens.3, f32[1,4096]{1,0:T(1,128)} %bitcast.14, ...), custom_call_target="tpu_custom_call" | custom-call | tf_op jit(solution)/shard_map/output_stage/pallas_call | solution.py:705
  170.1 1.9 %copy.20 = bf16[64,4096]{1,0:T(8,128)(2,1)} copy(bf16[64,4096]{1,0:T(8,128)(2,1)} %output_stage.1) | data formatting | bytes 1048576

commit v5 on v4

--- a/solution.py
+++ b/solution.py
@@ -15,7 +15,7 @@
 MESH = pl.DeviceIdType.MESH
 F32 = jnp.float32
 BF16 = jnp.bfloat16
-VMEM_LIMIT = 60 * 1024 * 1024
+VMEM_LIMIT = 63 * 1024 * 1024
 SIDE = 4
 GROUP = 16
 UNIT = 16
@@ -92,13 +92,24 @@
 )
 
 
-def front_kernel(
-    tokens, gain, bias, in_bias, table, slots, w_qkv, w_up, w_left, w_qkv_right, w_up_right,
-    out_attended, out_hidden, adapter,
+REDUCE_GROUPS = (
+    tuple((h, d1, 2) for h in (0, 1) for d1 in (2, 1, -1, 0)),
+    tuple((h, d1, d2) for h in (0, 1) for d1 in (2, 1) for d2 in (1, -1)),
+    tuple((h, d1, d2) for h in (0, 1) for d1 in (-1, 0) for d2 in (1, -1)),
+    tuple((h, d1, 0) for h in (0, 1) for d1 in (2, 1, -1, 0)),
+)
+FAR = {2: 0, 1: 1, -1: 2, 0: 3}
+
+
+def layer_kernel(
+    tokens, gain, bias, in_bias, out_bias, table, slots, w_qkv, w_up, w_left, w_qkv_right, w_up_right,
+    w_left_attn, w_left_hid, w_attn, w_down, w_right,
+    out,
     xs, weights, right_qkv, right_up, rows_in, acc, picked, packed, landed, full,
-    starts, row_index, row_start, row_adapter, names, cosine, sine, ranks, row_ranks, queries,
+    starts, adapter, row_index, row_start, row_adapter, names, cosine, sine, ranks, row_ranks, queries,
     early, late, pass_early, pass_late, top, total, summed,
-    load_sems, send_sem, recv_sems, ex_sems, near_send, near_recv,
+    inputs, left, chosen_rows, from2, from1,
+    load_sems, send_sem, recv_sems, ex_sems, near_send, near_recv, weight_sems, back_sem, sems2, sems1,
 ):
     plane = Plane()
     me = plane.me
@@ -115,6 +126,8 @@
         pltpu.make_async_copy(w_left, weights.at[:, pl.ds(QKV + hid, 128)], load_sems.at[2]),
         pltpu.make_async_copy(w_qkv_right, right_qkv, load_sems.at[3]),
         pltpu.make_async_copy(w_up_right, right_up, load_sems.at[4]),
+        pltpu.make_async_copy(w_left_attn, left.at[pl.ds(0, HEAD)], load_sems.at[5]),
+        pltpu.make_async_copy(w_left_hid, left.at[pl.ds(HEAD, hid)], load_sems.at[6]),
     ]
     for load in loads:
         load.start()
@@ -343,21 +356,34 @@
     for unit in range(4):
         fold = jnp.logical_and(col_id // 32 == unit, row_id % 32 == col_id % 32).astype(F32).astype(BF16)
         together = together + dot(picked[:, unit].reshape(256, 128), fold)
-    packed[...] = together.astype(BF16).reshape(GROUP, UNIT, 128)
-    exchange_start(me, packed, landed, ex_sems)
+    packed[0] = together.astype(BF16).reshape(GROUP, UNIT, 128)
+    exchange_start(me, packed.at[0], landed.at[0], ex_sems.at[0])
     multiply_wide(3, 1, 3)
     near_sends(3)
-    exchange_middle(me, landed, full, ex_sems)
+    exchange_middle(me, landed.at[0], full.at[0], ex_sems.at[0])
     multiply_wide(3, 0, 1)
     multiply_wide(3, 3, tiles)
+    depth = HEAD + hid
+    width = out.shape[1]
+    deep = depth + 128
+    stored = []
+    for n in range(width // 256):
+        columns = pl.ds(n // 4 * 256, 256)
+        for j, (ref, first, size) in enumerate(((w_attn, 0, HEAD), (w_down, HEAD, hid), (w_right, depth, 128))):
+            copy = pltpu.make_async_copy(
+                ref.at[:, pl.ds(n * 256, 256)], weights.at[pl.ds(n % 4 * deep + first, size), columns],
+                weight_sems.at[n * 3 + j],
+            )
+            copy.start()
+            stored.append(copy)
     near_relays(2)
     next_relays(0)
     for load in loads[3:]:
         load.wait()
-    exchange_end(landed, ex_sems)
+    exchange_end(landed.at[0], ex_sems.at[0])
     for unit in range(4):
         spread = jnp.logical_and(row_id - unit * 32 == col_id - 64, row_id // 32 == unit).astype(F32).astype(BF16)
-        ranks[:, unit] = dot(full[...].reshape(256, 128), spread).astype(BF16).reshape(GROUP, UNIT, 128)
+        ranks[:, unit] = dot(full[0].reshape(256, 128), spread).astype(BF16).reshape(GROUP, UNIT, 128)
     for number in range(4):
         for i, slot, half in pieces(number):
             row_ranks[number, i * 32 : (i + 1) * 32, :] = ranks[slot, 2 * half : 2 * half + 2].reshape(32, 128)
@@ -407,9 +433,9 @@
             value = value + dot(wide, right_up[:, columns]) + in_bias[:, columns]
             value = jax.nn.gelu(value, approximate=True).astype(BF16)
             for i, slot, half in pieces(number):
-                out_hidden[slot, 2 * half : 2 * half + 2, :, columns] = value[i * 32 : (i + 1) * 32, :].reshape(
-                    2, UNIT, 256
-                )
+                inputs[slot, 2 * half : 2 * half + 2, :, HEAD + part * 256 : HEAD + (part + 1) * 256] = value[
+                    i * 32 : (i + 1) * 32, :
+                ].reshape(2, UNIT, 256)
 
     def attend_all(slot, own=False):
         def body(b, carry):
@@ -444,14 +470,24 @@
         def _():
             attend_all(slot)
 
+    def lower(unit, first, begin, end):
+        mine = adapter[:, unit].reshape(256, 1) == owner
+        product = dot(inputs[:, unit, :, begin:end].reshape(256, end - begin), left[begin:end, :])
+        fold = (fold_col == unit * 32 + first + fold_row % RANK).astype(F32).astype(BF16)
+        return dot(jnp.where(mine, product, 0.0).astype(BF16), fold)
+
     near_relays(3)
     next_relays(1)
     next_relays(2)
+    finish_hidden(0)
     attend_all(0, True)
     near_low(4)
+    finish_hidden(1)
+    finish_hidden(2)
     near_passing(4)
     next_relays(3)
     take_all(5 - 4 * core, 3)
+    finish_hidden(3)
     attend_on(1, 1)
     near_high(4)
     attend_all(2)
@@ -459,105 +495,81 @@
     take_all(1 + 2 * core, 4, 5)
     attend_all(1 + 2 * core)
     attend_all(4)
+    together = lax.fori_loop(0, 4, lambda unit, sum_: sum_ + lower(unit, RANK, HEAD, depth), jnp.zeros((256, 128), F32))
     take_all(3 + 2 * core, 8, 9)
     attend_on(0, 3)
-    for number in range(4):
-        finish_hidden(number)
     for number in range(4):
         share = 1.0 / total[number]
         tail = (summed[number, :, HEAD:] * share).astype(BF16)
         wide = widened(tail, row_adapter[number] == owner, 0)
         value = (summed[number, :, :HEAD] * share + dot(wide, right_qkv[:, 2 * HEAD :])).astype(BF16)
         for i, slot, half in pieces(number):
-            out_attended[slot, 2 * half : 2 * half + 2] = value[i * 32 : (i + 1) * 32, :].reshape(2, UNIT, HEAD)
+            inputs[slot, 2 * half : 2 * half + 2, :, :HEAD] = value[i * 32 : (i + 1) * 32, :].reshape(2, UNIT, HEAD)
+    for unit in range(4):
+        together = together + lower(unit, 0, 0, HEAD)
+    packed[1] = together.astype(BF16).reshape(GROUP, UNIT, 128)
+    exchange_start(me, packed.at[1], landed.at[1], ex_sems.at[1])
     for copy in started:
         copy.wait_send()
     sent = xs.at[pl.ds(0, GROUP - 1)]
     pltpu.make_async_copy(sent, sent, send_sem).wait()
-
-
-REDUCE_GROUPS = (
-    tuple((h, d1, 2) for h in (0, 1) for d1 in (2, 1, -1, 0)),
-    tuple((h, d1, d2) for h in (0, 1) for d1 in (2, 1) for d2 in (1, -1)),
-    tuple((h, d1, d2) for h in (0, 1) for d1 in (-1, 0) for d2 in (1, -1)),
-    tuple((h, d1, 0) for h in (0, 1) for d1 in (2, 1, -1, 0)),
-)
-FAR = {2: 0, 1: 1, -1: 2, 0: 3}
-
-
-def output_kernel(
-    attended, hidden, adapter, tokens, out_bias, w_left_attn, w_left_hid, w_attn, w_down, w_right,
-    out,
-    inputs, left, weights, part, from2, from1, rows_in, packed, landed, full,
-    load_sems, send_sem, sems2, sems1, ex_sems,
-):
-    plane = Plane()
-    me = plane.me
-    hid = w_left_hid.shape[0]
-    depth = HEAD + hid
-    loads = [
-        pltpu.make_async_copy(attended, inputs.at[:, :, :, pl.ds(0, HEAD)], load_sems.at[0]),
-        pltpu.make_async_copy(hidden, inputs.at[:, :, :, pl.ds(HEAD, hid)], load_sems.at[1]),
-        pltpu.make_async_copy(w_left_attn, left.at[pl.ds(0, HEAD)], load_sems.at[2]),
-        pltpu.make_async_copy(w_left_hid, left.at[pl.ds(HEAD, hid)], load_sems.at[3]),
-        pltpu.make_async_copy(w_attn, weights.at[pl.ds(0, HEAD)], load_sems.at[4]),
-        pltpu.make_async_copy(w_down, weights.at[pl.ds(HEAD, hid)], load_sems.at[5]),
-        pltpu.make_async_copy(w_right, weights.at[pl.ds(depth, 128)], load_sems.at[6]),
-    ]
-    for load in loads:
-        load.start()
-    sem = barrier_all(me, GROUP)
-    for load in loads[:4]:
-        load.wait()
-
-    lane = lax.broadcasted_iota(jnp.int32, (1, 1024), 1)
-    fold_row = lax.broadcasted_iota(jnp.int32, (1024, 128), 0)
-    fold_col = lax.broadcasted_iota(jnp.int32, (1024, 128), 1)
-
-    def lower(unit, together):
-        mine = adapter[:, unit].reshape(256, 1) == (lane // RANK).astype(F32)
-        for first, begin, end in ((0, 0, HEAD), (RANK, HEAD, depth)):
-            product = dot(inputs[:, unit, :, begin:end].reshape(256, end - begin), left[begin:end, :])
-            kept = jnp.where(mine, product, 0.0).astype(BF16)
-            fold = (fold_col == unit * 32 + first + fold_row % RANK).astype(F32).astype(BF16)
-            together = together + dot(kept, fold)
-        return together
-
-    together = lax.fori_loop(0, 4, lower, jnp.zeros((256, 128), F32))
-    packed[...] = together.astype(BF16).reshape(GROUP, UNIT, 128)
-    pl.semaphore_wait(sem, GROUP - 1)
-    exchange_start(me, packed, landed, ex_sems)
-    exchange_middle(me, landed, full, ex_sems)
-    for load in loads[4:]:
-        load.wait()
-    exchange_end(landed, ex_sems)
-    lane = lax.broadcasted_iota(jnp.int32, (1, 128), 1)
-    row_id = lax.broadcasted_iota(jnp.int32, (128, 128), 0)
-    col_id = lax.broadcasted_iota(jnp.int32, (128, 128), 1)
+    for copy in stored:
+        copy.wait()
+
+    def back_weights(n, first, size):
+        return weights[pl.ds(pl.multiple_of(n % 4 * deep + first, 128), size), pl.ds(pl.multiple_of(n // 4 * 256, 256), 256)]
+
+    def base(n, carry):
+        acc[n % 4, :, pl.ds(pl.multiple_of(n // 4 * 256, 256), 256)] = dot(
+            chosen_rows[:, :depth], back_weights(n, 0, depth)
+        )
+        return carry
+
+    for i, (half, d1, d2) in enumerate(REDUCE_GROUPS[0]):
+        slot = plane.source(half, d1, d2)
+        chosen_rows[i * 32 : (i + 1) * 32, :depth] = inputs[slot, 2 * half : 2 * half + 2, :, :depth].reshape(32, depth)
+    tiles = width // 256
+    lax.fori_loop(0, tiles // 2, base, 0)
+    exchange_middle(me, landed.at[1], full.at[1], ex_sems.at[1])
+    lax.fori_loop(tiles // 2, tiles, base, 0)
+    exchange_end(landed.at[1], ex_sems.at[1])
+    held = (me * 4 + lane // 32).astype(F32)
     for unit in range(4):
-        mine = adapter[:, unit].reshape(256, 1) == (me * 4 + lane // 32).astype(F32)
+        mine = adapter[:, unit].reshape(256, 1) == held
         spread = (row_id == unit * 32 + col_id % 32).astype(F32).astype(BF16)
-        wide = jnp.where(mine, dot(full[...].reshape(256, 128), spread), 0.0).astype(BF16)
+        wide = jnp.where(mine, dot(full[1].reshape(256, 128), spread), 0.0).astype(BF16)
         inputs[:, unit, :, depth:] = wide.reshape(GROUP, UNIT, 128)
 
-    def multiply(number):
+    def first_group():
+        for i, (half, d1, d2) in enumerate(REDUCE_GROUPS[0]):
+            slot = plane.source(half, d1, d2)
+            chosen_rows[i * 32 : (i + 1) * 32, depth:] = inputs[slot, 2 * half : 2 * half + 2, :, depth:].reshape(32, 128)
+
+        def column(n, carry):
+            columns = pl.ds(pl.multiple_of(n * 256, 256), 256)
+            result = dot(chosen_rows[:, depth:], back_weights(n, depth, 128))
+            result = (result + acc[n % 4, :, pl.ds(pl.multiple_of(n // 4 * 256, 256), 256)]).astype(BF16)
+            for i, (half, d1, d2) in enumerate(REDUCE_GROUPS[0]):
+                xs[plane.source(half, d1, d2), pl.ds(half * 32, 32), columns] = result[i * 32 : (i + 1) * 32, :]
+            return carry
+
+        lax.fori_loop(0, width // 256, column, 0)
+
+    def multiply_back(number):
         for i, (half, d1, d2) in enumerate(REDUCE_GROUPS[number]):
             slot = plane.source(half, d1, d2)
-            for u in (0, 1):
-                at = i * 32 + u * UNIT
-                rows_in[at : at + UNIT, :] = inputs[slot, half * 2 + u]
+            chosen_rows[i * 32 : (i + 1) * 32, :] = inputs[slot, 2 * half : 2 * half + 2].reshape(32, deep)
 
         def column(n, carry):
             columns = pl.ds(pl.multiple_of(n * 256, 256), 256)
-            result = dot(rows_in[...], weights[:, columns]).astype(BF16)
+            result = dot(chosen_rows[...], back_weights(n, 0, deep)).astype(BF16)
             for i, (half, d1, d2) in enumerate(REDUCE_GROUPS[number]):
-                slot = plane.source(half, d1, d2)
-                part[slot, pl.ds(half * 32, 32), columns] = result[i * 32 : (i + 1) * 32, :]
+                xs[plane.source(half, d1, d2), pl.ds(half * 32, 32), columns] = result[i * 32 : (i + 1) * 32, :]
             return carry
 
-        lax.fori_loop(0, out.shape[1] // 256, column, 0)
-
-    def rows_of(half, u):
+        lax.fori_loop(0, width // 256, column, 0)
+
+    def unit_rows(half, u):
         return pl.ds(half * 32 + u * UNIT, UNIT)
 
     def landing(half, axis, side, d1, place):
@@ -566,7 +578,7 @@
             return from2.at[index, FAR[d1], place], sems2.at[index, FAR[d1] * 3 + place]
         return from1.at[index, place], sems1.at[index, place]
 
-    def send(half, d1, d2, u, axis):
+    def send_back(half, d1, d2, u, axis):
         d = d2 if axis == 2 else d1
         back = d if d != 2 else (1 if u == 0 else -1)
         side = 0 if back == 1 else 1
@@ -575,63 +587,63 @@
         to = plane.off(half, 0, -back) if axis == 2 else plane.off(half, -back, 0)
         target, arrived = landing(half, axis, side, d1, place)
         pltpu.make_async_remote_copy(
-            part.at[slot, rows_of(half, u), :], target, send_sem, arrived, device_id={"mlp": to}, device_id_type=MESH
+            xs.at[slot, unit_rows(half, u), :], target, back_sem, arrived, device_id={"mlp": to}, device_id_type=MESH
         ).start()
 
-    def arrive(half, axis, side, d1, place):
+    def arrive_back(half, axis, side, d1, place):
         ref, arrived = landing(half, axis, side, d1, place)
         pltpu.make_async_copy(ref, ref, arrived).wait()
         return ref
 
     def add(half, d1, d2, u, children):
-        refs = [arrive(half, axis, side, d1, place) for axis, side, place in children]
+        refs = [arrive_back(half, axis, side, d1, place) for axis, side, place in children]
         slot = plane.source(half, d1, d2)
-        here = part.at[slot, rows_of(half, u), :]
+        here = xs.at[slot, unit_rows(half, u), :]
         value = here[...].astype(F32)
         for ref in refs:
             value = value + ref[...].astype(F32)
         here[...] = value.astype(BF16)
 
-    multiply(0)
+    first_group()
     for d1 in (2, 1, -1, 0):
         for half in (0, 1):
             for u in (0, 1):
-                send(half, d1, 2, u, 2)
+                send_back(half, d1, 2, u, 2)
     for number in (1, 2):
-        multiply(number)
+        multiply_back(number)
         for half, d1, d2 in REDUCE_GROUPS[number]:
-            send(half, d1, d2, 1 if d2 == 1 else 0, 2)
+            send_back(half, d1, d2, 1 if d2 == 1 else 0, 2)
     for number in (1, 2):
         for half, d1, d2 in REDUCE_GROUPS[number]:
             u = 0 if d2 == 1 else 1
             add(half, d1, d2, u, ((2, 0 if d2 == 1 else 1, 2),))
-            send(half, d1, d2, u, 2)
-    multiply(3)
+            send_back(half, d1, d2, u, 2)
+    multiply_back(3)
     both = lambda u: ((2, 0, u), (2, 1, u))
     for half in (0, 1):
         for u in (0, 1):
             add(half, 2, 0, u, both(u))
-            send(half, 2, 0, u, 1)
+            send_back(half, 2, 0, u, 1)
     for d1 in (1, -1):
         for half in (0, 1):
             u = 1 if d1 == 1 else 0
             add(half, d1, 0, u, both(u))
-            send(half, d1, 0, u, 1)
+            send_back(half, d1, 0, u, 1)
     for d1 in (1, -1):
         for half in (0, 1):
             u = 0 if d1 == 1 else 1
             add(half, d1, 0, u, both(u) + ((1, 0 if d1 == 1 else 1, 2),))
-            send(half, d1, 0, u, 1)
+            send_back(half, d1, 0, u, 1)
     for half in (0, 1):
         for u in (0, 1):
-            refs = [arrive(half, axis, side, 0, place) for axis, side, place in both(u) + ((1, 0, u), (1, 1, u))]
-            rows = rows_of(half, u)
-            value = part[me, rows, :].astype(F32)
+            refs = [arrive_back(half, axis, side, 0, place) for axis, side, place in both(u) + ((1, 0, u), (1, 1, u))]
+            rows = unit_rows(half, u)
+            value = xs[me, rows, :].astype(F32)
             for ref in refs:
                 value = value + ref[...].astype(F32)
             out[rows, :] = (value + tokens[rows, :].astype(F32) + out_bias[...]).astype(BF16)
-    sent = part.at[pl.ds(0, GROUP - 1)]
-    pltpu.make_async_copy(sent, sent, send_sem).wait()
+    sent = xs.at[pl.ds(0, GROUP - 1)]
+    pltpu.make_async_copy(sent, sent, back_sem).wait()
 
 
 def per_device(
@@ -646,15 +658,12 @@
     anywhere = pl.BlockSpec(memory_space=pl.ANY)
     dma = pltpu.SemaphoreType.DMA
     by_unit = (GROUP, 4, UNIT)
-    attended, hidden, adapter = pl.pallas_call(
-        front_kernel,
-        out_shape=(
-            jax.ShapeDtypeStruct(by_unit + (HEAD,), BF16),
-            jax.ShapeDtypeStruct(by_unit + (hid,), BF16),
-            jax.ShapeDtypeStruct(by_unit + (1,), F32),
-        ),
-        in_specs=[vmem] * 5 + [smem] + [anywhere] * 5,
-        out_specs=(vmem, vmem, vmem),
+    depth = HEAD + hid
+    return pl.pallas_call(
+        layer_kernel,
+        out_shape=jax.ShapeDtypeStruct((rows, width), BF16),
+        in_specs=[vmem] * 6 + [smem] + [anywhere] * 10,
+        out_specs=vmem,
         scratch_shapes=[
             pltpu.VMEM((GROUP, rows, width), BF16),
             pltpu.VMEM((width, QKV + hid + 128), BF16),
@@ -663,9 +672,10 @@
             pltpu.VMEM((256, width), BF16),
             pltpu.VMEM((4, 256, QKV + hid), F32),
             pltpu.VMEM(by_unit + (128,), BF16),
-            pltpu.VMEM((GROUP, UNIT, 128), BF16),
-            pltpu.VMEM((GROUP, UNIT, 128), BF16),
-            pltpu.VMEM((GROUP, UNIT, 128), BF16),
+            pltpu.VMEM((2, GROUP, UNIT, 128), BF16),
+            pltpu.VMEM((2, GROUP, UNIT, 128), BF16),
+            pltpu.VMEM((2, GROUP, UNIT, 128), BF16),
+            pltpu.VMEM(by_unit + (1,), F32),
             pltpu.VMEM(by_unit + (1,), F32),
             pltpu.VMEM((4, 256, 1), F32),
             pltpu.VMEM((4, 256, 1), F32),
@@ -683,53 +693,31 @@
             pltpu.VMEM((4, 256, 1), F32),
             pltpu.VMEM((4, 256, 1), F32),
             pltpu.VMEM((4, 256, HEAD + LATE), F32),
-            dma((5,)),
+            pltpu.VMEM(by_unit + (depth + 128,), BF16),
+            pltpu.VMEM((depth, 1024), BF16),
+            pltpu.VMEM((256, depth + 128), BF16),
+            pltpu.VMEM((4, 4, 3, UNIT, width), BF16),
+            pltpu.VMEM((4, 3, UNIT, width), BF16),
+            dma((7,)),
             dma,
             dma((GROUP, 4)),
-            dma((4,)),
+            dma((2, 4)),
             dma((50,)),
             dma((50,)),
+            dma((width // 256 * 3,)),
+            dma,
+            dma((4, 12)),
+            dma((4, 3)),
         ],
         compiler_params=pltpu.CompilerParams(
             collective_id=0, has_side_effects=True, vmem_limit_bytes=VMEM_LIMIT
         ),
-        name="front_stage",
+        name="layer_stage",
     )(
         tokens, layer_norm_gain[None, :], layer_norm_bias[None, :], input_bias[None, :],
-        jnp.stack([lengths, request_adapter]), slot_adapter,
+        output_bias[None, :], jnp.stack([lengths, request_adapter]), slot_adapter,
         query_key_weight.reshape(width, QKV), up_weight, input_adapter_left,
         query_key_value_right.reshape(-1, QKV), up_adapter_right,
-    )
-
-    depth = HEAD + hid + 128
-    return pl.pallas_call(
-        output_kernel,
-        out_shape=jax.ShapeDtypeStruct((rows, width), BF16),
-        in_specs=[anywhere] * 2 + [vmem] * 3 + [anywhere] * 5,
-        out_specs=vmem,
-        scratch_shapes=[
-            pltpu.VMEM(by_unit + (depth,), BF16),
-            pltpu.VMEM((HEAD + hid, 1024), BF16),
-            pltpu.VMEM((depth, width), BF16),
-            pltpu.VMEM((GROUP, rows, width), BF16),
-            pltpu.VMEM((4, 4, 3, UNIT, width), BF16),
-            pltpu.VMEM((4, 3, UNIT, width), BF16),
-            pltpu.VMEM((256, depth), BF16),
-            pltpu.VMEM((GROUP, UNIT, 128), BF16),
-            pltpu.VMEM((GROUP, UNIT, 128), BF16),
-            pltpu.VMEM((GROUP, UNIT, 128), BF16),
-            dma((7,)),
-            dma,
-            dma((4, 12)),
-            dma((4, 3)),
-            dma((4,)),
-        ],
-        compiler_params=pltpu.CompilerParams(
-            collective_id=1, has_side_effects=True, vmem_limit_bytes=VMEM_LIMIT
-        ),
-        name="output_stage",
-    )(
-        attended, hidden, adapter, tokens, output_bias[None, :],
         output_adapter_left.reshape(HEAD, -1), down_adapter_left, output_weight.reshape(HEAD, width), down_weight,
         output_adapter_right,
     )

time: 172 us -> 165 us (0.959)
  Pallas kernels: 168 us -> 161 us
    pallas_call x2 -> x1, Pallas kernels: 168 us -> 161 us  [per_device(): pl.pallas_call(layer_kernel, out_shape=jax.ShapeDtypeStruct((rows, width)...]
where the time goes in v5:
time: 165 us
  Pallas kernels  161 us (98%)
  local copies, waits for them, and re-layouts  3.23 us (2%)
    pallas_call x1, Pallas kernels, per_device(): pl.pallas_call(layer_kernel, out_shape=jax.ShapeDtypeStruct((rows, width)...  161 us

profile of v5, /device:TPU:0, one launch (start us, length us, event | category | flops | bytes accessed | tf_op | source)
XLA Modules:
  0.0 164.8 jit_solution(2258150655275814196)
XLA Ops:
  0.0 0.7 stack.9
  0.7 0.7 stack.10
  1.4 0.6 pad_add_fusion.table
  2.0 160.9 %layer_stage.1 = bf16[64,4096]{1,0:T(8,128)(2,1)} custom-call(bf16[64,4096]{1,0:T(8,128)(2,1)} %tokens.1, f32[1,4096]{1,0:T(1,128)} %bitcast.12, f32[1,4096]{1,0:T(1,128)} %bitcast.13, f32[1,512]{1,0:T(1,128)} %bitcast.15, f32[1,4096]{1,0:T(1,128)} %bitcast.14, s32[2,257]{1,0:T(2,128)} %pad_add_fusion.table, s32[4]{0:T(128)} %slots.1, ...), custom_call_target="tpu_custom_call" | custom-call | tf_op jit(solution)/shard_map/layer_stage/pallas_call | solution.py:662
  162.9 1.9 %copy.20 = bf16[64,4096]{1,0:T(8,128)(2,1)} copy(bf16[64,4096]{1,0:T(8,128)(2,1)} %layer_stage.1) | data formatting | bytes 1048576

commit v6 on v5

--- a/solution.py
+++ b/solution.py
@@ -51,31 +51,30 @@
     return sem
 
 
-def exchange_start(me, packed, landed, sems):
-    def scatter(k, carry):
-        to = (me + k) % GROUP
+FARTHEST = sorted(
+    ((dz, dy) for dz in (0, 1, -1, 2) for dy in (0, 1, -1, 2) if (dz, dy) != (0, 0)), key=lambda d: -abs(d[0]) - abs(d[1])
+)
+
+
+def exchange_start(plane, packed, landed, sems):
+    me = plane.me
+    for dz, dy in FARTHEST:
+        to = plane.at(dz, dy)
         pltpu.make_async_remote_copy(
             packed.at[to], landed.at[me], sems.at[0], sems.at[1], device_id={"mlp": to}, device_id_type=MESH
         ).start()
-        return carry
-
-    lax.fori_loop(1, GROUP, scatter, 0)
     landed[me] = packed[me]
 
 
-def exchange_middle(me, landed, full, sems):
+def exchange_middle(plane, landed, full, sems):
+    me = plane.me
     many = landed.at[pl.ds(0, GROUP - 1)]
     pltpu.make_async_copy(many, many, sems.at[1]).wait()
     full[me] = jnp.sum(landed[...].astype(F32), axis=0).astype(BF16)
-
-    def gather(k, carry):
-        to = (me + k) % GROUP
+    for dz, dy in FARTHEST:
         pltpu.make_async_remote_copy(
-            full.at[me], full.at[me], sems.at[2], sems.at[3], device_id={"mlp": to}, device_id_type=MESH
+            full.at[me], full.at[me], sems.at[2], sems.at[3], device_id={"mlp": plane.at(dz, dy)}, device_id_type=MESH
         ).start()
-        return carry
-
-    lax.fori_loop(1, GROUP, gather, 0)
 
 
 def exchange_end(landed, sems):
@@ -102,7 +101,7 @@
 
 
 def layer_kernel(
-    tokens, gain, bias, in_bias, out_bias, table, slots, w_qkv, w_up, w_left, w_qkv_right, w_up_right,
+    tokens, gain, bias, in_bias, out_bias, lengths, request_adapter, slots, w_qkv, w_up, w_left, w_qkv_right, w_up_right,
     w_left_attn, w_left_hid, w_attn, w_down, w_right,
     out,
     xs, weights, right_qkv, right_up, rows_in, acc, picked, packed, landed, full,
@@ -167,14 +166,14 @@
         for step in (1, -1):
             send(me, half, whole, 2, step)
 
-    long = table[0:1, :].astype(F32)
+    long = lengths[...].reshape(1, -1).astype(F32)
     requests = long.shape[1]
     before = lax.broadcasted_iota(jnp.int32, (requests, requests), 0) < lax.broadcasted_iota(
         jnp.int32, (requests, requests), 1
     )
     begins = dot(jnp.broadcast_to(long, (8, requests)).astype(BF16), before.astype(F32).astype(BF16))[:1, :]
     ends = begins + long
-    ids = table[1:2, :].astype(F32)
+    ids = request_adapter[...].reshape(1, -1).astype(F32)
 
     def locate(block, carry):
         rows = lax.broadcasted_iota(jnp.int32, (64, 1), 0)
@@ -357,25 +356,12 @@
         fold = jnp.logical_and(col_id // 32 == unit, row_id % 32 == col_id % 32).astype(F32).astype(BF16)
         together = together + dot(picked[:, unit].reshape(256, 128), fold)
     packed[0] = together.astype(BF16).reshape(GROUP, UNIT, 128)
-    exchange_start(me, packed.at[0], landed.at[0], ex_sems.at[0])
+    exchange_start(plane, packed.at[0], landed.at[0], ex_sems.at[0])
     multiply_wide(3, 1, 3)
     near_sends(3)
-    exchange_middle(me, landed.at[0], full.at[0], ex_sems.at[0])
+    exchange_middle(plane, landed.at[0], full.at[0], ex_sems.at[0])
     multiply_wide(3, 0, 1)
     multiply_wide(3, 3, tiles)
-    depth = HEAD + hid
-    width = out.shape[1]
-    deep = depth + 128
-    stored = []
-    for n in range(width // 256):
-        columns = pl.ds(n // 4 * 256, 256)
-        for j, (ref, first, size) in enumerate(((w_attn, 0, HEAD), (w_down, HEAD, hid), (w_right, depth, 128))):
-            copy = pltpu.make_async_copy(
-                ref.at[:, pl.ds(n * 256, 256)], weights.at[pl.ds(n % 4 * deep + first, size), columns],
-                weight_sems.at[n * 3 + j],
-            )
-            copy.start()
-            stored.append(copy)
     near_relays(2)
     next_relays(0)
     for load in loads[3:]:
@@ -402,11 +388,19 @@
         swapped = jnp.where(even, pltpu.roll(head, 127, 1), pltpu.roll(head, 1, 1))
         return head * cosine[number] + swapped * sine[number]
 
-    def heads(number, carry):
-        mine = row_adapter[number] == owner
+    def wide_of(number):
+        return rows_in.at[:, pl.ds(pl.multiple_of(number * 1024, 1024), 1024)]
+
+    def late_keys(number, carry):
         own = row_ranks[number]
-        wide = widened(own, mine, 0)
-        query = acc[number, :, :HEAD] + dot(wide, right_qkv[:, :HEAD])
+        wide = widened(own, row_adapter[number] == owner, 0)
+        wide_of(number)[...] = wide
+        key = acc[number, :, HEAD : HEAD + 128] + dot(wide, right_qkv[:, HEAD : HEAD + 128])
+        late[0, number] = jnp.where(lane < ROT, turn(key, number), own.astype(F32)).astype(BF16)
+        return carry
+
+    def query_rows(number, carry):
+        query = acc[number, :, :HEAD] + dot(wide_of(number)[...], right_qkv[:, :HEAD])
         scale = jnp.asarray(HEAD ** (-0.5), BF16)
         first = turn(query[:, :128], number).astype(BF16) * scale
         second = query[:, 128:].astype(BF16) * scale
@@ -415,15 +409,14 @@
             main, right_qkv[:, HEAD : 2 * HEAD], (((1,), (1,)), ((), ())), preferred_element_type=F32
         )
         fold = (fold_col == 64 + fold_row % RANK).astype(F32).astype(BF16)
-        low_rank = dot(jnp.where(mine, back, 0.0).astype(BF16), fold)
+        low_rank = dot(jnp.where(row_adapter[number] == owner, back, 0.0).astype(BF16), fold)
         queries[number, :, :HEAD] = main
         queries[number, :, HEAD:] = jnp.where(lane < ROT, first.astype(F32), low_rank).astype(BF16)
-        key = acc[number, :, HEAD : HEAD + 128] + dot(wide, right_qkv[:, HEAD : HEAD + 128])
-        late[0, number] = jnp.where(lane < ROT, turn(key, number), own.astype(F32)).astype(BF16)
         return carry
 
-    lax.fori_loop(0, 4, heads, 0)
+    lax.fori_loop(0, 4, late_keys, 0)
     near_sends(4)
+    lax.fori_loop(0, 4, query_rows, 0)
 
     def finish_hidden(number):
         wide = widened(row_ranks[number], row_adapter[number] == owner, RANK)
@@ -470,6 +463,21 @@
         def _():
             attend_all(slot)
 
+    depth = HEAD + hid
+    width = out.shape[1]
+    deep = depth + 128
+    stored = []
+
+    def store_weights():
+        for n in range(width // 1024):
+            for j, (ref, first, size) in enumerate(((w_attn, 0, HEAD), (w_down, HEAD, hid), (w_right, depth, 128))):
+                copy = pltpu.make_async_copy(
+                    ref.at[:, pl.ds(n * 1024, 1024)], weights.at[pl.ds(n * deep + first, size), pl.ds(0, 1024)],
+                    weight_sems.at[n * 3 + j],
+                )
+                copy.start()
+                stored.append(copy)
+
     def lower(unit, first, begin, end):
         mine = adapter[:, unit].reshape(256, 1) == owner
         product = dot(inputs[:, unit, :, begin:end].reshape(256, end - begin), left[begin:end, :])
@@ -478,23 +486,24 @@
 
     near_relays(3)
     next_relays(1)
+    near_low(4)
+    finish_hidden(0)
+    finish_hidden(1)
+    near_passing(4)
     next_relays(2)
-    finish_hidden(0)
     attend_all(0, True)
-    near_low(4)
-    finish_hidden(1)
-    finish_hidden(2)
-    near_passing(4)
     next_relays(3)
     take_all(5 - 4 * core, 3)
-    finish_hidden(3)
     attend_on(1, 1)
+    store_weights()
     near_high(4)
     attend_all(2)
     next_relays(4)
     take_all(1 + 2 * core, 4, 5)
     attend_all(1 + 2 * core)
     attend_all(4)
+    finish_hidden(2)
+    finish_hidden(3)
     together = lax.fori_loop(0, 4, lambda unit, sum_: sum_ + lower(unit, RANK, HEAD, depth), jnp.zeros((256, 128), F32))
     take_all(3 + 2 * core, 8, 9)
     attend_on(0, 3)
@@ -508,7 +517,7 @@
     for unit in range(4):
         together = together + lower(unit, 0, 0, HEAD)
     packed[1] = together.astype(BF16).reshape(GROUP, UNIT, 128)
-    exchange_start(me, packed.at[1], landed.at[1], ex_sems.at[1])
+    exchange_start(plane, packed.at[1], landed.at[1], ex_sems.at[1])
     for copy in started:
         copy.wait_send()
     sent = xs.at[pl.ds(0, GROUP - 1)]
@@ -517,7 +526,7 @@
         copy.wait()
 
     def back_weights(n, first, size):
-        return weights[pl.ds(pl.multiple_of(n % 4 * deep + first, 128), size), pl.ds(pl.multiple_of(n // 4 * 256, 256), 256)]
+        return weights[pl.ds(pl.multiple_of(n // 4 * deep + first, 128), size), pl.ds(pl.multiple_of(n % 4 * 256, 256), 256)]
 
     def base(n, carry):
         acc[n % 4, :, pl.ds(pl.multiple_of(n // 4 * 256, 256), 256)] = dot(
@@ -530,7 +539,7 @@
         chosen_rows[i * 32 : (i + 1) * 32, :depth] = inputs[slot, 2 * half : 2 * half + 2, :, :depth].reshape(32, depth)
     tiles = width // 256
     lax.fori_loop(0, tiles // 2, base, 0)
-    exchange_middle(me, landed.at[1], full.at[1], ex_sems.at[1])
+    exchange_middle(plane, landed.at[1], full.at[1], ex_sems.at[1])
     lax.fori_loop(tiles // 2, tiles, base, 0)
     exchange_end(landed.at[1], ex_sems.at[1])
     held = (me * 4 + lane // 32).astype(F32)
@@ -662,7 +671,7 @@
     return pl.pallas_call(
         layer_kernel,
         out_shape=jax.ShapeDtypeStruct((rows, width), BF16),
-        in_specs=[vmem] * 6 + [smem] + [anywhere] * 10,
+        in_specs=[vmem] * 7 + [smem] + [anywhere] * 10,
         out_specs=vmem,
         scratch_shapes=[
             pltpu.VMEM((GROUP, rows, width), BF16),
@@ -704,7 +713,7 @@
             dma((2, 4)),
             dma((50,)),
             dma((50,)),
-            dma((width // 256 * 3,)),
+            dma((width // 1024 * 3,)),
             dma,
             dma((4, 12)),
             dma((4, 3)),
@@ -715,7 +724,7 @@
         name="layer_stage",
     )(
         tokens, layer_norm_gain[None, :], layer_norm_bias[None, :], input_bias[None, :],
-        output_bias[None, :], jnp.stack([lengths, request_adapter]), slot_adapter,
+        output_bias[None, :], lengths, request_adapter, slot_adapter,
         query_key_weight.reshape(width, QKV), up_weight, input_adapter_left,
         query_key_value_right.reshape(-1, QKV), up_adapter_right,
         output_adapter_left.reshape(HEAD, -1), down_adapter_left, output_weight.reshape(HEAD, width), down_weight,

time: 165 us -> 164 us (level)
  no operation moved by 1% of the time
where the time goes in v6:
time: 164 us
  Pallas kernels  162 us (99%)
  local copies, waits for them, and re-layouts  1.87 us (1%)
    pallas_call x1, Pallas kernels, per_device(): pl.pallas_call(layer_kernel, out_shape=jax.ShapeDtypeStruct((rows, width)...  162 us

profile of v6, /device:TPU:0, one launch (start us, length us, event | category | flops | bytes accessed | tf_op | source)
XLA Modules:
  0.0 163.7 jit_solution(1772096841713323977)
XLA Ops:
  0.0 161.8 %layer_stage.1 = bf16[64,4096]{1,0:T(8,128)(2,1)} custom-call(bf16[64,4096]{1,0:T(8,128)(2,1)} %tokens.1, f32[1,4096]{1,0:T(1,128)} %bitcast.12, f32[1,4096]{1,0:T(1,128)} %bitcast.13, f32[1,512]{1,0:T(1,128)} %bitcast.15, f32[1,4096]{1,0:T(1,128)} %bitcast.14, s32[257]{0:T(512)} %lengths.1, s32[257]{0:T(512)} %request_adapter.1, s32[4]{0:T(128)} %slots.1, ...), custom_call_target="tpu_custom_call" | custom-call | tf_op jit(solution)/shard_map/layer_stage/pallas_call | solution.py:671
  161.8 1.9 %copy.20 = bf16[64,4096]{1,0:T(8,128)(2,1)} copy(bf16[64,4096]{1,0:T(8,128)(2,1)} %layer_stage.1) | data formatting | bytes 1048576

commit v7 on v6

--- a/solution.py
+++ b/solution.py
@@ -431,32 +431,37 @@
                 ].reshape(2, UNIT, 256)
 
     def attend_all(slot, own=False):
-        def body(b, carry):
+        def body(pair, carry):
             tail = late[slot].reshape(count, LATE)
             keys = jnp.concatenate([early[slot, :, :, :HEAD].reshape(count, HEAD), tail], axis=1)
             values = jnp.concatenate([early[slot, :, :, HEAD:].reshape(count, HEAD), tail], axis=1)
-            scores = lax.dot_general(queries[b], keys, (((1,), (1,)), ((), ())), preferred_element_type=F32)
             key_id = names[...] + ((req - slot) * count).astype(F32)
-            allowed = key_id >= row_start[b]
-            if own:
-                allowed = jnp.logical_and(allowed, key_id <= row_index[b])
-            scores = jnp.where(allowed, scores, NEGATIVE_FILL)
-            peak = jnp.max(scores, axis=1, keepdims=True)
-            if own:
-                kept = jnp.exp(scores - peak)
-                total[b] = jnp.sum(kept, axis=1, keepdims=True)
-                summed[b] = dot(kept.astype(BF16), values)
-            else:
-                old = top[b]
-                peak = jnp.maximum(old, peak)
-                kept = jnp.exp(scores - peak)
-                decay = jnp.exp(old - peak)
-                total[b] = total[b] * decay + jnp.sum(kept, axis=1, keepdims=True)
-                summed[b] = summed[b] * decay + dot(kept.astype(BF16), values)
-            top[b] = peak
+            blocks = (pair * 2, pair * 2 + 1)
+            scores = [
+                lax.dot_general(queries[b], keys, (((1,), (1,)), ((), ())), preferred_element_type=F32) for b in blocks
+            ]
+            results = []
+            for b, score in zip(blocks, scores):
+                allowed = key_id >= row_start[b]
+                if own:
+                    allowed = jnp.logical_and(allowed, key_id <= row_index[b])
+                score = jnp.where(allowed, score, NEGATIVE_FILL)
+                peak = jnp.max(score, axis=1, keepdims=True)
+                if not own:
+                    peak = jnp.maximum(top[b], peak)
+                kept = jnp.exp(score - peak)
+                results.append((peak, jnp.sum(kept, axis=1, keepdims=True), dot(kept.astype(BF16), values)))
+            for b, (peak, part, product) in zip(blocks, results):
+                if not own:
+                    decay = jnp.exp(top[b] - peak)
+                    part = part + total[b] * decay
+                    product = product + summed[b] * decay
+                top[b] = peak
+                total[b] = part
+                summed[b] = product
             return carry
 
-        lax.fori_loop(0, 4, body, 0)
+        lax.fori_loop(0, 2, body, 0)
 
     def attend_on(which, slot):
         @pl.when(core == which)

time: 164 us -> 159 us (0.970)
  Pallas kernels: 162 us -> 157 us
    pallas_call x1, Pallas kernels: 162 us -> 157 us  [per_device(): pl.pallas_call(layer_kernel, out_shape=jax.ShapeDtypeStruct((rows, width)...]
where the time goes in v7:
time: 159 us
  Pallas kernels  157 us (99%)
  local copies, waits for them, and re-layouts  1.87 us (1%)
    pallas_call x1, Pallas kernels, per_device(): pl.pallas_call(layer_kernel, out_shape=jax.ShapeDtypeStruct((rows, width)...  157 us

profile of v7, /device:TPU:0, one launch (start us, length us, event | category | flops | bytes accessed | tf_op | source)
XLA Modules:
  0.0 158.8 jit_solution(13414752930078206799)
XLA Ops:
  0.0 156.9 %layer_stage.1 = bf16[64,4096]{1,0:T(8,128)(2,1)} custom-call(bf16[64,4096]{1,0:T(8,128)(2,1)} %tokens.1, f32[1,4096]{1,0:T(1,128)} %bitcast.12, f32[1,4096]{1,0:T(1,128)} %bitcast.13, f32[1,512]{1,0:T(1,128)} %bitcast.15, f32[1,4096]{1,0:T(1,128)} %bitcast.14, s32[257]{0:T(512)} %lengths.1, s32[257]{0:T(512)} %request_adapter.1, s32[4]{0:T(128)} %slots.1, ...), custom_call_target="tpu_custom_call" | custom-call | tf_op jit(solution)/shard_map/layer_stage/pallas_call | solution.py:676
  156.9 1.9 %copy.20 = bf16[64,4096]{1,0:T(8,128)(2,1)} copy(bf16[64,4096]{1,0:T(8,128)(2,1)} %layer_stage.1) | data formatting | bytes 1048576

commit v8 on v7

--- a/solution.py
+++ b/solution.py
@@ -42,13 +42,6 @@
 
     def source(self, half, d1, d2):
         return self.off(half, -d1, -d2)
-
-
-def barrier_all(me, count):
-    sem = pltpu.get_barrier_semaphore()
-    for k in range(1, count):
-        pl.semaphore_signal(sem, inc=1, device_id={"mlp": (me + k) % count}, device_id_type=MESH)
-    return sem
 
 
 FARTHEST = sorted(
@@ -130,7 +123,9 @@
     ]
     for load in loads:
         load.start()
-    sem = barrier_all(me, GROUP)
+    sem = pltpu.get_barrier_semaphore()
+    for dz, dy in ((1, 0), (-1, 0), (0, 1), (0, -1)):
+        pl.semaphore_signal(sem, inc=1, device_id={"mlp": plane.at(dz, dy)}, device_id_type=MESH)
     for device in (ahead, behind, other):
         pl.semaphore_signal(sem, inc=1, device_id={"req": device}, device_id_type=MESH)
     for part in range(0, 64, 16):
@@ -139,7 +134,7 @@
         spread = jnp.mean(center * center, axis=1, keepdims=True)
         scaled = center * lax.rsqrt(spread + EPSILON)
         xs[me, part : part + 16, :] = (scaled * gain[...] + bias[...]).astype(BF16)
-    pl.semaphore_wait(sem, GROUP + 2)
+    pl.semaphore_wait(sem, 7)
 
     def send(slot, half, units, axis, step):
         first, many = units
@@ -414,9 +409,9 @@
         queries[number, :, HEAD:] = jnp.where(lane < ROT, first.astype(F32), low_rank).astype(BF16)
         return carry
 
-    lax.fori_loop(0, 4, late_keys, 0)
+    lax.fori_loop(0, 4, late_keys, 0, unroll=True)
     near_sends(4)
-    lax.fori_loop(0, 4, query_rows, 0)
+    lax.fori_loop(0, 4, query_rows, 0, unroll=2)
 
     def finish_hidden(number):
         wide = widened(row_ranks[number], row_adapter[number] == owner, RANK)
@@ -509,7 +504,7 @@
     attend_all(4)
     finish_hidden(2)
     finish_hidden(3)
-    together = lax.fori_loop(0, 4, lambda unit, sum_: sum_ + lower(unit, RANK, HEAD, depth), jnp.zeros((256, 128), F32))
+    together = lax.fori_loop(0, 4, lambda unit, sum_: sum_ + lower(unit, RANK, HEAD, depth), jnp.zeros((256, 128), F32), unroll=2)
     take_all(3 + 2 * core, 8, 9)
     attend_on(0, 3)
     for number in range(4):

time: 159 us -> 157 us (0.987)
  Pallas kernels: 157 us -> 155 us
    pallas_call x1, Pallas kernels: 157 us -> 155 us  [per_device(): pl.pallas_call(layer_kernel, out_shape=jax.ShapeDtypeStruct((rows, width)...]
where the time goes in v8:
time: 157 us
  Pallas kernels  155 us (99%)
  local copies, waits for them, and re-layouts  1.87 us (1%)
    pallas_call x1, Pallas kernels, per_device(): pl.pallas_call(layer_kernel, out_shape=jax.ShapeDtypeStruct((rows, width)...  155 us

profile of v8, /device:TPU:0, one launch (start us, length us, event | category | flops | bytes accessed | tf_op | source)
XLA Modules:
  0.0 157.2 jit_solution(1215670963919599152)
XLA Ops:
  0.0 155.3 %layer_stage.1 = bf16[64,4096]{1,0:T(8,128)(2,1)} custom-call(bf16[64,4096]{1,0:T(8,128)(2,1)} %tokens.1, f32[1,4096]{1,0:T(1,128)} %bitcast.12, f32[1,4096]{1,0:T(1,128)} %bitcast.13, f32[1,512]{1,0:T(1,128)} %bitcast.15, f32[1,4096]{1,0:T(1,128)} %bitcast.14, s32[257]{0:T(512)} %lengths.1, s32[257]{0:T(512)} %request_adapter.1, s32[4]{0:T(128)} %slots.1, ...), custom_call_target="tpu_custom_call" | custom-call | tf_op jit(solution)/shard_map/layer_stage/pallas_call | solution.py:671
  155.3 1.9 %copy.20 = bf16[64,4096]{1,0:T(8,128)(2,1)} copy(bf16[64,4096]{1,0:T(8,128)(2,1)} %layer_stage.1) | data formatting | bytes 1048576
